TPU v7x, 32 devices: a whole 2x2x4 slice. The times are simulated.
32 devices in a mesh: groups: 2 (over y), gx: 4 (over z), gy: 2 (over x), gz: 2 (over core).
Axes of the slice: x: 2, y: 2, z: 4, core: 2. Of those that a mesh axis runs over, the one named last changes fastest.
Arguments:
- atoms: bfloat16 [8, 2, 8, 16, 128], P(('groups', 'gx'), 'gy', 'gz'), parts along dimension 0, may hold values from -6 to 6
- places: bfloat16 [8, 2, 8, 3, 16], P(('groups', 'gx'), 'gy', 'gz'), parts along dimension 0, may hold values from 0 to 1
- counts: int32 [8, 2, 8], P(('groups', 'gx'), 'gy', 'gz'), parts along dimension 0, may hold values from 8 to 16, as said below
- in_weight: bfloat16 [128, 128], replicated, may hold values from -0.5 to 0.5
- basis_weight: bfloat16 [50, 128], replicated, may hold values from -0.875 to 0.875
- basis_bias: float32 [128], replicated, may hold values from -3 to 3
- filter_weight: bfloat16 [128, 128], replicated, may hold values from -0.5 to 0.5
- filter_bias: float32 [128], replicated, may hold values from -3 to 3
- dense_weight: bfloat16 [128, 128], replicated, may hold values from -0.5 to 0.5
- dense_bias: float32 [128], replicated, may hold values from -3 to 3
- final_weight: bfloat16 [128, 128], replicated, may hold values from -0.5 to 0.5
- final_bias: float32 [128], replicated, may hold values from -3 to 3
Outputs:
- updated: bfloat16 [8, 2, 8, 16, 128], P(('groups', 'gx'), 'gy', 'gz'), parts along dimension 0
There are 2 independent parts, one for each index of `groups`. A program takes and returns all parts, laid end to end along the dimension named above; an argument that names none is the same for every part. Nothing has to cross between parts.
Inputs may be any that keep to these rules, and one draw needn't show every extreme that they name: Each cell's atoms fill its first counts slots; some cell holds 16 atoms in every draw.
All inputs are finite; a program needn't handle non-finite values.
Results may differ from a plain program's by a relative error of at most 0.008.
Values may be sent and summed in bfloat16 or wider, within the bound.
No kernel may reach another device: no remote copies, remote signals or barrier semaphores. Data moves between devices by JAX's collectives and lax.ppermute only.
A program may use at most 64 MiB of HBM per device.

v0:
```python
import jax
import jax.numpy as jnp
import numpy as np
from jax import lax
from jax.sharding import PartitionSpec as P

CELL_EDGE = 5.0
BASIS_GAMMA = 10.0
LOG_TWO = 0.6931471805599453


def passed_along(value, axis, steps):
    count = lax.axis_size(axis)
    pairs = [(source, (source + steps) % count) for source in range(count)]
    return lax.ppermute(value, axis, pairs)


def shifted_softplus(values):
    return jax.nn.softplus(values) - LOG_TWO


def forward_offsets():
    listed = []
    for p in (-1, 0, 1):
        for q in (-1, 0, 1):
            for r in (-1, 0, 1):
                if p > 0 or (p == 0 and q > 0) or (p == 0 and q == 0 and (r > 0)):
                    listed.append((p, q, r))
    return listed


def pair_filters(
    coords_i,
    occupied_i,
    coords_j,
    occupied_j,
    offset,
    itself,
    basis_weight,
    basis_bias,
    filter_weight,
    filter_bias,
):
    n = coords_i.shape[0]
    a = coords_i.shape[2]
    k = basis_weight.shape[0]
    f = basis_weight.shape[1]
    separation = coords_j[:, :, None, :] + offset[:, :, None, None] - coords_i[:, :, :, None]
    radius = CELL_EDGE * jnp.sqrt(jnp.sum(separation * separation, axis=1))
    diagonal = jnp.eye(a, dtype=jnp.float32)
    allowed = (
        occupied_i[:, :, None]
        * occupied_j[:, None, :]
        * (1.0 - itself[:, None, None] * diagonal[None])
    )
    inside = jnp.where(radius < CELL_EDGE, 0.5 * (jnp.cos(jnp.pi * radius / CELL_EDGE) + 1.0), 0.0)
    weight = (allowed * inside).reshape(1, n * a * a)
    centers = lax.iota(jnp.float32, k) * (CELL_EDGE / (k - 1))
    distance_gap = radius.reshape(1, n * a * a) - centers[:, None]
    expand = jnp.exp(-BASIS_GAMMA * distance_gap * distance_gap).astype(jnp.bfloat16)
    hidden = (
        jnp.dot(basis_weight.T, expand, preferred_element_type=jnp.float32) + basis_bias[:, None]
    )
    hidden = shifted_softplus(hidden).astype(jnp.bfloat16)
    filters = (
        jnp.dot(filter_weight.T, hidden, preferred_element_type=jnp.float32) + filter_bias[:, None]
    )
    return (filters * weight).astype(jnp.bfloat16).reshape(f, n, a, a)


def split_groups(listed, width):
    groups = []
    start = 0
    while start < len(listed):
        rest = len(listed) - start
        take = rest if rest <= width + 1 else width
        groups.append(listed[start : start + take])
        start = start + take
    return groups


def shards(
    atoms,
    places,
    counts,
    in_weight,
    basis_weight,
    basis_bias,
    filter_weight,
    filter_bias,
    dense_weight,
    dense_bias,
    final_weight,
    final_bias,
):
    cells_x, cells_y, cells_z, a, f = atoms.shape
    n = cells_x * cells_y * cells_z
    projected = (
        jnp.dot(atoms.reshape(n * a, f), in_weight, preferred_element_type=jnp.float32)
        .astype(jnp.bfloat16)
        .reshape(atoms.shape)
    )
    occupied = (lax.iota(jnp.int32, a)[None, None, None, :] < counts[:, :, :, None]).astype(
        jnp.bfloat16
    )
    geometry = jnp.concatenate([places, occupied[:, :, :, None, :]], axis=3)
    own_coords = places.astype(jnp.float32).reshape(n, 3, a)
    own_occupied = occupied.astype(jnp.float32).reshape(n, a)
    own_features = projected.reshape(n, a, f)

    def view_cells(wide_coords, wide_occupied, wide_features, corner):
        px, py, pz = corner
        coords_part = wide_coords[px : px + cells_x, py : py + cells_y, pz : pz + cells_z].reshape(
            n, 3, a
        )
        occupied_part = wide_occupied[
            px : px + cells_x, py : py + cells_y, pz : pz + cells_z
        ].reshape(n, a)
        features_part = wide_features[
            px : px + cells_x, py : py + cells_y, pz : pz + cells_z
        ].reshape(n, a, f)
        return (coords_part, occupied_part, features_part)

    def offset_rows(group, self_flag):
        along = jnp.asarray(np.repeat(np.array(group, np.float32), n, axis=0))
        itself = jnp.full((len(group) * n,), self_flag, jnp.float32)
        return (along, itself)

    def make_filters(coords_i, occupied_i, coords_j, occupied_j, along, itself):
        return pair_filters(
            coords_i,
            occupied_i,
            coords_j,
            occupied_j,
            along,
            itself,
            basis_weight,
            basis_bias,
            filter_weight,
            filter_bias,
        )

    packed = jnp.concatenate(
        [
            projected.reshape(cells_x, cells_y, cells_z, a * f),
            geometry.reshape(cells_x, cells_y, cells_z, 4 * a),
        ],
        axis=3,
    )
    upper = passed_along(packed, "gx", -1)
    packed = jnp.concatenate([packed, upper], axis=0)
    upper = passed_along(packed, "gy", -1)
    packed = jnp.concatenate([packed, upper], axis=1)
    upper = passed_along(packed[:, :, :1], "gz", -1)
    packed = jnp.concatenate([packed, upper], axis=2)
    wide_features = packed[:, :, :, : a * f].reshape(cells_x + 1, cells_y + 1, cells_z + 1, a, f)
    wide_geometry = packed[:, :, :, a * f :].reshape(cells_x + 1, cells_y + 1, cells_z + 1, 4, a)
    wide_coords = wide_geometry[:, :, :, :3, :].astype(jnp.float32)
    wide_occupied = wide_geometry[:, :, :, 3, :].astype(jnp.float32)
    along, itself = offset_rows([(0, 0, 0)], 1.0)
    self_filters = make_filters(own_coords, own_occupied, own_coords, own_occupied, along, itself)
    local = jnp.einsum(
        "fnij,njf->nif", self_filters, own_features, preferred_element_type=jnp.float32
    )
    collected = jnp.zeros((cells_x + 1, cells_y + 1, cells_z + 1, a, f), jnp.float32)
    collected = collected.at[:cells_x, :cells_y, :cells_z].add(
        local.reshape(cells_x, cells_y, cells_z, a, f)
    )
    for group in split_groups(forward_offsets(), 3):
        count = len(group)
        lows = [tuple((max(-v, 0) for v in o)) for o in group]
        highs = [tuple((lo[d] + o[d] for d in range(3))) for lo, o in zip(lows, group)]
        low_views = [view_cells(wide_coords, wide_occupied, wide_features, c) for c in lows]
        high_views = [view_cells(wide_coords, wide_occupied, wide_features, c) for c in highs]
        along, itself = offset_rows(group, 0.0)
        filters = make_filters(
            jnp.concatenate([v[0] for v in low_views], axis=0),
            jnp.concatenate([v[1] for v in low_views], axis=0),
            jnp.concatenate([v[0] for v in high_views], axis=0),
            jnp.concatenate([v[1] for v in high_views], axis=0),
            along,
            itself,
        )
        to_low = jnp.einsum(
            "fnij,njf->nif",
            filters,
            jnp.concatenate([v[2] for v in high_views], axis=0),
            preferred_element_type=jnp.float32,
        )
        to_high = jnp.einsum(
            "fnij,nif->njf",
            filters,
            jnp.concatenate([v[2] for v in low_views], axis=0),
            preferred_element_type=jnp.float32,
        )
        to_low = to_low.reshape(count, cells_x, cells_y, cells_z, a, f)
        to_high = to_high.reshape(count, cells_x, cells_y, cells_z, a, f)
        for index in range(count):
            lx, ly, lz = lows[index]
            hx, hy, hz = highs[index]
            collected = collected.at[lx : lx + cells_x, ly : ly + cells_y, lz : lz + cells_z].add(
                to_low[index]
            )
            collected = collected.at[hx : hx + cells_x, hy : hy + cells_y, hz : hz + cells_z].add(
                to_high[index]
            )
    border = passed_along(collected[cells_x:], "gx", 1)
    collected = jnp.concatenate([collected[:1] + border, collected[1:cells_x]], axis=0)
    border = passed_along(collected[:, cells_y:], "gy", 1)
    collected = jnp.concatenate([collected[:, :1] + border, collected[:, 1:cells_y]], axis=1)
    border = passed_along(collected[:, :, cells_z:], "gz", 1)
    collected = jnp.concatenate([collected[:, :, :1] + border, collected[:, :, 1:cells_z]], axis=2)
    summed = collected.reshape(n, a, f)
    message = summed.astype(jnp.bfloat16).reshape(n * a, f)
    inner = shifted_softplus(
        jnp.dot(message, dense_weight, preferred_element_type=jnp.float32) + dense_bias
    ).astype(jnp.bfloat16)
    update = jnp.dot(inner, final_weight, preferred_element_type=jnp.float32) + final_bias
    result = (atoms.reshape(n * a, f).astype(jnp.float32) + update) * own_occupied.reshape(n * a, 1)
    return result.astype(jnp.bfloat16).reshape(atoms.shape)


def solution(mesh):
    placed = (
        P(("groups", "gx"), "gy", "gz", None, None),
        P(("groups", "gx"), "gy", "gz", None, None),
        P(("groups", "gx"), "gy", "gz"),
        P(),
        P(),
        P(),
        P(),
        P(),
        P(),
        P(),
        P(),
        P(),
    )
    return jax.shard_map(
        shards,
        mesh=mesh,
        in_specs=placed,
        out_specs=P(("groups", "gx"), "gy", "gz", None, None),
        check_vma=False,
    )
```

profile of v0, /device:TPU:0, one launch (start us, length us, event | category | flops | bytes accessed | tf_op | source)
XLA Modules:
  0.0 42.9 jit_solution(15356215170112296792)
XLA Ops:
  0.0 0.9 %bitcast_convert_fusion.1 = (f32[4,128,16]{1,2,0:T(8,128)S(1)}, bf16[64,128]{1,0:T(8,128)(2,1)S(1)}) fusion(bf16[64,128]{1,0:T(8,128)(2,1)} %bitcast.406, bf16[128,128]{1,0:T(8,128)(2,1)} %param.74), kind=kOutput, calls=%fused_computation.308 | convolution fusion | flops 2113536 | bytes 98304 | tf_op jit(solution)/shard_map/dot_general | solution.py:99
  1.0 0.7 %fusion.167 = bf16[1,1,4,1,16]{4,2,3,1,0:T(4,128)(2,1)S(1)} fusion(s32[4]{0:T(128)} %bitcast.413), kind=kLoop, calls=%fused_computation.303 | loop fusion | flops 128 | bytes 144 | tf_op jit(solution)/shard_map/convert_element_type | solution.py:103
  1.7 0.7 %pad_maximum_fusion.42 = bf16[1,1,4,4,16]{4,2,3,1,0:T(4,128)(2,1)S(1)} fusion(bf16[1,1,4,1,16]{4,2,3,1,0:T(4,128)(2,1)S(1)} %fusion.167, bf16[1,1,4,3,16]{4,2,3,1,0:T(4,128)(2,1)} %param.72), kind=kLoop, calls=%fused_computation.297 | loop fusion | flops 256 | bytes 1024 | tf_op jit(solution)/shard_map/concatenate | solution.py:106
  2.5 5.1 %collective-permute-start = (bf16[1,1,4,2112]{3,1,2,0:T(2,128)(2,1)S(1)}, bf16[1,1,4,2112]{3,1,2,0:T(2,128)(2,1)S(1)}, u32[]{:S(2)}, u32[]{:S(2)}) collective-permute-start(bf16[1,1,4,2112]{3,1,2,0:T(2,128)(2,1)S(1)} %constant_dynamic-update-slice_fusion.2), channel_id=1, source_target_pairs={{0,12},{4,0},{8,4},{12,8},{1,13},{5,1},{9,5},{13,9},{2,14},{6,2},{... | collective-permute-start | bytes 50696 | tf_op jit(solution)/shard_map/ppermute | solution.py:15
  7.6 0.7 %fusion.168 = f32[4,16]{1,0:T(4,128)S(1)} fusion(s32[4]{0:T(128)} %bitcast.414), kind=kLoop, calls=%fused_computation.305 | loop fusion | flops 192 | bytes 272 | tf_op jit(solution)/shard_map/convert_element_type | solution.py:108
  8.3 0.7 %bitcast_convert_fusion = f32[4,3,16]{2,0,1:T(4,128)S(1)} fusion(bf16[1,1,4,3,16]{4,2,3,1,0:T(4,128)(2,1)} %param.72), kind=kLoop, calls=%fused_computation.299 | loop fusion | flops 192 | bytes 1152 | tf_op jit(solution)/shard_map/broadcast_in_dim;reshape | solution.py:48
  9.7 1.6 %collective-permute-start.1 = (bf16[2,1,4,2112]{3,1,2,0:T(2,128)(2,1)S(1)}, bf16[2,1,4,2112]{3,1,2,0:T(2,128)(2,1)S(1)}, u32[]{:S(2)}, u32[]{:S(2)}) collective-permute-start(bf16[2,1,4,2112]{3,1,2,0:T(2,128)(2,1)S(1)} %pad_maximum_fusion.1), channel_id=1, source_target_pairs={{0,2},{2,0},{1,3},{3,1},{4,6},{6,4},{5,7},{7,5},{8,10},{10,8},{9,1... | collective-permute-start | bytes 101384 | tf_op jit(solution)/shard_map/ppermute | solution.py:15
  11.3 2.8 %collective-permute-done.1 = bf16[2,1,4,2112]{3,1,2,0:T(2,128)(2,1)S(1)} collective-permute-done((bf16[2,1,4,2112]{3,1,2,0:T(2,128)(2,1)S(1)}, bf16[2,1,4,2112]{3,1,2,0:T(2,128)(2,1)S(1)}, u32[]{:S(2)}, u32[]{:S(2)}) %collective-permute-start.1) | collective-permute-done | bytes 33824 | tf_op jit(solution)/shard_map/ppermute | solution.py:15
  14.2 1.5 %multiply_reduce_fusion.8 = f32[4,128,16]{1,2,0:T(8,128)S(1)} fusion(f32[4,128,16]{1,2,0:T(8,128)S(1)} %get-tuple-element.380, f32[1024]{0:T(1024)S(1)} %select_multiply_fusion.4, f32[128]{0:T(128)} %param.78, bf16[128,128]{1,0:T(8,128)(2,1)S(1)} %copy-done, bf16[50,128]{1,0:T(8,128)(2,1)} %param.75, f32[128]{0:T(128)} %param.76, ...), kind=kOutput, calls=%fused_computation.78 | convolution fusion | flops 48824320 | bytes 120520 | tf_op jit(solution)/shard_map/dot_general | solution.py:66
  16.5 0.4 sqrt_multiply_fusion.3
  17.1 1.5 %fusion.9 = bf16[3072,128]{1,0:T(8,128)(2,1)S(1)} fusion(bf16[128,128]{1,0:T(8,128)(2,1)S(1)} %copy-done, bf16[50,128]{1,0:T(8,128)(2,1)S(1)} %copy-done.9, f32[3072]{0:T(1024)S(1)} %select_multiply_fusion.3, f32[128]{0:T(128)S(1)} %copy-done.10, f32[128]{0:T(128)S(1)} %copy-done.11, f32[50]{0:T(128)S(1)} %iota_multiply_fusion, f32[3072]{0:T(1024)S(1)} %mul.441), kind=kOutput, calls=%fused_computation.21 | convolution fusion | flops 145317888 | bytes 857800 | tf_op jit(solution)/shard_map/dot_general | solution.py:66
  19.0 0.3 multiply_reduce_fusion.7
  20.3 0.4 sqrt_multiply_fusion.2
  20.9 1.5 %fusion.10 = bf16[3072,128]{1,0:T(8,128)(2,1)S(1)} fusion(bf16[128,128]{1,0:T(8,128)(2,1)S(1)} %copy-done, bf16[50,128]{1,0:T(8,128)(2,1)S(1)} %copy-done.9, f32[3072]{0:T(1024)S(1)} %select_multiply_fusion.2, f32[128]{0:T(128)S(1)} %copy-done.10, f32[128]{0:T(128)S(1)} %copy-done.11, f32[3072]{0:T(1024)S(1)} %mul.454, f32[50]{0:T(128)S(1)} %iota_multiply_fusion), kind=kOutput, calls=%fused_computation.22 | convolution fusion | flops 145317888 | bytes 857800 | tf_op jit(solution)/shard_map/dot_general | solution.py:66
  22.4 0.3 multiply_reduce_fusion.5
  23.1 0.4 sqrt_multiply_fusion.1
  23.7 1.5 %fusion.11 = bf16[3072,128]{1,0:T(8,128)(2,1)S(1)} fusion(bf16[128,128]{1,0:T(8,128)(2,1)S(1)} %copy-done, bf16[50,128]{1,0:T(8,128)(2,1)S(1)} %copy-done.9, f32[3072]{0:T(1024)S(1)} %select_multiply_fusion.1, f32[128]{0:T(128)S(1)} %copy-done.10, f32[128]{0:T(128)S(1)} %copy-done.11, f32[3072]{0:T(1024)S(1)} %mul.467, f32[50]{0:T(128)S(1)} %iota_multiply_fusion), kind=kOutput, calls=%fused_computation.23 | convolution fusion | flops 145317888 | bytes 857800 | tf_op jit(solution)/shard_map/dot_general | solution.py:66
  26.5 0.5 %sqrt_multiply_fusion = (f32[16,16,16]{2,1,0:T(8,128)S(1)}, f32[16,16,16]{2,1,0:T(8,128)S(1)}) fusion(f32[16,16,16]{2,1,0:T(8,128)S(1)} %multiply_reduce_fusion.9), kind=kLoop, calls=%fused_computation.102 | loop fusion | flops 16384 | bytes 49152 | tf_op jit(solution)/shard_map/mul | solution.py:49
  27.2 2.1 %multiply_reduce_fusion.1 = (f32[16,128,16]{1,2,0:T(8,128)S(1)}, bf16[4096,128]{1,0:T(8,128)(2,1)S(1)}) fusion(f32[16,128,16]{1,2,0:T(8,128)S(1)} %get-tuple-element.390, f32[4096]{0:T(1024)S(1)} %select_multiply_fusion, f32[128]{0:T(128)S(1)} %copy-done.10, bf16[128,128]{1,0:T(8,128)(2,1)S(1)} %copy-done, bf16[50,128]{1,0:T(8,128)(2,1)S(1)} %copy-done.9, ...), kind=kOutput, calls=%fused_computation.27 | convolution fusion | flops 195297280 | bytes 1390280 | tf_op jit(solution)/shard_map/dot_general | solution.py:66
  29.8 6.8 %collective-permute-done.3 = f32[1,2,5,16,128]{4,3,2,1,0:T(8,128)S(1)} collective-permute-done((f32[1,2,5,16,128]{4,3,2,1,0:T(8,128)S(1)}, f32[1,2,5,16,128]{4,3,2,1,0:T(8,128)S(1)}, u32[]{:S(2)}, u32[]{:S(2)}) %collective-permute-start.3) | collective-permute-done | bytes 81952 | tf_op jit(solution)/shard_map/ppermute | solution.py:15
  36.6 1.6 %collective-permute-start.4 = (f32[1,1,5,16,128]{4,3,2,1,0:T(8,128)S(1)}, f32[1,1,5,16,128]{4,3,2,1,0:T(8,128)S(1)}, u32[]{:S(2)}, u32[]{:S(2)}) collective-permute-start(f32[1,1,5,16,128]{4,3,2,1,0:T(8,128)S(1)} %slice.1538), channel_id=1, source_target_pairs={{0,2},{2,0},{1,3},{3,1},{4,6},{6,4},{5,7},{7,5},{8,10},{10,8},{9,1... | collective-permute-start | bytes 122888 | tf_op jit(solution)/shard_map/ppermute | solution.py:15
  38.4 2.3 %collective-permute-done.4 = f32[1,1,5,16,128]{4,3,2,1,0:T(8,128)S(1)} collective-permute-done((f32[1,1,5,16,128]{4,3,2,1,0:T(8,128)S(1)}, f32[1,1,5,16,128]{4,3,2,1,0:T(8,128)S(1)}, u32[]{:S(2)}, u32[]{:S(2)}) %collective-permute-start.4) | collective-permute-done | bytes 40992 | tf_op jit(solution)/shard_map/ppermute | solution.py:15
  40.8 1.1 %collective-permute-done.5 = f32[1,1,1,16,128]{4,3,2,1,0:T(8,128)S(1)} collective-permute-done((f32[1,1,1,16,128]{4,3,2,1,0:T(8,128)S(1)}, f32[1,1,1,16,128]{4,3,2,1,0:T(8,128)S(1)}, u32[]{:S(2)}, u32[]{:S(2)}) %collective-permute-start.5) | collective-permute-done | bytes 8224 | tf_op jit(solution)/shard_map/ppermute | solution.py:15
  42.0 0.9 %fusion.25 = bf16[64,128]{1,0:T(8,128)(2,1)} fusion(bf16[128,128]{1,0:T(8,128)(2,1)S(1)} %copy-done.7, bf16[64,128]{1,0:T(8,128)(2,1)S(1)} %bitcast.405, bf16[128,128]{1,0:T(8,128)(2,1)S(1)} %copy-done.8, bf16[64,128]{1,0:T(8,128)(2,1)S(1)} %bitcast.407, f32[64]{0:T(128)S(1)} %fusion.169, f32[128]{0:T(128)S(1)} %copy-done.12, f32[128]{0:T(128)S(1)} %copy-done.13), kind=kOutput, calls=%fused_computation.51 | convolution fusion | flops 4308992 | bytes 115968 | tf_op jit(solution)/shard_map/dot_general | solution.py:218
  (136 shorter events, 5.9 us)
Async XLA Ops:
  0.0 14.2 %copy-start = (bf16[128,128]{1,0:T(8,128)(2,1)S(1)}, bf16[128,128]{1,0:T(8,128)(2,1)}, u32[]{:S(2)}) copy-start(bf16[128,128]{1,0:T(8,128)(2,1)} %param.77) | copy-start | bytes 98308
  2.5 7.1 %collective-permute-start = (bf16[1,1,4,2112]{3,1,2,0:T(2,128)(2,1)S(1)}, bf16[1,1,4,2112]{3,1,2,0:T(2,128)(2,1)S(1)}, u32[]{:S(2)}, u32[]{:S(2)}) collective-permute-start(bf16[1,1,4,2112]{3,1,2,0:T(2,128)(2,1)S(1)} %constant_dynamic-update-slice_fusion.2), channel_id=1, source_target_pairs={{0,12},{4,0},{8,4},{12,8},{1,13},{5,1},{9,5},{13,9},{2,14},{6,2},{... | collective-permute-start | bytes 50696 | tf_op jit(solution)/shard_map/ppermute | solution.py:15
  9.1 7.1 %copy-start.3 = (f32[12,3]{1,0:T(8,128)S(1)}, f32[12,3]{1,0:T(8,128)}, u32[]{:S(2)}) copy-start(f32[12,3]{1,0:T(8,128)} %constant.733.clone) | copy-start | bytes 436
  9.1 7.1 %copy-start.4 = (f32[12,3]{1,0:T(8,128)S(1)}, f32[12,3]{1,0:T(8,128)}, u32[]{:S(2)}) copy-start(f32[12,3]{1,0:T(8,128)} %constant.734.clone) | copy-start | bytes 436
  9.7 4.4 %collective-permute-start.1 = (bf16[2,1,4,2112]{3,1,2,0:T(2,128)(2,1)S(1)}, bf16[2,1,4,2112]{3,1,2,0:T(2,128)(2,1)S(1)}, u32[]{:S(2)}, u32[]{:S(2)}) collective-permute-start(bf16[2,1,4,2112]{3,1,2,0:T(2,128)(2,1)S(1)} %pad_maximum_fusion.1), channel_id=1, source_target_pairs={{0,2},{2,0},{1,3},{3,1},{4,6},{6,4},{5,7},{7,5},{8,10},{10,8},{9,1... | collective-permute-start | bytes 101384 | tf_op jit(solution)/shard_map/ppermute | solution.py:15
  14.1 1.7 %collective-permute-start.2 = (bf16[2,2,1,2112]{3,1,2,0:T(2,128)(2,1)S(1)}, bf16[2,2,1,2112]{3,1,2,0:T(2,128)(2,1)S(1)}, u32[]{:S(2)}, u32[]{:S(2)}) collective-permute-start(bf16[2,2,1,2112]{3,1,2,0:T(2,128)(2,1)S(1)} %pad_maximum_fusion.25), channel_id=1, source_target_pairs={{0,1},{1,0},{2,3},{3,2},{4,5},{5,4},{6,7},{7,6},{8,9},{9,8},{10,11... | collective-permute-start | bytes 50696 | tf_op jit(solution)/shard_map/ppermute | solution.py:15
  15.7 1.3 %copy-start.9 = (bf16[50,128]{1,0:T(8,128)(2,1)S(1)}, bf16[50,128]{1,0:T(8,128)(2,1)}, u32[]{:S(2)}) copy-start(bf16[50,128]{1,0:T(8,128)(2,1)} %param.75) | copy-start | bytes 38404
  15.8 1.3 %copy-start.10 = (f32[128]{0:T(128)S(1)}, f32[128]{0:T(128)}, u32[]{:S(2)}) copy-start(f32[128]{0:T(128)} %param.78) | copy-start | bytes 1540
  15.8 1.3 %copy-start.11 = (f32[128]{0:T(128)S(1)}, f32[128]{0:T(128)}, u32[]{:S(2)}) copy-start(f32[128]{0:T(128)} %param.76) | copy-start | bytes 1540
  19.3 0.7 %copy-start.5 = (f32[12,3]{1,0:T(8,128)S(1)}, f32[12,3]{1,0:T(8,128)}, u32[]{:S(2)}) copy-start(f32[12,3]{1,0:T(8,128)} %constant.735.clone) | copy-start | bytes 436
  25.5 0.7 %copy-start.2 = (f32[16,3]{1,0:T(8,128)S(1)}, f32[16,3]{1,0:T(8,128)}, u32[]{:S(2)}) copy-start(f32[16,3]{1,0:T(8,128)} %constant.736.clone) | copy-start | bytes 580
  29.3 9.0 %copy-start.6 = (s32[1,1,4]{2,1,0:T(1,128)S(1)}, s32[1,1,4]{2,1,0:T(1,128)}, u32[]{:S(2)}) copy-start(s32[1,1,4]{2,1,0:T(1,128)} %param.73) | copy-start | bytes 52
  29.3 12.6 %copy-start.1 = (bf16[1,1,4,16,128]{4,3,2,1,0:T(8,128)(2,1)S(1)}, bf16[1,1,4,16,128]{4,3,2,1,0:T(8,128)(2,1)}, u32[]{:S(2)}) copy-start(bf16[1,1,4,16,128]{4,3,2,1,0:T(8,128)(2,1)} %param.71) | copy-start | bytes 49156
  29.4 12.6 %copy-start.7 = (bf16[128,128]{1,0:T(8,128)(2,1)S(1)}, bf16[128,128]{1,0:T(8,128)(2,1)}, u32[]{:S(2)}) copy-start(bf16[128,128]{1,0:T(8,128)(2,1)} %param.81) | copy-start | bytes 98308
  29.4 12.6 %copy-start.8 = (bf16[128,128]{1,0:T(8,128)(2,1)S(1)}, bf16[128,128]{1,0:T(8,128)(2,1)}, u32[]{:S(2)}) copy-start(bf16[128,128]{1,0:T(8,128)(2,1)} %param.79) | copy-start | bytes 98308
  29.4 12.6 %copy-start.12 = (f32[128]{0:T(128)S(1)}, f32[128]{0:T(128)}, u32[]{:S(2)}) copy-start(f32[128]{0:T(128)} %param.82) | copy-start | bytes 1540
  29.4 12.6 %copy-start.13 = (f32[128]{0:T(128)S(1)}, f32[128]{0:T(128)}, u32[]{:S(2)}) copy-start(f32[128]{0:T(128)} %param.80) | copy-start | bytes 1540
  29.7 6.9 %collective-permute-start.3 = (f32[1,2,5,16,128]{4,3,2,1,0:T(8,128)S(1)}, f32[1,2,5,16,128]{4,3,2,1,0:T(8,128)S(1)}, u32[]{:S(2)}, u32[]{:S(2)}) collective-permute-start(f32[1,2,5,16,128]{4,3,2,1,0:T(8,128)S(1)} %slice.1536), channel_id=1, source_target_pairs={{0,4},{4,8},{8,12},{12,0},{1,5},{5,9},{9,13},{13,1},{2,6},{6,10},{... | collective-permute-start | bytes 245768 | tf_op jit(solution)/shard_map/ppermute | solution.py:15
  36.6 4.1 %collective-permute-start.4 = (f32[1,1,5,16,128]{4,3,2,1,0:T(8,128)S(1)}, f32[1,1,5,16,128]{4,3,2,1,0:T(8,128)S(1)}, u32[]{:S(2)}, u32[]{:S(2)}) collective-permute-start(f32[1,1,5,16,128]{4,3,2,1,0:T(8,128)S(1)} %slice.1538), channel_id=1, source_target_pairs={{0,2},{2,0},{1,3},{3,1},{4,6},{6,4},{5,7},{7,5},{8,10},{10,8},{9,1... | collective-permute-start | bytes 122888 | tf_op jit(solution)/shard_map/ppermute | solution.py:15
  40.7 1.2 %collective-permute-start.5 = (f32[1,1,1,16,128]{4,3,2,1,0:T(8,128)S(1)}, f32[1,1,1,16,128]{4,3,2,1,0:T(8,128)S(1)}, u32[]{:S(2)}, u32[]{:S(2)}) collective-permute-start(f32[1,1,1,16,128]{4,3,2,1,0:T(8,128)S(1)} %slice.1540), channel_id=1, source_target_pairs={{0,1},{1,0},{2,3},{3,2},{4,5},{5,4},{6,7},{7,6},{8,9},{9,8},{10,11... | collective-permute-start | bytes 24584 | tf_op jit(solution)/shard_map/ppermute | solution.py:15
where the time goes:
time: 43.3 us; the launch traced here: 42.9 us
  waiting for transfers between devices  13 us (30%)
  matrix products  9.78 us (23%)
  starting transfers between devices  8.4 us (19%)
  other arithmetic  8.25 us (19%)
  local copies, waits for them, and re-layouts  2.53 us (6%)
  between operations  0.93 us (2%)
    ppermute x6, waiting for transfers between devices, passed_along(): return lax.ppermute(value, axis, pairs)  13 us
    ppermute x6, starting transfers between devices, passed_along(): return lax.ppermute(value, axis, pairs)  8.4 us
    dot_general x5, matrix products, pair_filters(): jnp.dot(filter_weight.T, hidden, preferred_element_type=jnp.float32)  7.98 us
    mul x5, other arithmetic, pair_filters(): radius = CELL_EDGE * jnp.sqrt(jnp.sum(separation * separation, axis=1))  1.7 us
    dot_general x3, other arithmetic, shards(): jnp.einsum('fnij,njf->nif', filters, jnp.concatenate([v[2] for v in high_...  1.03 us
    dot_general x1, matrix products, shards(): jnp.dot(atoms.reshape(n * a, f), in_weight, preferred_element_type=jnp.fl...  0.91 us
    dot_general x1, matrix products, shards(): jnp.dot(inner, final_weight, preferred_element_type=jnp.float32)  0.89 us
  transfers between devices with their start and end apart: 6, of which 4 were waited for; matrix products, arithmetic and copies ran while one was open for 9% of the time, Pallas kernels for 0%

commit v1 on v0

v1 whole, which is shorter than its diff:
```python
import math

import jax
import jax.numpy as jnp
import numpy as np
from jax import lax
from jax.experimental import pallas as pl
from jax.experimental.pallas import tpu as pltpu
from jax.sharding import PartitionSpec as P

LOG_TWO = 0.6931471805599453
BASIS_GAMMA = 10.0
CELL_EDGE = 5.0
FAR = 8.0
PAD_K = 64

COS_SERIES = [(-1.0) ** m * (math.pi / 2) ** (2 * m) / math.factorial(2 * m) for m in range(9)]


def ssp(values):
    return jnp.log(0.5 + jnp.exp(values - LOG_TWO))


def pack_kernel(counts_ref, atoms_ref, places_ref, out_ref):
    cells, a, f = atoms_ref.shape
    for c in range(cells):
        out_ref[c * a : (c + 1) * a, :] = atoms_ref[c]
    slot = lax.broadcasted_iota(jnp.int32, (3, a), 1)
    out_ref[cells * a :, :] = jnp.zeros((out_ref.shape[0] - cells * a, f), out_ref.dtype)
    spots = [
        jnp.where(slot < counts_ref[c], places_ref[c].astype(jnp.float32), FAR)
        for c in range(cells)
    ]
    table = jnp.stack(spots, axis=1).reshape(3 * cells, a)
    out_ref[cells * a : cells * a + 3 * cells, :a] = table.astype(out_ref.dtype)


def split_bf16(values, parts):
    out = []
    rest = values
    for _ in range(parts):
        head = rest.astype(jnp.bfloat16)
        out.append(head)
        rest = rest - head.astype(jnp.float32)
    return out


def main_kernel(layout, counts_ref, *refs):
    cells, a, f, k, y_count, block_of = layout
    n_blocks = len(block_of["names"])
    blocks = refs[:n_blocks]
    (in_w, basis_w, basis_b, filt_w, filt_b, dense_w, dense_b, final_w, final_b, out_ref) = refs[
        n_blocks : n_blocks + 10
    ]
    proj, zrow, rads, wgts, acc, w1_ref, w2_ref = refs[n_blocks + 10 :]
    wide = cells + 2
    lanes = a * a
    f32, bf16 = jnp.float32, jnp.bfloat16

    w1_ref[...] = jnp.zeros(w1_ref.shape, bf16)
    w1_ref[:, :k] = basis_w[...].astype(f32).T.astype(bf16)
    bias = (basis_b[...] - LOG_TWO).T
    for n, part in enumerate(split_bf16(bias, 3)):
        w1_ref[:, PAD_K + n : PAD_K + n + 1] = part
    w2_ref[...] = jnp.zeros(w2_ref.shape, bf16)
    w2_ref[:, :f] = filt_w[...].astype(f32).T.astype(bf16)
    for n, part in enumerate(split_bf16(filt_b[...].T, 2)):
        w2_ref[:, f + n : f + n + 1] = part

    def place_of(x, y, z):
        if z < 0:
            return blocks[block_of[(y, -1)]], x, cells - 1
        if z >= cells:
            return blocks[block_of[(y, 1)]], x, 0
        return blocks[block_of[(y, 0)]], x, z

    reps = 128 // a
    for x in range(3):
        for y in range(y_count):
            for z in range(-1, cells + 1):
                ref, bx, bz = place_of(x, y, z)
                rows = ref[bx, bz * a : (bz + 1) * a, :]
                rows = jnp.concatenate([rows] * reps, axis=0)
                tile = lax.dot_general(
                    in_w[...], rows, (((0,), (1,)), ((), ())), preferred_element_type=f32
                )
                proj[(x * y_count + y) * wide + z + 1] = tile.astype(bf16).astype(f32)

    row_id = lax.broadcasted_iota(jnp.int32, (f, lanes), 0)
    lane_id = lax.broadcasted_iota(jnp.int32, (f, lanes), 1)
    by_j = (row_id == lane_id % a).astype(f32).astype(bf16)
    by_i = (row_id == lane_id // a).astype(f32).astype(bf16)
    base = cells * a
    for x in range(3):
        for y in range(y_count):
            tables = {}
            for side in (-1, 0, 1):
                b = block_of[(y, side)]
                if b not in tables:
                    tables[b] = jnp.dot(
                        blocks[b][x, base : base + 16, :], by_j, preferred_element_type=f32
                    )
            for d in range(3):
                at = ((x * y_count + y) * 3) + d
                low = tables[block_of[(y, -1)]][d * cells + cells - 1 : d * cells + cells]
                mid = tables[block_of[(y, 0)]][d * cells : (d + 1) * cells]
                high = tables[block_of[(y, 1)]][d * cells : d * cells + 1]
                zrow[at, 0:1, :] = low
                zrow[at, 1 : 1 + cells, :] = mid
                zrow[at, 1 + cells : 2 + cells, :] = high
    own = jnp.dot(
        blocks[block_of[(0, 0)]][1, base : base + 16, :], by_i, preferred_element_type=f32
    )
    own = [own[d * cells : (d + 1) * cells] for d in range(3)]
    small = lax.broadcasted_iota(jnp.int32, (cells, lanes), 1)
    other = small % a != small // a
    for p in range(3):
        for q in range(3):
            y = block_of["y_index"][q]
            for r in range(3):
                shift = (p - 1, q - 1, r - 1)
                square = jnp.zeros((cells, lanes), f32)
                for d in range(3):
                    there = zrow[(p * y_count + y) * 3 + d, r : r + cells, :]
                    gap = there + float(shift[d]) - own[d]
                    square = square + gap * gap
                radius = CELL_EDGE * jnp.sqrt(square)
                cosine = jnp.full(square.shape, COS_SERIES[-1], f32)
                for term in COS_SERIES[-2::-1]:
                    cosine = cosine * square + term
                keep = radius < CELL_EDGE
                if shift == (0, 0, 0):
                    keep = keep & other
                at = (p * 3 + q) * 3 + r
                rads[at] = radius
                wgts[at] = jnp.where(keep, cosine * cosine, 0.0)

    acc[...] = jnp.zeros(acc.shape, f32)
    centers = lax.broadcasted_iota(jnp.int32, (PAD_K, 128), 0).astype(f32) * (CELL_EDGE / (k - 1))
    centers = jnp.concatenate([centers] * (lanes // 128), axis=1)
    ones = jnp.ones((16, lanes), bf16)

    def step(t, carry):
        p = t // 3
        q = t - p * 3
        y = jnp.where(q == 1, 0, 1) if y_count == 2 else (q + 2) % 3
        first = (p * y_count + y) * wide
        for c in range(cells):
            total = None
            for r in range(3):
                radius = rads[t * 3 + r, c : c + 1, :]
                gap = radius - centers
                grid = jnp.exp(gap * gap * (-BASIS_GAMMA)).astype(bf16)
                hidden = jnp.dot(
                    w1_ref[...], jnp.concatenate([grid, ones], axis=0), preferred_element_type=f32
                )
                hidden = jnp.log(0.5 + jnp.exp(hidden)).astype(bf16)
                weight = wgts[t * 3 + r, c : c + 1, :]
                weight = jnp.broadcast_to(weight, (16, lanes)).astype(bf16)
                hidden = (hidden.reshape(f // 16, 16, lanes) * weight[None]).reshape(f, lanes)
                filt = jnp.dot(
                    w2_ref[...], jnp.concatenate([hidden, weight], axis=0), preferred_element_type=f32
                )
                feat = proj[first + c + r]
                term = filt * jnp.concatenate([feat] * (lanes // 128), axis=1)
                total = term if total is None else total + term
            acc[c] += total
        return carry

    lax.fori_loop(0, 9, step, 0)

    rows = lax.broadcasted_iota(jnp.int32, (a, lanes), 0)
    cols = lax.broadcasted_iota(jnp.int32, (a, lanes), 1)
    pick = (rows == cols // a).astype(f32).astype(bf16)
    messages = []
    for c in range(cells):
        head, tail = split_bf16(acc[c], 2)
        dims = (((1,), (1,)), ((), ()))
        messages.append(
            lax.dot_general(pick, head, dims, preferred_element_type=f32)
            + lax.dot_general(pick, tail, dims, preferred_element_type=f32)
        )
    message = jnp.concatenate(messages, axis=0).astype(bf16)
    inner = jnp.dot(message, dense_w[...], preferred_element_type=f32) + dense_b[...]
    inner = (jax.nn.softplus(inner) - LOG_TWO).astype(bf16)
    update = jnp.dot(inner, final_w[...], preferred_element_type=f32) + final_b[...]
    slot = lax.broadcasted_iota(jnp.int32, (a, f), 0)
    own_block = blocks[block_of[(0, 0)]]
    for c in range(cells):
        here = own_block[1, c * a : (c + 1) * a, :].astype(f32)
        value = here + update[c * a : (c + 1) * a]
        out_ref[c] = jnp.where(slot < counts_ref[c], value, 0.0).astype(bf16)


def shifted(value, steps):
    axes = [axis for axis, s in steps if s % lax.axis_size(axis)]
    if not axes:
        return value
    sizes = [lax.axis_size(axis) for axis in axes]
    moves = [dict(steps)[axis] for axis in axes]
    pairs = []
    for at in np.ndindex(*sizes):
        to = [(i + s) % n for i, s, n in zip(at, moves, sizes)]
        pairs.append((int(np.ravel_multi_index(at, sizes)), int(np.ravel_multi_index(to, sizes))))
    return lax.ppermute(value, tuple(axes), pairs)


def shards(
    atoms,
    places,
    counts,
    in_weight,
    basis_weight,
    basis_bias,
    filter_weight,
    filter_bias,
    dense_weight,
    dense_bias,
    final_weight,
    final_bias,
):
    cells_x, cells_y, cells_z, a, f = atoms.shape
    assert cells_x == 1 and cells_y == 1
    cells = cells_z
    k = basis_weight.shape[0]
    vmem = pl.BlockSpec(memory_space=pltpu.VMEM)
    smem = pl.BlockSpec(memory_space=pltpu.SMEM)
    counts = counts.reshape(cells)
    packed = pl.pallas_call(
        pack_kernel,
        out_shape=jax.ShapeDtypeStruct((cells * a + 16, f), jnp.bfloat16),
        in_specs=[smem, vmem, vmem],
        out_specs=vmem,
    )(counts, atoms.reshape(cells, a, f), places.reshape(cells, 3, a))
    below = shifted(packed, [("gx", 1)])
    above = shifted(packed, [("gx", -1)])
    line = jnp.stack([below, packed, above])

    y_size, z_size = lax.axis_size("gy"), lax.axis_size("gz")
    y_steps = [0] if y_size == 1 else [0, 1] if y_size == 2 else [0, 1, -1]
    y_index = [0, 0, 0] if y_size == 1 else [1, 0, 1] if y_size == 2 else [2, 0, 1]
    names, block_of = [], {"names": None, "y_index": y_index}
    for yi, y in enumerate(y_steps):
        for z in (0, -1, 1):
            name = (y % y_size, z % z_size)
            if name not in names:
                names.append(name)
            block_of[(yi, z)] = names.index(name)
    block_of["names"] = names
    blocks = [shifted(line, [("gy", -y), ("gz", -z)]) for y, z in names]

    y_count = len(y_steps)
    lanes = a * a
    layout = (cells, a, f, k, y_count, block_of)
    halo = 3 * y_count * (cells + 2)
    out = pl.pallas_call(
        lambda *refs: main_kernel(layout, *refs),
        out_shape=jax.ShapeDtypeStruct((cells, a, f), jnp.bfloat16),
        in_specs=[smem] + [vmem] * (len(blocks) + 9),
        out_specs=vmem,
        scratch_shapes=[
            pltpu.VMEM((halo, f, 128), jnp.float32),
            pltpu.VMEM((3 * y_count * 3, 8, lanes), jnp.float32),
            pltpu.VMEM((27, cells, lanes), jnp.float32),
            pltpu.VMEM((27, cells, lanes), jnp.float32),
            pltpu.VMEM((cells, f, lanes), jnp.float32),
            pltpu.VMEM((f, PAD_K + 16), jnp.bfloat16),
            pltpu.VMEM((f, f + 16), jnp.bfloat16),
        ],
    )(
        counts,
        *blocks,
        in_weight,
        basis_weight,
        basis_bias.reshape(1, f),
        filter_weight,
        filter_bias.reshape(1, f),
        dense_weight,
        dense_bias.reshape(1, f),
        final_weight,
        final_bias.reshape(1, f),
    )
    return out.reshape(atoms.shape)


def solution(mesh):
    placed = (
        P(("groups", "gx"), "gy", "gz", None, None),
        P(("groups", "gx"), "gy", "gz", None, None),
        P(("groups", "gx"), "gy", "gz"),
    ) + (P(),) * 9
    return jax.shard_map(
        shards,
        mesh=mesh,
        in_specs=placed,
        out_specs=P(("groups", "gx"), "gy", "gz", None, None),
        check_vma=False,
    )
```

time: 43.3 us -> 31.6 us (0.73)
  Pallas kernels: 0 us -> 12 us
  matrix products: 9.78 us -> 0 us
  other arithmetic: 8.25 us -> 0.74 us
  waiting for transfers between devices: 13 us -> 9.55 us
  starting transfers between devices: 8.4 us -> 6.97 us
  between operations: 0.93 us -> 0.03 us
  local copies, waits for them, and re-layouts: 2.53 us -> 1.91 us
    pallas_call x0 -> x2, Pallas kernels: none -> 12 us  [the longest x1 10.7 us: shards(): pl.pallas_call(lambda *refs: main_kernel(layout, *refs), out_shape=jax.Sh...]
    dot_general x7 -> x0, matrix products: 9.78 us -> none  [the longest x5 7.98 us: pair_filters(): jnp.dot(filter_weight.T, hidden, preferred_element_type=jnp.float32)]
    ppermute x6 -> x5, waiting for transfers between devices: 13 us -> 9.55 us  [shifted(): return lax.ppermute(value, tuple(axes), pairs)]
    mul x15 -> x0, other arithmetic: 2.11 us -> none  [the longest x5 1.7 us: pair_filters(): radius = CELL_EDGE * jnp.sqrt(jnp.sum(separation * separation, axis=1))]
    dot_general x7 -> x0, other arithmetic: 1.71 us -> none  [the longest x3 1.03 us: shards(): jnp.einsum('fnij,njf->nif', filters, jnp.concatenate([v[2] for v in high_...]
    convert_element_type x5 -> x0, other arithmetic: 1.48 us -> none  [the longest x2 0.73 us: shards(): own_occupied = occupied.astype(jnp.float32).reshape(n, a)]
    ppermute x6 -> x5, starting transfers between devices: 8.4 us -> 6.97 us  [shifted(): return lax.ppermute(value, tuple(axes), pairs)]
    unnamed x29 -> x9, local copies, waits for them, and re-layouts: 0.53 us -> 1.91 us
  transfers between devices with their start and end apart: 6 -> 5, of which waited for: 4 -> 4; matrix products, arithmetic and copies ran while one was open for 9% -> 0% of each run, Pallas kernels for 0% -> 0%
where the time goes in v1:
time: 31.6 us; the launch traced here: 31.2 us
  Pallas kernels  12 us (38%)
  waiting for transfers between devices  9.55 us (30%)
  starting transfers between devices  6.97 us (22%)
  local copies, waits for them, and re-layouts  1.91 us (6%)
  other arithmetic  0.74 us (2%)
    pallas_call x1, Pallas kernels, shards(): pl.pallas_call(lambda *refs: main_kernel(layout, *refs), out_shape=jax.Sh...  10.7 us
    ppermute x5, waiting for transfers between devices, shifted(): return lax.ppermute(value, tuple(axes), pairs)  9.55 us
    ppermute x5, starting transfers between devices, shifted(): return lax.ppermute(value, tuple(axes), pairs)  6.97 us
    unnamed x9, local copies, waits for them, and re-layouts  1.91 us
    pallas_call x1, Pallas kernels, shards(): pl.pallas_call(pack_kernel, out_shape=jax.ShapeDtypeStruct((cells * a + 1...  1.34 us
    another operation x1, other arithmetic, shards(): line = jnp.stack([below, packed, above])  0.74 us
  transfers between devices with their start and end apart: 5, of which 4 were waited for; matrix products, arithmetic and copies ran while one was open for 0% of the time, Pallas kernels for 0%

profile of v1, /device:TPU:0, one launch (start us, length us, event | category | flops | bytes accessed | tf_op | source)
XLA Modules:
  0.0 31.2 jit_solution(7267082859489845555)
XLA Ops:
  0.0 1.3 %copy.15 = bf16[1,1,4,3,16]{4,3,2,1,0:T(4,128)(2,1)} copy(bf16[1,1,4,3,16]{4,2,3,1,0:T(4,128)(2,1)} %param.13) | data formatting | bytes 768 | tf_op args[1]
  1.3 1.3 %shard_map.118 = bf16[80,128]{1,0:T(8,128)(2,1)} custom-call(s32[4]{0:T(128)} %bitcast.18, bf16[4,16,128]{2,1,0:T(8,128)(2,1)} %bitcast.16, bf16[4,3,16]{2,1,0:T(4,128)(2,1)} %bitcast.17), custom_call_target="tpu_custom_call" | custom-call | tf_op jit(solution)/shard_map/pallas_call | solution.py:229
  2.6 5.0 %collective-permute-start.1 = (bf16[80,128]{1,0:T(8,128)(2,1)}, bf16[80,128]{1,0:T(8,128)(2,1)S(1)}, u32[]{:S(2)}, u32[]{:S(2)}) collective-permute-start(bf16[80,128]{1,0:T(8,128)(2,1)} %shard_map.118), channel_id=1, source_target_pairs={{0,12},{4,0},{8,4},{12,8},{1,13},{5,1},{9,5},{13,9},{2,14},{6,2},{... | collective-permute-start | bytes 61448 | tf_op jit(solution)/shard_map/ppermute | solution.py:205
  7.7 0.0 collective-permute-start
  7.7 1.7 %collective-permute-done.1 = bf16[80,128]{1,0:T(8,128)(2,1)S(1)} collective-permute-done((bf16[80,128]{1,0:T(8,128)(2,1)}, bf16[80,128]{1,0:T(8,128)(2,1)S(1)}, u32[]{:S(2)}, u32[]{:S(2)}) %collective-permute-start.1) | collective-permute-done | bytes 20512 | tf_op jit(solution)/shard_map/ppermute | solution.py:205
  9.4 4.1 %collective-permute-done = bf16[80,128]{1,0:T(8,128)(2,1)S(1)} collective-permute-done((bf16[80,128]{1,0:T(8,128)(2,1)}, bf16[80,128]{1,0:T(8,128)(2,1)S(1)}, u32[]{:S(2)}, u32[]{:S(2)}) %collective-permute-start) | collective-permute-done | bytes 20512 | tf_op jit(solution)/shard_map/ppermute | solution.py:205
  13.5 0.7 %pad_maximum_fusion.refs_1_ = bf16[3,80,128]{2,1,0:T(8,128)(2,1)S(1)} fusion(bf16[1,80,128]{2,1,0:T(8,128)(2,1)S(1)} %bitcast.14, bf16[1,80,128]{2,1,0:T(8,128)(2,1)} %bitcast.13, bf16[1,80,128]{2,1,0:T(8,128)(2,1)S(1)} %bitcast.15), kind=kLoop, calls=%fused_computation | loop fusion | flops 61440 | bytes 122880 | tf_op jit(solution)/shard_map/stack | solution.py:237
  14.2 0.0 copy-start
  14.2 0.1 collective-permute-start.4
  14.3 1.6 %collective-permute-start.3 = (bf16[3,80,128]{2,1,0:T(8,128)(2,1)S(1)}, bf16[3,80,128]{2,1,0:T(8,128)(2,1)S(1)}, u32[]{:S(2)}, u32[]{:S(2)}) collective-permute-start(bf16[3,80,128]{2,1,0:T(8,128)(2,1)S(1)} %pad_maximum_fusion.refs_1_), channel_id=1, source_target_pairs={{0,2},{2,0},{1,3},{3,1},{4,6},{6,4},{5,7},{7,5},{8,10},{10,8},{9,1... | collective-permute-start | bytes 184328 | tf_op jit(solution)/shard_map/ppermute | solution.py:205
  15.8 0.3 collective-permute-start.2
  16.1 2.4 %collective-permute-done.4.refs_4_ = bf16[3,80,128]{2,1,0:T(8,128)(2,1)S(1)} collective-permute-done((bf16[3,80,128]{2,1,0:T(8,128)(2,1)S(1)}, bf16[3,80,128]{2,1,0:T(8,128)(2,1)S(1)}, u32[]{:S(2)}, u32[]{:S(2)}) %collective-permute-start.4) | collective-permute-done | bytes 61472 | tf_op jit(solution)/shard_map/ppermute | solution.py:205
  18.5 0.0 copy-start.1
  18.5 1.4 %collective-permute-done.3.refs_3_ = bf16[3,80,128]{2,1,0:T(8,128)(2,1)S(1)} collective-permute-done((bf16[3,80,128]{2,1,0:T(8,128)(2,1)S(1)}, bf16[3,80,128]{2,1,0:T(8,128)(2,1)S(1)}, u32[]{:S(2)}, u32[]{:S(2)}) %collective-permute-start.3) | collective-permute-done | bytes 61472 | tf_op jit(solution)/shard_map/ppermute | solution.py:205
  19.9 0.0 copy-start.2
  19.9 0.0 collective-permute-done.2.refs_2_
  19.9 0.0 copy-start.3
  19.9 0.0 copy-done
  19.9 0.0 copy-done.1
  19.9 0.6 %copy-done.2 = bf16[3,80,128]{2,1,0:T(8,128)(2,1)} copy-done((bf16[3,80,128]{2,1,0:T(8,128)(2,1)}, bf16[3,80,128]{2,1,0:T(8,128)(2,1)S(1)}, u32[]{:S(2)}) %copy-start.2) | copy-done | bytes 61464
  20.5 0.0 copy-done.3
  20.5 10.7 %shard_map.119 = bf16[4,16,128]{2,1,0:T(8,128)(2,1)} custom-call(s32[4]{0:T(128)} %bitcast.19, bf16[3,80,128]{2,1,0:T(8,128)(2,1)} %copy-done, bf16[3,80,128]{2,1,0:T(8,128)(2,1)} %copy-done.3, bf16[3,80,128]{2,1,0:T(8,128)(2,1)} %copy-done.2, bf16[3,80,128]{2,1,0:T(8,128)(2,1)} %copy-done.1, bf16[128,128]{1,0:T(8,128)(2,1)} %refs_5_.1, ...), custom_call_target="tpu_custom_call" | custom-call | tf_op jit(solution)/shard_map/pallas_call | solution.py:256
Async XLA Ops:
  2.6 6.7 %collective-permute-start.1 = (bf16[80,128]{1,0:T(8,128)(2,1)}, bf16[80,128]{1,0:T(8,128)(2,1)S(1)}, u32[]{:S(2)}, u32[]{:S(2)}) collective-permute-start(bf16[80,128]{1,0:T(8,128)(2,1)} %shard_map.118), channel_id=1, source_target_pairs={{0,12},{4,0},{8,4},{12,8},{1,13},{5,1},{9,5},{13,9},{2,14},{6,2},{... | collective-permute-start | bytes 61448 | tf_op jit(solution)/shard_map/ppermute | solution.py:205
  7.7 5.8 %collective-permute-start = (bf16[80,128]{1,0:T(8,128)(2,1)}, bf16[80,128]{1,0:T(8,128)(2,1)S(1)}, u32[]{:S(2)}, u32[]{:S(2)}) collective-permute-start(bf16[80,128]{1,0:T(8,128)(2,1)} %shard_map.118), channel_id=1, source_target_pairs={{0,4},{4,8},{8,12},{12,0},{1,5},{5,9},{9,13},{13,1},{2,6},{6,10},{... | collective-permute-start | bytes 61448 | tf_op jit(solution)/shard_map/ppermute | solution.py:205
  14.2 5.7 %copy-start = (bf16[3,80,128]{2,1,0:T(8,128)(2,1)}, bf16[3,80,128]{2,1,0:T(8,128)(2,1)S(1)}, u32[]{:S(2)}) copy-start(bf16[3,80,128]{2,1,0:T(8,128)(2,1)S(1)} %pad_maximum_fusion.refs_1_) | copy-start | bytes 184324
  14.2 4.3 %collective-permute-start.4 = (bf16[3,80,128]{2,1,0:T(8,128)(2,1)S(1)}, bf16[3,80,128]{2,1,0:T(8,128)(2,1)S(1)}, u32[]{:S(2)}, u32[]{:S(2)}) collective-permute-start(bf16[3,80,128]{2,1,0:T(8,128)(2,1)S(1)} %pad_maximum_fusion.refs_1_), channel_id=1, source_target_pairs={{0,3},{1,2},{2,1},{3,0},{4,7},{5,6},{6,5},{7,4},{8,11},{9,10},{10,... | collective-permute-start | bytes 184328 | tf_op jit(solution)/shard_map/ppermute | solution.py:205
  14.3 5.6 %collective-permute-start.3 = (bf16[3,80,128]{2,1,0:T(8,128)(2,1)S(1)}, bf16[3,80,128]{2,1,0:T(8,128)(2,1)S(1)}, u32[]{:S(2)}, u32[]{:S(2)}) collective-permute-start(bf16[3,80,128]{2,1,0:T(8,128)(2,1)S(1)} %pad_maximum_fusion.refs_1_), channel_id=1, source_target_pairs={{0,2},{2,0},{1,3},{3,1},{4,6},{6,4},{5,7},{7,5},{8,10},{10,8},{9,1... | collective-permute-start | bytes 184328 | tf_op jit(solution)/shard_map/ppermute | solution.py:205
  15.8 4.1 %collective-permute-start.2 = (bf16[3,80,128]{2,1,0:T(8,128)(2,1)S(1)}, bf16[3,80,128]{2,1,0:T(8,128)(2,1)S(1)}, u32[]{:S(2)}, u32[]{:S(2)}) collective-permute-start(bf16[3,80,128]{2,1,0:T(8,128)(2,1)S(1)} %pad_maximum_fusion.refs_1_), channel_id=1, source_target_pairs={{0,1},{1,0},{2,3},{3,2},{4,5},{5,4},{6,7},{7,6},{8,9},{9,8},{10,11... | collective-permute-start | bytes 184328 | tf_op jit(solution)/shard_map/ppermute | solution.py:205
  18.5 1.4 %copy-start.1 = (bf16[3,80,128]{2,1,0:T(8,128)(2,1)}, bf16[3,80,128]{2,1,0:T(8,128)(2,1)S(1)}, u32[]{:S(2)}) copy-start(bf16[3,80,128]{2,1,0:T(8,128)(2,1)S(1)} %collective-permute-done.4.refs_4_) | copy-start | bytes 184324
  19.9 0.6 %copy-start.2 = (bf16[3,80,128]{2,1,0:T(8,128)(2,1)}, bf16[3,80,128]{2,1,0:T(8,128)(2,1)S(1)}, u32[]{:S(2)}) copy-start(bf16[3,80,128]{2,1,0:T(8,128)(2,1)S(1)} %collective-permute-done.3.refs_3_) | copy-start | bytes 184324
  19.9 0.6 %copy-start.3 = (bf16[3,80,128]{2,1,0:T(8,128)(2,1)}, bf16[3,80,128]{2,1,0:T(8,128)(2,1)S(1)}, u32[]{:S(2)}) copy-start(bf16[3,80,128]{2,1,0:T(8,128)(2,1)S(1)} %collective-permute-done.2.refs_2_) | copy-start | bytes 184324

commit v2 on v1

v2 whole, which is shorter than its diff:
```python
import math

import jax
import jax.numpy as jnp
import numpy as np
from jax import lax
from jax.experimental import pallas as pl
from jax.experimental.pallas import tpu as pltpu
from jax.sharding import PartitionSpec as P

LOG_TWO = 0.6931471805599453
LOG2_E = 1.4426950408889634
BASIS_GAMMA = 10.0
CELL_EDGE = 5.0
GAP_SCALE = math.sqrt(BASIS_GAMMA * LOG2_E)
FAR = 8.0
PAD_K = 64
EXTRA = 16

COS_SERIES = [(-1.0) ** m * (math.pi / 2) ** (2 * m) / math.factorial(2 * m) for m in range(9)]
F32, BF16 = jnp.float32, jnp.bfloat16
NT = (((1,), (1,)), ((), ()))


def split_bf16(values, parts):
    out = []
    rest = values
    for _ in range(parts):
        head = rest.astype(BF16)
        out.append(head)
        rest = rest - head.astype(F32)
    return out


def pack_kernel(counts_ref, atoms_ref, places_ref, out_ref):
    cells, a, f = atoms_ref.shape
    for c in range(cells):
        out_ref[c * a : (c + 1) * a, :] = atoms_ref[c]
    cell = lax.broadcasted_iota(jnp.int32, (cells, a), 0)
    slot = lax.broadcasted_iota(jnp.int32, (cells, a), 1)
    filled = jnp.zeros((cells, a), jnp.int32)
    for c in range(cells):
        filled = jnp.where(cell == c, counts_ref[c], filled)
    out_ref[cells * a :, :] = jnp.zeros((out_ref.shape[0] - cells * a, f), BF16)
    spots = [jnp.where(slot < filled, places_ref[d].astype(F32), FAR) for d in range(3)]
    table = jnp.concatenate(spots, axis=0)
    out_ref[cells * a : cells * a + 3 * cells, :a] = table.astype(BF16)


def spread(a, lanes, rows, by_j):
    row = lax.broadcasted_iota(jnp.int32, (rows, lanes), 0)
    lane = lax.broadcasted_iota(jnp.int32, (rows, lanes), 1)
    return (row == (lane % a if by_j else lane // a)).astype(F32).astype(BF16)


def project(rows, in_w, reps):
    return lax.dot_general(
        in_w[...], jnp.concatenate([rows] * reps, axis=0), (((0,), (1,)), ((), ())), preferred_element_type=F32
    )


def pair_terms(there, own, moves, drop):
    square = None
    for d, move in enumerate(moves):
        gap = there[d] - own[d]
        if len(move) == 2:
            gap = jnp.minimum(jnp.abs(gap + 1.0), jnp.abs(gap - 1.0))
        else:
            gap = gap + float(move[0])
        square = gap * gap if square is None else square + gap * gap
    far = jnp.sqrt(square)
    cosine = jnp.full(square.shape, COS_SERIES[-1], F32)
    for term in COS_SERIES[-2::-1]:
        cosine = cosine * square + term
    keep = CELL_EDGE * far < CELL_EDGE
    if drop is not None:
        keep = keep & drop
    return far * (CELL_EDGE * GAP_SCALE), jnp.where(keep, cosine * cosine * LOG_TWO, 0.0)


def add_pairs(units, cells, lanes, w1, w2, acc, k, f):
    reps = lanes // 128
    centers = lax.broadcasted_iota(jnp.int32, (PAD_K, 128), 0).astype(F32)
    centers = centers * (GAP_SCALE * CELL_EDGE / (k - 1))
    centers = jnp.concatenate([centers] * reps, axis=1)
    ones = jnp.ones((EXTRA, lanes), BF16)
    totals = [None] * cells
    left = [sum(u[0] == c for u in units) for c in range(cells)]
    first, second = {}, {}
    for n in range(len(units) + 2):
        if n < len(units):
            gap = (units[n][1]() - centers).astype(BF16)
            grid = jnp.exp2(gap * -gap)
            first[n] = jnp.dot(w1[...], jnp.concatenate([grid, ones], axis=0), preferred_element_type=F32)
        if 0 <= n - 1 < len(units):
            hidden = first.pop(n - 1).astype(BF16)
            hidden = jnp.log2(jnp.exp2(hidden) + jnp.array(0.5, BF16))
            weight = jnp.broadcast_to(units[n - 1][2](), (EXTRA, lanes)).astype(BF16)
            hidden = (hidden.reshape(f // EXTRA, EXTRA, lanes) * weight[None]).reshape(f, lanes)
            second[n - 1] = jnp.dot(w2[...], jnp.concatenate([hidden, weight], axis=0), preferred_element_type=F32)
        if 0 <= n - 2 < len(units):
            c = units[n - 2][0]
            term = second.pop(n - 2) * jnp.concatenate([units[n - 2][3]()] * reps, axis=1)
            totals[c] = term if totals[c] is None else totals[c] + term
            left[c] -= 1
            if left[c] == 0:
                acc[c] += totals[c]


def near_kernel(
    sizes, line, in_w, basis_w, basis_b, filt_w, filt_b, acc, w1, w2, proj, zrow, rads, wgts
):
    cells, a, f, k = sizes
    lanes = a * a
    w1[...] = jnp.zeros(w1.shape, BF16)
    w1[:, :k] = (basis_w[...].astype(F32).T * LOG2_E).astype(BF16)
    bias = (basis_b[...] * LOG2_E - 1.0).T
    for n, part in enumerate(split_bf16(bias, 3)):
        w1[:, PAD_K + n : PAD_K + n + 1] = part
    w2[...] = jnp.zeros(w2.shape, BF16)
    w2[:, :f] = filt_w[...].astype(F32).T.astype(BF16)
    for n, part in enumerate(split_bf16(filt_b[...].T * LOG2_E, 2)):
        w2[:, f + n : f + n + 1] = part
    base = cells * a
    by_j, by_i = spread(a, lanes, f, True), spread(a, lanes, f, False)
    own = jnp.dot(line[1, base : base + 16, :], by_i, preferred_element_type=F32)
    own = [own[d * cells : (d + 1) * cells] for d in range(3)]
    small = lax.broadcasted_iota(jnp.int32, (cells, lanes), 1)
    other = small % a != small // a
    for p in range(3):
        for c in range(cells):
            proj[p * cells + c] = project(line[p, c * a : (c + 1) * a, :], in_w, 128 // a)
        table = jnp.dot(line[p, base : base + 16, :], by_j, preferred_element_type=F32)
        for d in range(3):
            mid = table[d * cells : (d + 1) * cells]
            zrow[d, 0:cells, :] = mid
            zrow[d, 2 : 2 + cells, :] = mid
            zrow[d, 1 : 1 + cells, :] = mid
        for r in range(3):
            there = [zrow[d, r : r + cells, :] for d in range(3)]
            moves = ((1 - p,), (0,), (r - 1,))
            rads[p * 3 + r], wgts[p * 3 + r] = pair_terms(there, own, moves, other if p == 1 and r == 1 else None)
    acc[...] = jnp.zeros(acc.shape, F32)

    def step(p, carry):
        units = []
        for c in range(cells):
            for r in range(3):
                if 0 <= c + r - 1 < cells:
                    units.append((
                        c,
                        lambda c=c, r=r: rads[p * 3 + r, c : c + 1, :],
                        lambda c=c, r=r: wgts[p * 3 + r, c : c + 1, :],
                        lambda c=c, r=r: proj[p * cells + c + r - 1],
                    ))
        add_pairs(units, cells, lanes, w1, w2, acc, k, f)
        return carry

    lax.fori_loop(0, 3, step, 0)


def far_kernel(sizes, plan, counts_ref, *refs):
    cells, a, f, k = sizes
    block_of, ways, n_blocks = plan
    blocks, refs = refs[:n_blocks], refs[n_blocks:]
    near, w1, w2, in_w, dense_w, dense_b, final_w, final_b, out_ref, acc, proj, zrow, rads, wgts = refs
    lanes, wide, n_ways = a * a, cells + 2, len(ways)
    base = cells * a
    by_j, by_i = spread(a, lanes, f, True), spread(a, lanes, f, False)
    own_block = blocks[block_of[(0, 0)]]
    own = jnp.dot(own_block[1, base : base + 16, :], by_i, preferred_element_type=F32)
    own = [own[d * cells : (d + 1) * cells] for d in range(3)]

    def place_of(way, z):
        if z < 0:
            return blocks[block_of[(way, -1)]], cells - 1
        if z >= cells:
            return blocks[block_of[(way, 1)]], 0
        return blocks[block_of[(way, 0)]], z

    for p in range(3):
        for way in range(n_ways):
            at = p * n_ways + way
            for z in range(-1, cells + 1):
                if way == 0 and 0 <= z < cells:
                    continue
                ref, here = place_of(way, z)
                proj[at * wide + z + 1] = project(ref[p, here * a : (here + 1) * a, :], in_w, 128 // a)
            tables = {}
            for side in (-1, 0, 1):
                b = block_of[(way, side)]
                if b not in tables:
                    tables[b] = jnp.dot(blocks[b][p, base : base + 16, :], by_j, preferred_element_type=F32)
            for d in range(3):
                low, mid, high = (tables[block_of[(way, side)]] for side in (-1, 0, 1))
                zrow[d, 0:1, :] = low[d * cells + cells - 1 : d * cells + cells]
                zrow[d, 1 : 1 + cells, :] = mid[d * cells : (d + 1) * cells]
                zrow[d, 1 + cells : wide, :] = high[d * cells : d * cells + 1]
            for r in range(3):
                if way == 0 and r == 1:
                    continue
                there = [zrow[d, r : r + cells, :] for d in range(3)]
                moves = ((1 - p,), ways[way], (r - 1,))
                rads[at * 3 + r], wgts[at * 3 + r] = pair_terms(there, own, moves, None)
    acc[...] = jnp.zeros(acc.shape, F32)

    def step(p, carry):
        units = []
        for c in range(cells):
            for way in range(n_ways):
                for r in range(3):
                    if way == 0 and 0 <= c + r - 1 < cells:
                        continue
                    at = p * n_ways + way
                    units.append((
                        c,
                        lambda at=at, c=c, r=r: rads[at * 3 + r, c : c + 1, :],
                        lambda at=at, c=c, r=r: wgts[at * 3 + r, c : c + 1, :],
                        lambda at=at, c=c, r=r: proj[at * wide + c + r],
                    ))
        add_pairs(units, cells, lanes, w1, w2, acc, k, f)
        return carry

    lax.fori_loop(0, 3, step, 0)

    pick = spread(a, lanes, a, False)
    messages = []
    for c in range(cells):
        head, tail = split_bf16(acc[c] + near[c], 2)
        messages.append(
            lax.dot_general(pick, head, NT, preferred_element_type=F32)
            + lax.dot_general(pick, tail, NT, preferred_element_type=F32)
        )
    message = jnp.concatenate(messages, axis=0).astype(BF16)
    inner = jnp.dot(message, dense_w[...], preferred_element_type=F32) + dense_b[...]
    inner = (jax.nn.softplus(inner) - LOG_TWO).astype(BF16)
    update = jnp.dot(inner, final_w[...], preferred_element_type=F32) + final_b[...]
    slot = lax.broadcasted_iota(jnp.int32, (a, f), 0)
    for c in range(cells):
        here = own_block[1, c * a : (c + 1) * a, :].astype(F32)
        value = here + update[c * a : (c + 1) * a]
        out_ref[c] = jnp.where(slot < counts_ref[c], value, 0.0).astype(BF16)


def shifted(value, steps):
    axes = [axis for axis, s in steps if s % lax.axis_size(axis)]
    if not axes:
        return value
    sizes = [lax.axis_size(axis) for axis in axes]
    moves = [dict(steps)[axis] for axis in axes]
    pairs = []
    for at in np.ndindex(*sizes):
        to = [(i + s) % n for i, s, n in zip(at, moves, sizes)]
        pairs.append((int(np.ravel_multi_index(at, sizes)), int(np.ravel_multi_index(to, sizes))))
    return lax.ppermute(value, tuple(axes), pairs)


def on_chip(value):
    return pltpu.with_memory_space_constraint(value, pltpu.VMEM)


def shards(
    atoms,
    places,
    counts,
    in_weight,
    basis_weight,
    basis_bias,
    filter_weight,
    filter_bias,
    dense_weight,
    dense_bias,
    final_weight,
    final_bias,
):
    cells_x, cells_y, cells_z, a, f = atoms.shape
    assert cells_x == 1 and cells_y == 1
    cells = cells_z
    k = basis_weight.shape[0]
    lanes = a * a
    sizes = (cells, a, f, k)
    vmem = pl.BlockSpec(memory_space=pltpu.VMEM)
    smem = pl.BlockSpec(memory_space=pltpu.SMEM)
    counts = counts.reshape(cells)
    packed = pl.pallas_call(
        pack_kernel,
        out_shape=pltpu.VMEM((cells * a + 16, f), BF16),
        in_specs=[smem, vmem, vmem],
        out_specs=vmem,
    )(counts, atoms.reshape(cells, a, f), jnp.swapaxes(places, 2, 3).reshape(3, cells, a))
    above = shifted(packed, [("gx", -1)])
    below = shifted(packed, [("gx", 1)])
    line = jnp.stack([above, packed, below])

    y_size, z_size = lax.axis_size("gy"), lax.axis_size("gz")
    y_steps, ways = ([0, 1], [(0,), (1, -1)]) if y_size == 2 else ([0, 1, -1], [(0,), (1,), (-1,)])
    names, block_of = [], {}
    for way, y in enumerate(y_steps):
        for z in (0, -1, 1):
            name = (y % y_size, z % z_size)
            if name not in names:
                names.append(name)
            block_of[(way, z)] = names.index(name)
    blocks = [shifted(line, [("gy", -y), ("gz", -z)]) for y, z in names]

    n_ways = len(ways)
    terms = [pltpu.VMEM((9 * n_ways, cells, lanes), F32)] * 2
    near, w1, w2 = pl.pallas_call(
        lambda *refs: near_kernel(sizes, *refs),
        out_shape=[
            pltpu.VMEM((cells, f, lanes), F32),
            pltpu.VMEM((f, PAD_K + EXTRA), BF16),
            pltpu.VMEM((f, f + EXTRA), BF16),
        ],
        in_specs=[vmem] * 6,
        out_specs=[vmem] * 3,
        scratch_shapes=[pltpu.VMEM((3 * cells, f, 128), F32), pltpu.VMEM((3, 8, lanes), F32)]
        + [pltpu.VMEM((9, cells, lanes), F32)] * 2,
        cost_estimate=pl.CostEstimate(flops=10**9, transcendentals=10**6, bytes_accessed=10**6),
    )(
        *map(
            on_chip,
            (line, in_weight, basis_weight, basis_bias.reshape(1, f), filter_weight, filter_bias.reshape(1, f)),
        )
    )
    out = pl.pallas_call(
        lambda *refs: far_kernel(sizes, (block_of, ways, len(blocks)), *refs),
        out_shape=jax.ShapeDtypeStruct((cells, a, f), BF16),
        in_specs=[smem] + [vmem] * (len(blocks) + 8),
        out_specs=vmem,
        scratch_shapes=[
            pltpu.VMEM((cells, f, lanes), F32),
            pltpu.VMEM((3 * n_ways * (cells + 2), f, 128), F32),
            pltpu.VMEM((3, 8, lanes), F32),
        ]
        + terms,
        cost_estimate=pl.CostEstimate(flops=10**9, transcendentals=10**6, bytes_accessed=10**6),
    )(
        counts,
        *map(
            on_chip,
            (
                *blocks,
                near,
                w1,
                w2,
                in_weight,
                dense_weight,
                dense_bias.reshape(1, f),
                final_weight,
                final_bias.reshape(1, f),
            ),
        ),
    )
    return out.reshape(atoms.shape)


def solution(mesh):
    placed = (
        P(("groups", "gx"), "gy", "gz", None, None),
        P(("groups", "gx"), "gy", "gz", None, None),
        P(("groups", "gx"), "gy", "gz"),
    ) + (P(),) * 9
    return jax.shard_map(
        shards,
        mesh=mesh,
        in_specs=placed,
        out_specs=P(("groups", "gx"), "gy", "gz", None, None),
        check_vma=False,
    )
```

time: 31.6 us -> 19.8 us (0.63)
  waiting for transfers between devices: 9.55 us -> 2.29 us
  Pallas kernels: 12 us -> 8.8 us
  other arithmetic: 0.74 us -> 0.01 us
  local copies, waits for them, and re-layouts: 1.91 us -> 1.33 us
    ppermute x5, waiting for transfers between devices: 9.55 us -> 2.29 us  [shifted(): return lax.ppermute(value, tuple(axes), pairs)]
    pallas_call x2 -> x3, Pallas kernels: 12 us -> 8.8 us  [the longest x1 5.37 us: shards(): pl.pallas_call(lambda *refs: far_kernel(sizes, (block_of, ways, len(block...]
    another operation x1, other arithmetic: 0.74 us -> 0.01 us  [shards(): line = jnp.stack([above, packed, below])]
    unnamed x9 -> x18, local copies, waits for them, and re-layouts: 1.91 us -> 1.33 us
  transfers between devices with their start and end apart: 5 -> 5, of which waited for: 4 -> 3; matrix products, arithmetic and copies ran while one was open for 0% -> 0% of each run, Pallas kernels for 0% -> 14%
where the time goes in v2:
time: 19.8 us; the launch traced here: 19.6 us
  Pallas kernels  8.8 us (44%)
  starting transfers between devices  7.09 us (36%)
  waiting for transfers between devices  2.29 us (12%)
  local copies, waits for them, and re-layouts  1.33 us (7%)
    ppermute x5, starting transfers between devices, shifted(): return lax.ppermute(value, tuple(axes), pairs)  7.09 us
    pallas_call x1, Pallas kernels, shards(): pl.pallas_call(lambda *refs: far_kernel(sizes, (block_of, ways, len(block...  5.37 us
    pallas_call x1, Pallas kernels, shards(): pl.pallas_call(lambda *refs: near_kernel(sizes, *refs), out_shape=[pltpu....  2.69 us
    ppermute x5, waiting for transfers between devices, shifted(): return lax.ppermute(value, tuple(axes), pairs)  2.29 us
    unnamed x18, local copies, waits for them, and re-layouts  1.33 us
    pallas_call x1, Pallas kernels, shards(): pl.pallas_call(pack_kernel, out_shape=pltpu.VMEM((cells * a + 16, f), BF1...  0.74 us
  transfers between devices with their start and end apart: 5, of which 3 were waited for; matrix products, arithmetic and copies ran while one was open for 0% of the time, Pallas kernels for 14%

profile of v2, /device:TPU:0, one launch (start us, length us, event | category | flops | bytes accessed | tf_op | source)
XLA Modules:
  0.0 19.6 jit_solution(1444044752465142354)
XLA Ops:
  0.0 0.7 %shard_map.118 = bf16[80,128]{1,0:T(8,128)(2,1)S(1)} custom-call(s32[4]{0:T(128)} %bitcast.22, bf16[4,16,128]{2,1,0:T(8,128)(2,1)} %bitcast.20, bf16[3,4,16]{2,1,0:T(4,128)(2,1)} %bitcast.21), custom_call_target="tpu_custom_call" | custom-call | tf_op jit(solution)/shard_map/pallas_call | solution.py:285
  0.7 3.1 %collective-permute-start.1 = (bf16[80,128]{1,0:T(8,128)(2,1)S(1)}, bf16[80,128]{1,0:T(8,128)(2,1)S(1)}, u32[]{:S(2)}, u32[]{:S(2)}) collective-permute-start(bf16[80,128]{1,0:T(8,128)(2,1)S(1)} %shard_map.118), channel_id=1, source_target_pairs={{0,4},{4,8},{8,12},{12,0},{1,5},{5,9},{9,13},{13,1},{2,6},{6,10},{... | collective-permute-start | bytes 61448 | tf_op jit(solution)/shard_map/ppermute | solution.py:255
  3.8 2.1 %collective-permute-start = (bf16[80,128]{1,0:T(8,128)(2,1)S(1)}, bf16[80,128]{1,0:T(8,128)(2,1)S(1)}, u32[]{:S(2)}, u32[]{:S(2)}) collective-permute-start(bf16[80,128]{1,0:T(8,128)(2,1)S(1)} %shard_map.118), channel_id=1, source_target_pairs={{0,12},{4,0},{8,4},{12,8},{1,13},{5,1},{9,5},{13,9},{2,14},{6,2},{... | collective-permute-start | bytes 61448 | tf_op jit(solution)/shard_map/ppermute | solution.py:255
  5.9 1.8 %collective-permute-done.1 = bf16[80,128]{1,0:T(8,128)(2,1)S(1)} collective-permute-done((bf16[80,128]{1,0:T(8,128)(2,1)S(1)}, bf16[80,128]{1,0:T(8,128)(2,1)S(1)}, u32[]{:S(2)}, u32[]{:S(2)}) %collective-permute-start.1) | collective-permute-done | bytes 20512 | tf_op jit(solution)/shard_map/ppermute | solution.py:255
  7.7 0.1 collective-permute-done
  7.8 0.0 copy-start
  7.8 0.0 copy-start.1
  7.8 0.1 collective-permute-start.4
  7.9 1.6 %collective-permute-start.3 = (bf16[3,80,128]{2,1,0:T(8,128)(2,1)S(1)}, bf16[3,80,128]{2,1,0:T(8,128)(2,1)S(1)}, u32[]{:S(2)}, u32[]{:S(2)}) collective-permute-start(bf16[3,80,128]{2,1,0:T(8,128)(2,1)S(1)} %pad_maximum_fusion.refs_0_.refs_1_), channel_id=1, source_target_pairs={{0,2},{2,0},{1,3},{3,1},{4,6},{6,4},{5,7},{7,5},{8,10},{10,8},{9,1... | collective-permute-start | bytes 184328 | tf_op jit(solution)/shard_map/ppermute | solution.py:255
  9.5 0.3 %collective-permute-start.2 = (bf16[3,80,128]{2,1,0:T(8,128)(2,1)S(1)}, bf16[3,80,128]{2,1,0:T(8,128)(2,1)S(1)}, u32[]{:S(2)}, u32[]{:S(2)}) collective-permute-start(bf16[3,80,128]{2,1,0:T(8,128)(2,1)S(1)} %pad_maximum_fusion.refs_0_.refs_1_), channel_id=1, source_target_pairs={{0,1},{1,0},{2,3},{3,2},{4,5},{5,4},{6,7},{7,6},{8,9},{9,8},{10,11... | collective-permute-start | bytes 184328 | tf_op jit(solution)/shard_map/ppermute | solution.py:255
  9.8 0.0 copy-done
  9.8 0.0 copy-done.1
  9.8 0.0 copy-done.4
  9.8 0.6 %copy-done.5 = f32[128]{0:T(128)S(1)} copy-done((f32[128]{0:T(128)S(1)}, f32[128]{0:T(128)}, u32[]{:S(2)}) %copy-start.5) | copy-done | bytes 536
  10.4 0.0 copy-done.6
  10.4 2.7 %shard_map.119 = (f32[4,128,256]{2,1,0:T(8,128)S(1)}, bf16[128,80]{1,0:T(8,128)(2,1)S(1)}, bf16[128,144]{1,0:T(8,128)(2,1)S(1)}) custom-call(bf16[3,80,128]{2,1,0:T(8,128)(2,1)S(1)} %pad_maximum_fusion.refs_0_.refs_1_, bf16[128,128]{1,0:T(8,128)(2,1)S(1)} %copy-done.1, bf16[50,128]{1,0:T(8,128)(2,1)S(1)} %copy-done.4, f32[1,128]{1,0:T(1,128)S(1)} %bitcast.14, ...), custom_call_target="tpu_custom_call" | custom-call | flops 1000000000 | bytes 1000000 | tf_op jit(solution)/shard_map/pallas_call | solution.py:308
  13.1 0.0 collective-permute-done.4.refs_4_
  13.2 0.4 %collective-permute-done.3.refs_3_ = bf16[3,80,128]{2,1,0:T(8,128)(2,1)S(1)} collective-permute-done((bf16[3,80,128]{2,1,0:T(8,128)(2,1)S(1)}, bf16[3,80,128]{2,1,0:T(8,128)(2,1)S(1)}, u32[]{:S(2)}, u32[]{:S(2)}) %collective-permute-start.3) | collective-permute-done | bytes 61472 | tf_op jit(solution)/shard_map/ppermute | solution.py:255
  13.5 0.0 collective-permute-done.2.refs_2_
  13.5 0.0 copy-done.2
  13.5 0.0 copy-done.3
  13.6 0.6 %copy-done.7 = f32[128]{0:T(128)S(1)} copy-done((f32[128]{0:T(128)S(1)}, f32[128]{0:T(128)}, u32[]{:S(2)}) %copy-start.7) | copy-done | bytes 536
  14.2 0.0 copy-done.8
  14.2 5.4 %shard_map.120 = bf16[4,16,128]{2,1,0:T(8,128)(2,1)} custom-call(s32[4]{0:T(128)} %bitcast.23, bf16[3,80,128]{2,1,0:T(8,128)(2,1)S(1)} %pad_maximum_fusion.refs_0_.refs_1_, bf16[3,80,128]{2,1,0:T(8,128)(2,1)S(1)} %collective-permute-done.2.refs_2_, bf16[3,80,128]{2,1,0:T(8,128)(2,1)S(1)} %collective-permute-done.3.refs_3_, ...), custom_call_target="tpu_custom_call" | custom-call | flops 1000000000 | bytes 1000000 | tf_op jit(solution)/shard_map/pallas_call | solution.py:326
  (8 shorter events, 0.0 us)
Async XLA Ops:
  0.7 7.0 %collective-permute-start.1 = (bf16[80,128]{1,0:T(8,128)(2,1)S(1)}, bf16[80,128]{1,0:T(8,128)(2,1)S(1)}, u32[]{:S(2)}, u32[]{:S(2)}) collective-permute-start(bf16[80,128]{1,0:T(8,128)(2,1)S(1)} %shard_map.118), channel_id=1, source_target_pairs={{0,4},{4,8},{8,12},{12,0},{1,5},{5,9},{9,13},{13,1},{2,6},{6,10},{... | collective-permute-start | bytes 61448 | tf_op jit(solution)/shard_map/ppermute | solution.py:255
  3.8 4.0 %collective-permute-start = (bf16[80,128]{1,0:T(8,128)(2,1)S(1)}, bf16[80,128]{1,0:T(8,128)(2,1)S(1)}, u32[]{:S(2)}, u32[]{:S(2)}) collective-permute-start(bf16[80,128]{1,0:T(8,128)(2,1)S(1)} %shard_map.118), channel_id=1, source_target_pairs={{0,12},{4,0},{8,4},{12,8},{1,13},{5,1},{9,5},{13,9},{2,14},{6,2},{... | collective-permute-start | bytes 61448 | tf_op jit(solution)/shard_map/ppermute | solution.py:255
  7.8 2.0 %copy-start = (bf16[128,128]{1,0:T(8,128)(2,1)S(1)}, bf16[128,128]{1,0:T(8,128)(2,1)}, u32[]{:S(2)}) copy-start(bf16[128,128]{1,0:T(8,128)(2,1)} %refs_4_.1) | copy-start | bytes 98308
  7.8 2.0 %copy-start.1 = (bf16[128,128]{1,0:T(8,128)(2,1)S(1)}, bf16[128,128]{1,0:T(8,128)(2,1)}, u32[]{:S(2)}) copy-start(bf16[128,128]{1,0:T(8,128)(2,1)} %refs_8_.1) | copy-start | bytes 98308
  7.8 2.0 %copy-start.4 = (bf16[50,128]{1,0:T(8,128)(2,1)S(1)}, bf16[50,128]{1,0:T(8,128)(2,1)}, u32[]{:S(2)}) copy-start(bf16[50,128]{1,0:T(8,128)(2,1)} %refs_2_.1) | copy-start | bytes 38404
  7.8 5.3 %collective-permute-start.4 = (bf16[3,80,128]{2,1,0:T(8,128)(2,1)S(1)}, bf16[3,80,128]{2,1,0:T(8,128)(2,1)S(1)}, u32[]{:S(2)}, u32[]{:S(2)}) collective-permute-start(bf16[3,80,128]{2,1,0:T(8,128)(2,1)S(1)} %pad_maximum_fusion.refs_0_.refs_1_), channel_id=1, source_target_pairs={{0,3},{1,2},{2,1},{3,0},{4,7},{5,6},{6,5},{7,4},{8,11},{9,10},{10,... | collective-permute-start | bytes 184328 | tf_op jit(solution)/shard_map/ppermute | solution.py:255
  7.9 5.6 %collective-permute-start.3 = (bf16[3,80,128]{2,1,0:T(8,128)(2,1)S(1)}, bf16[3,80,128]{2,1,0:T(8,128)(2,1)S(1)}, u32[]{:S(2)}, u32[]{:S(2)}) collective-permute-start(bf16[3,80,128]{2,1,0:T(8,128)(2,1)S(1)} %pad_maximum_fusion.refs_0_.refs_1_), channel_id=1, source_target_pairs={{0,2},{2,0},{1,3},{3,1},{4,6},{6,4},{5,7},{7,5},{8,10},{10,8},{9,1... | collective-permute-start | bytes 184328 | tf_op jit(solution)/shard_map/ppermute | solution.py:255
  9.5 4.0 %collective-permute-start.2 = (bf16[3,80,128]{2,1,0:T(8,128)(2,1)S(1)}, bf16[3,80,128]{2,1,0:T(8,128)(2,1)S(1)}, u32[]{:S(2)}, u32[]{:S(2)}) collective-permute-start(bf16[3,80,128]{2,1,0:T(8,128)(2,1)S(1)} %pad_maximum_fusion.refs_0_.refs_1_), channel_id=1, source_target_pairs={{0,1},{1,0},{2,3},{3,2},{4,5},{5,4},{6,7},{7,6},{8,9},{9,8},{10,11... | collective-permute-start | bytes 184328 | tf_op jit(solution)/shard_map/ppermute | solution.py:255
  9.8 0.7 %copy-start.5 = (f32[128]{0:T(128)S(1)}, f32[128]{0:T(128)}, u32[]{:S(2)}) copy-start(f32[128]{0:T(128)} %param.17) | copy-start | bytes 1540
  9.8 0.7 %copy-start.6 = (f32[128]{0:T(128)S(1)}, f32[128]{0:T(128)}, u32[]{:S(2)}) copy-start(f32[128]{0:T(128)} %param.19) | copy-start | bytes 1540
  10.4 3.1 %copy-start.2 = (bf16[128,128]{1,0:T(8,128)(2,1)S(1)}, bf16[128,128]{1,0:T(8,128)(2,1)}, u32[]{:S(2)}) copy-start(bf16[128,128]{1,0:T(8,128)(2,1)} %refs_9_.1) | copy-start | bytes 98308
  10.4 3.1 %copy-start.3 = (bf16[128,128]{1,0:T(8,128)(2,1)S(1)}, bf16[128,128]{1,0:T(8,128)(2,1)}, u32[]{:S(2)}) copy-start(bf16[128,128]{1,0:T(8,128)(2,1)} %refs_11_.1) | copy-start | bytes 98308
  13.5 0.7 %copy-start.7 = (f32[128]{0:T(128)S(1)}, f32[128]{0:T(128)}, u32[]{:S(2)}) copy-start(f32[128]{0:T(128)} %param.21) | copy-start | bytes 1540
  13.5 0.7 %copy-start.8 = (f32[128]{0:T(128)S(1)}, f32[128]{0:T(128)}, u32[]{:S(2)}) copy-start(f32[128]{0:T(128)} %param.23) | copy-start | bytes 1540

commit v3 on v2

v3 whole, which is shorter than its diff:
```python
import math

import jax
import jax.numpy as jnp
import numpy as np
from jax import lax
from jax.experimental import pallas as pl
from jax.experimental.pallas import tpu as pltpu
from jax.sharding import PartitionSpec as P

LOG_TWO = 0.6931471805599453
LOG2_E = 1.4426950408889634
BASIS_GAMMA = 10.0
CELL_EDGE = 5.0
GAP_SCALE = math.sqrt(BASIS_GAMMA * LOG2_E)
FAR = 8.0
PAD_K = 64
EXTRA = 16

COS_SERIES = [(-1.0) ** m * (math.pi / 2) ** (2 * m) / math.factorial(2 * m) for m in range(9)]
F32, BF16 = jnp.float32, jnp.bfloat16
NT = (((1,), (1,)), ((), ()))


def split_bf16(values, parts):
    out = []
    rest = values
    for _ in range(parts):
        head = rest.astype(BF16)
        out.append(head)
        rest = rest - head.astype(F32)
    return out


def pack_kernel(counts_ref, atoms_ref, places_ref, out_ref):
    cells, a, f = atoms_ref.shape
    for c in range(cells):
        out_ref[c * a : (c + 1) * a, :] = atoms_ref[c]
    cell = lax.broadcasted_iota(jnp.int32, (cells, a), 0)
    slot = lax.broadcasted_iota(jnp.int32, (cells, a), 1)
    filled = jnp.zeros((cells, a), jnp.int32)
    for c in range(cells):
        filled = jnp.where(cell == c, counts_ref[c], filled)
    out_ref[cells * a :, :] = jnp.zeros((out_ref.shape[0] - cells * a, f), BF16)
    spots = [jnp.where(slot < filled, places_ref[d].astype(F32), FAR) for d in range(3)]
    table = jnp.concatenate(spots, axis=0)
    out_ref[cells * a : cells * a + 3 * cells, :a] = table.astype(BF16)


def spread(a, lanes, rows, by_j):
    row = lax.broadcasted_iota(jnp.int32, (rows, lanes), 0)
    lane = lax.broadcasted_iota(jnp.int32, (1, lanes), 1)
    return (row == (lane % a if by_j else lane // a)).astype(F32).astype(BF16)


def project(block, p, c, a, in_t):
    rows = block[p, c * a : (c + 1) * a, :]
    return lax.dot_general(in_t[...], jnp.concatenate([rows] * (128 // a), axis=0), NT, preferred_element_type=F32)


def spots(block, p, base, by_j):
    return jnp.dot(block[p, base : base + 16, :], by_j[...], preferred_element_type=F32)


def pair_terms(there, own, moves, drop):
    square = None
    for d, move in enumerate(moves):
        gap = there[d] - own[d]
        if len(move) == 2:
            gap = jnp.minimum(jnp.abs(gap + 1.0), jnp.abs(gap - 1.0))
        else:
            gap = gap + float(move[0])
        square = gap * gap if square is None else square + gap * gap
    far = jnp.sqrt(square)
    cosine = jnp.full(square.shape, COS_SERIES[-1], F32)
    for term in COS_SERIES[-2::-1]:
        cosine = cosine * square + term
    keep = CELL_EDGE * far < CELL_EDGE
    if drop is not None:
        keep = keep & drop
    return far * (CELL_EDGE * GAP_SCALE), jnp.where(keep, cosine * cosine * LOG_TWO, 0.0)


def add_pairs(units, cells, lanes, w1, w2, acc, k, f):
    reps = lanes // 128
    centers = lax.broadcasted_iota(jnp.int32, (PAD_K, 128), 0).astype(F32)
    centers = centers * (GAP_SCALE * CELL_EDGE / (k - 1))
    centers = jnp.concatenate([centers] * reps, axis=1)
    ones = jnp.ones((EXTRA, lanes), BF16)
    totals = [None] * cells
    left = [sum(u[0] == c for u in units) for c in range(cells)]
    first, second = {}, {}
    for n in range(len(units) + 2):
        if n < len(units):
            gap = (units[n][1]() - centers).astype(BF16)
            grid = jnp.exp2(gap * -gap)
            first[n] = jnp.dot(w1[...], jnp.concatenate([grid, ones], axis=0), preferred_element_type=F32)
        if 0 <= n - 1 < len(units):
            hidden = first.pop(n - 1).astype(BF16)
            hidden = jnp.log2(jnp.exp2(hidden) + jnp.array(0.5, BF16))
            weight = jnp.broadcast_to(units[n - 1][2](), (EXTRA, lanes)).astype(BF16)
            hidden = (hidden.reshape(f // EXTRA, EXTRA, lanes) * weight[None]).reshape(f, lanes)
            second[n - 1] = jnp.dot(w2[...], jnp.concatenate([hidden, weight], axis=0), preferred_element_type=F32)
        if 0 <= n - 2 < len(units):
            c = units[n - 2][0]
            term = second.pop(n - 2) * jnp.concatenate([units[n - 2][3]()] * reps, axis=1)
            totals[c] = term if totals[c] is None else totals[c] + term
            left[c] -= 1
            if left[c] == 0:
                acc[c] += totals[c]


def unit(rads, wgts, proj, c, at, cell):
    return (c, lambda: rads[at, c : c + 1, :], lambda: wgts[at, c : c + 1, :], lambda: proj[cell])


def inside(cells):
    return [(c, r) for c in range(cells) for r in range(3) if 0 <= c + r - 1 < cells]


def window(zrow, tables, cells):
    for d in range(3):
        low, mid, high = (t[d * cells : (d + 1) * cells] for t in tables)
        zrow[d, 1 + cells : 1 + 2 * cells, :] = high
        zrow[d, 1 : 1 + cells, :] = mid
        zrow[d, 0:1, :] = low[cells - 1 : cells]


def own_rows(own, cells):
    return [own[d * cells : (d + 1) * cells, :] for d in range(3)]


def first_kernel(
    sizes, packed, in_w, basis_w, basis_b, filt_w, filt_b, dense_w, dense_b, final_w, final_b,
    acc, w1, w2, in_t, dense_o, final_o, biases, by_j, pick, own, proj, zrow, rads, wgts
):
    cells, a, f, k = sizes
    lanes, base = a * a, cells * a
    w1[...] = jnp.zeros(w1.shape, BF16)
    w1[:, :k] = (basis_w[...].astype(F32).T * LOG2_E).astype(BF16)
    bias = (basis_b[...] * LOG2_E - 1.0).T
    for n, part in enumerate(split_bf16(bias, 3)):
        w1[:, PAD_K + n : PAD_K + n + 1] = part
    w2[...] = jnp.zeros(w2.shape, BF16)
    w2[:, :f] = filt_w[...].astype(F32).T.astype(BF16)
    for n, part in enumerate(split_bf16(filt_b[...].T * LOG2_E, 2)):
        w2[:, f + n : f + n + 1] = part
    in_t[...] = in_w[...].astype(F32).T.astype(BF16)
    dense_o[...] = dense_w[...]
    final_o[...] = final_w[...]
    biases[0:1, :] = dense_b[...]
    biases[1:2, :] = final_b[...]
    by_j[...] = spread(a, lanes, f, True)
    pick[...] = spread(a, lanes, a, False)
    line = packed.reshape(1, *packed.shape)
    own[...] = spots(line, 0, base, spread(a, lanes, f, False))
    table = spots(line, 0, base, by_j)
    window(zrow, (table, table, table), cells)
    small = lax.broadcasted_iota(jnp.int32, (1, lanes), 1)
    other = small % a != small // a
    for c in range(cells):
        proj[c] = project(line, 0, c, a, in_t)
    for r in range(3):
        there = [zrow[d, r : r + cells, :] for d in range(3)]
        moves = ((0,), (0,), (r - 1,))
        rads[r], wgts[r] = pair_terms(there, own_rows(own, cells), moves, other if r == 1 else None)
    acc[...] = jnp.zeros(acc.shape, F32)
    units = [unit(rads, wgts, proj, c, r, c + r - 1) for c, r in inside(cells)]
    add_pairs(units, cells, lanes, w1, w2, acc, k, f)


def near_kernel(sizes, line, low_line, high_line, own, w1, w2, in_t, by_j, acc, proj, zrow, rads, wgts):
    cells, a, f, k = sizes
    lanes, base, wide = a * a, cells * a, cells + 2
    for p in range(3):
        proj[p * wide] = project(low_line, p, cells - 1, a, in_t)
        proj[p * wide + cells + 1] = project(high_line, p, 0, a, in_t)
        for c in range(cells if p != 1 else 0):
            proj[p * wide + c + 1] = project(line, p, c, a, in_t)
        window(zrow, [spots(l, p, base, by_j) for l in (low_line, line, high_line)], cells)
        for r in range(3):
            there = [zrow[d, r : r + cells, :] for d in range(3)]
            moves = ((1 - p,), (0,), (r - 1,))
            rads[p * 3 + r], wgts[p * 3 + r] = pair_terms(there, own_rows(own, cells), moves, None)
    acc[...] = jnp.zeros(acc.shape, F32)

    def step(t, carry):
        p = 2 * t
        units = [unit(rads, wgts, proj, c, p * 3 + r, p * wide + c + r) for c in range(cells) for r in range(3)]
        add_pairs(units, cells, lanes, w1, w2, acc, k, f)
        return carry

    lax.fori_loop(0, 2, step, 0)
    units = [unit(rads, wgts, proj, c, 3 + r, wide + c + r) for c, r in ((0, 0), (cells - 1, 2))]
    add_pairs(units, cells, lanes, w1, w2, acc, k, f)


def plane_kernel(sizes, ways, *refs):
    cells, a, f, k = sizes
    lines, refs = refs[: len(ways)], refs[len(ways) :]
    own, w1, w2, in_t, by_j, acc, proj, zrow, rads, wgts = refs
    lanes, base, n_ways = a * a, cells * a, len(ways)
    for p in range(3):
        for way, moves_y in enumerate(ways):
            at = p * n_ways + way
            for c in range(cells):
                proj[at * cells + c] = project(lines[way], p, c, a, in_t)
            window(zrow, [spots(lines[way], p, base, by_j)] * 3, cells)
            for r in range(3):
                there = [zrow[d, r : r + cells, :] for d in range(3)]
                moves = ((1 - p,), moves_y, (r - 1,))
                rads[at * 3 + r], wgts[at * 3 + r] = pair_terms(there, own_rows(own, cells), moves, None)
    acc[...] = jnp.zeros(acc.shape, F32)

    def step(at, carry):
        units = [unit(rads, wgts, proj, c, at * 3 + r, at * cells + c + r - 1) for c, r in inside(cells)]
        add_pairs(units, cells, lanes, w1, w2, acc, k, f)
        return carry

    lax.fori_loop(0, 3 * n_ways, step, 0)


def last_kernel(sizes, ways, counts_ref, *refs):
    cells, a, f, k = sizes
    lows, highs, refs = refs[: len(ways)], refs[len(ways) : 2 * len(ways)], refs[2 * len(ways) :]
    packed, own, w1, w2, in_t, by_j, pick, dense_w, final_w, biases, acc0, acc1, acc2 = refs[:13]
    out_ref, acc, proj, rads, wgts = refs[13:]
    lanes, base, n_ways = a * a, cells * a, len(ways)
    coords = own_rows(own, cells)
    units = []
    for p in range(3):
        for way, moves_y in enumerate(ways):
            for high in range(2):
                block, cell, c, r = (highs[way], 0, cells - 1, 2) if high else (lows[way], cells - 1, 0, 0)
                at = (p * n_ways + way) * 2 + high
                proj[at] = project(block, p, cell, a, in_t)
                table = spots(block, p, base, by_j)
                there = [table[d * cells + cell : d * cells + cell + 1] for d in range(3)]
                here = [coords[d][c : c + 1] for d in range(3)]
                moves = ((1 - p,), moves_y, (r - 1,))
                rads[at], wgts[at] = pair_terms(there, here, moves, None)
                units.append((
                    c, lambda at=at: rads[at], lambda at=at: wgts[at], lambda at=at: proj[at],
                ))
    acc[...] = acc0[...] + acc1[...] + acc2[...]
    add_pairs(units, cells, lanes, w1, w2, acc, k, f)

    messages = []
    for c in range(cells):
        head, tail = split_bf16(acc[c], 2)
        messages.append(
            lax.dot_general(pick[...], head, NT, preferred_element_type=F32)
            + lax.dot_general(pick[...], tail, NT, preferred_element_type=F32)
        )
    message = jnp.concatenate(messages, axis=0).astype(BF16)
    inner = jnp.dot(message, dense_w[...], preferred_element_type=F32) + biases[0:1, :]
    inner = (jax.nn.softplus(inner) - LOG_TWO).astype(BF16)
    update = jnp.dot(inner, final_w[...], preferred_element_type=F32) + biases[1:2, :]
    slot = lax.broadcasted_iota(jnp.int32, (a, f), 0)
    for c in range(cells):
        here = packed[c * a : (c + 1) * a, :].astype(F32)
        value = here + update[c * a : (c + 1) * a]
        out_ref[c] = jnp.where(slot < counts_ref[c], value, 0.0).astype(BF16)


def shifted(value, steps):
    axes = [axis for axis, s in steps if s % lax.axis_size(axis)]
    if not axes:
        return value
    sizes = [lax.axis_size(axis) for axis in axes]
    moves = [dict(steps)[axis] for axis in axes]
    pairs = []
    for at in np.ndindex(*sizes):
        to = [(i + s) % n for i, s, n in zip(at, moves, sizes)]
        pairs.append((int(np.ravel_multi_index(at, sizes)), int(np.ravel_multi_index(to, sizes))))
    return lax.ppermute(value, tuple(axes), pairs)


def on_chip(value):
    return pltpu.with_memory_space_constraint(value, pltpu.VMEM)


def shards(
    atoms,
    places,
    counts,
    in_weight,
    basis_weight,
    basis_bias,
    filter_weight,
    filter_bias,
    dense_weight,
    dense_bias,
    final_weight,
    final_bias,
):
    cells_x, cells_y, cells_z, a, f = atoms.shape
    assert cells_x == 1 and cells_y == 1
    cells = cells_z
    k = basis_weight.shape[0]
    lanes = a * a
    sizes = (cells, a, f, k)
    vmem = pl.BlockSpec(memory_space=pltpu.VMEM)
    smem = pl.BlockSpec(memory_space=pltpu.SMEM)
    counts = counts.reshape(cells)
    packed = pl.pallas_call(
        pack_kernel,
        out_shape=pltpu.VMEM((cells * a + 16, f), BF16),
        in_specs=[smem, vmem, vmem],
        out_specs=vmem,
    )(counts, atoms.reshape(cells, a, f), jnp.swapaxes(places, 2, 3).reshape(3, cells, a))
    above = shifted(packed, [("gx", -1)])
    below = shifted(packed, [("gx", 1)])
    sums = pltpu.VMEM((cells, f, lanes), F32)
    row = pltpu.VMEM((3, 16, lanes), F32)

    def call(kernel, out_shape, scratch, args, scalars=()):
        single = not isinstance(out_shape, list)
        return pl.pallas_call(
            kernel,
            out_shape=out_shape,
            in_specs=[smem] * len(scalars) + [vmem] * len(args),
            out_specs=vmem if single else [vmem] * len(out_shape),
            scratch_shapes=scratch,
            cost_estimate=pl.CostEstimate(flops=10**9, transcendentals=10**6, bytes_accessed=10**6),
        )(*scalars, *args)

    def tiles(n):
        return pltpu.VMEM((n, f, 128), F32)

    def terms(n, rows):
        return [pltpu.VMEM((n, rows, lanes), F32)] * 2

    acc0, w1, w2, in_t, dense_w, final_w, biases, by_j, pick, own = call(
        lambda *refs: first_kernel(sizes, *refs),
        [
            sums,
            pltpu.VMEM((f, PAD_K + EXTRA), BF16),
            pltpu.VMEM((f, f + EXTRA), BF16),
            pltpu.VMEM((f, f), BF16),
            pltpu.VMEM((f, f), BF16),
            pltpu.VMEM((f, f), BF16),
            pltpu.VMEM((2, f), F32),
            pltpu.VMEM((f, lanes), BF16),
            pltpu.VMEM((a, lanes), BF16),
            pltpu.VMEM((16, lanes), F32),
        ],
        [tiles(cells), row] + terms(3, cells),
        (
            on_chip(packed),
            in_weight,
            basis_weight,
            basis_bias.reshape(1, f),
            filter_weight,
            filter_bias.reshape(1, f),
            dense_weight,
            dense_bias.reshape(1, f),
            final_weight,
            final_bias.reshape(1, f),
        ),
    )
    above, below, acc0 = lax.optimization_barrier((above, below, acc0))
    line = jnp.stack([above, packed, below])

    y_steps, ways = ([1], [(1, -1)]) if lax.axis_size("gy") == 2 else ([1, -1], [(1,), (-1,)])
    z_steps = [1] if lax.axis_size("gz") == 2 else [-1, 1]
    y_lines = [shifted(line, [("gy", -y)]) for y in y_steps]
    near_z = [shifted(line, [("gz", -z)]) for z in z_steps]

    n_ways = len(ways)
    shared = tuple(map(on_chip, (own, w1, w2, in_t, by_j)))
    acc1 = call(
        lambda *refs: near_kernel(sizes, *refs),
        sums,
        [tiles(3 * (cells + 2)), row] + terms(9, cells),
        (on_chip(line), on_chip(near_z[0]), on_chip(near_z[-1])) + shared,
    )
    y_lines, acc1 = lax.optimization_barrier((y_lines, acc1))
    far_z = [[shifted(y_line, [("gz", -z)]) for z in z_steps] for y_line in y_lines]
    acc2 = call(
        lambda *refs: plane_kernel(sizes, ways, *refs),
        sums,
        [tiles(3 * n_ways * cells), row] + terms(9 * n_ways, cells),
        tuple(map(on_chip, y_lines)) + shared,
    )
    far_z, acc2 = lax.optimization_barrier((far_z, acc2))
    out = call(
        lambda *refs: last_kernel(sizes, ways, *refs),
        jax.ShapeDtypeStruct((cells, a, f), BF16),
        [sums, tiles(6 * n_ways)] + terms(6 * n_ways, 1),
        tuple(map(on_chip, [z[0] for z in far_z] + [z[-1] for z in far_z] + [packed]))
        + shared
        + tuple(map(on_chip, (pick, dense_w, final_w, biases, acc0, acc1, acc2))),
        (counts,),
    )
    return out.reshape(atoms.shape)


def solution(mesh):
    placed = (
        P(("groups", "gx"), "gy", "gz", None, None),
        P(("groups", "gx"), "gy", "gz", None, None),
        P(("groups", "gx"), "gy", "gz"),
    ) + (P(),) * 9
    return jax.shard_map(
        shards,
        mesh=mesh,
        in_specs=placed,
        out_specs=P(("groups", "gx"), "gy", "gz", None, None),
        check_vma=False,
    )
```

time: 19.8 us -> 17.9 us (0.904)
  waiting for transfers between devices: 2.29 us -> 0.16 us
  Pallas kernels: 8.8 us -> 10.4 us
  local copies, waits for them, and re-layouts: 1.33 us -> 0 us
    ppermute x5, waiting for transfers between devices: 2.29 us -> 0.16 us  [shifted(): return lax.ppermute(value, tuple(axes), pairs)]
    pallas_call x2 -> x4, Pallas kernels: 8.06 us -> 9.62 us  [call(): pl.pallas_call(kernel, out_shape=out_shape, in_specs=[smem] * len(scalars...]
    unnamed x18 -> x0, local copies, waits for them, and re-layouts: 1.33 us -> none
  transfers between devices with their start and end apart: 5 -> 5, of which waited for: 3 -> 1; matrix products, arithmetic and copies ran while one was open for 0% -> 0% of each run, Pallas kernels for 14% -> 41%
where the time goes in v3:
time: 17.9 us; the launch traced here: 17.6 us
  Pallas kernels  10.4 us (58%)
  starting transfers between devices  7.06 us (39%)
    pallas_call x4, Pallas kernels, call(): pl.pallas_call(kernel, out_shape=out_shape, in_specs=[smem] * len(scalars...  9.62 us
    ppermute x5, starting transfers between devices, shifted(): return lax.ppermute(value, tuple(axes), pairs)  7.06 us
    pallas_call x1, Pallas kernels, shards(): pl.pallas_call(pack_kernel, out_shape=pltpu.VMEM((cells * a + 16, f), BF1...  0.74 us
  transfers between devices with their start and end apart: 5, of which 1 were waited for; matrix products, arithmetic and copies ran while one was open for 0% of the time, Pallas kernels for 41%

profile of v3, /device:TPU:0, one launch (start us, length us, event | category | flops | bytes accessed | tf_op | source)
XLA Modules:
  0.0 17.6 jit_solution(6348930849958533451)
XLA Ops:
  0.0 0.7 %shard_map.118.refs_0_.refs_3_ = bf16[80,128]{1,0:T(8,128)(2,1)S(1)} custom-call(s32[4]{0:T(128)} %bitcast.18, bf16[4,16,128]{2,1,0:T(8,128)(2,1)} %bitcast.16, bf16[3,4,16]{2,1,0:T(4,128)(2,1)} %bitcast.17), custom_call_target="tpu_custom_call" | custom-call | tf_op jit(solution)/shard_map/pallas_call | solution.py:306
  0.7 3.1 %collective-permute-start.1 = (bf16[80,128]{1,0:T(8,128)(2,1)S(1)}, bf16[80,128]{1,0:T(8,128)(2,1)S(1)}, u32[]{:S(2)}, u32[]{:S(2)}) collective-permute-start(bf16[80,128]{1,0:T(8,128)(2,1)S(1)} %shard_map.118.refs_0_.refs_3_), channel_id=1, source_target_pairs={{0,4},{4,8},{8,12},{12,0},{1,5},{5,9},{9,13},{13,1},{2,6},{6,10},{... | collective-permute-start | bytes 61448 | tf_op jit(solution)/shard_map/ppermute | solution.py:276
  3.8 2.1 %collective-permute-start = (bf16[80,128]{1,0:T(8,128)(2,1)S(1)}, bf16[80,128]{1,0:T(8,128)(2,1)S(1)}, u32[]{:S(2)}, u32[]{:S(2)}) collective-permute-start(bf16[80,128]{1,0:T(8,128)(2,1)S(1)} %shard_map.118.refs_0_.refs_3_), channel_id=1, source_target_pairs={{0,12},{4,0},{8,4},{12,8},{1,13},{5,1},{9,5},{13,9},{2,14},{6,2},{... | collective-permute-start | bytes 61448 | tf_op jit(solution)/shard_map/ppermute | solution.py:276
  5.9 1.8 %shard_map.119 = (f32[4,128,256]{2,1,0:T(8,128)S(1)}, bf16[128,80]{1,0:T(8,128)(2,1)S(1)}, bf16[128,144]{1,0:T(8,128)(2,1)S(1)}, bf16[128,128]{1,0:T(8,128)(2,1)...) custom-call(bf16[80,128]{1,0:T(8,128)(2,1)S(1)} %shard_map.118.refs_, ...), custom_call_target="tpu_custom_call" | custom-call | flops 1000000000 | bytes 1000000 | tf_op jit(solution)/shard_map/pallas_call | solution.py:319
  7.8 0.0 collective-permute-done.1
  7.8 0.0 collective-permute-done
  7.8 0.1 collective-permute-start.3
  7.9 1.7 %collective-permute-start.2 = (bf16[3,80,128]{2,1,0:T(8,128)(2,1)S(1)}, bf16[3,80,128]{2,1,0:T(8,128)(2,1)S(1)}, u32[]{:S(2)}, u32[]{:S(2)}) collective-permute-start(bf16[3,80,128]{2,1,0:T(8,128)(2,1)S(1)} %pad_maximum_fusion.refs_0_), channel_id=1, source_target_pairs={{0,2},{2,0},{1,3},{3,1},{4,6},{6,4},{5,7},{7,5},{8,10},{10,8},{9,1... | collective-permute-start | bytes 184328 | tf_op jit(solution)/shard_map/ppermute | solution.py:276
  9.6 0.0 collective-permute-done.3.refs_1_.refs_2_
  9.6 2.6 %shard_map.120.refs_14_ = f32[4,128,256]{2,1,0:T(8,128)S(1)} custom-call(bf16[3,80,128]{2,1,0:T(8,128)(2,1)S(1)} %pad_maximum_fusion.refs_0_, bf16[3,80,128]{2,1,0:T(8,128)(2,1)S(1)} %collective-permute-done.3.refs_1_.refs_2_, bf16[3,80,128]{2,1,0:T(8,128)(2,1)S(1)} %collective-permute-done.3.refs_1_.refs_2_, ...), custom_call_target="tpu_custom_call" | custom-call | flops 1000000000 | bytes 1000000 | tf_op jit(solution)/shard_map/pallas_call | solution.py:319
  12.2 0.1 collective-permute-done.2.refs_0_
  12.3 0.1 collective-permute-start.4
  12.5 2.7 %shard_map.121.refs_15_ = f32[4,128,256]{2,1,0:T(8,128)S(1)} custom-call(bf16[3,80,128]{2,1,0:T(8,128)(2,1)S(1)} %collective-permute-done.2.refs_0_, f32[16,256]{1,0:T(8,128)S(1)} %get-tuple-element.25.refs_3_.refs_1_.refs_4_, bf16[128,80]{1,0:T(8,128)(2,1)S(1)} %get-tuple-element.26.refs_4_.refs_2_.refs_5_, ...), custom_call_target="tpu_custom_call" | custom-call | flops 1000000000 | bytes 1000000 | tf_op jit(solution)/shard_map/pallas_call | solution.py:319
  15.2 0.0 collective-permute-done.4.refs_1_.refs_2_
  15.2 2.5 %shard_map.122 = bf16[4,16,128]{2,1,0:T(8,128)(2,1)} custom-call(s32[4]{0:T(128)} %bitcast.19, bf16[3,80,128]{2,1,0:T(8,128)(2,1)S(1)} %collective-permute-done.4.refs_1_.refs_2_, bf16[3,80,128]{2,1,0:T(8,128)(2,1)S(1)} %collective-permute-done.4.refs_1_.refs_2_, bf16[80,128]{1,0:T(8,128)(2,1)S(1)} %shard_map.118.refs_0_.refs_3_, ...), custom_call_target="tpu_custom_call" | custom-call | flops 1000000000 | bytes 1000000 | tf_op jit(solution)/shard_map/pallas_call | solution.py:319
  (1 shorter events, 0.0 us)
Async XLA Ops:
  0.7 7.0 %collective-permute-start.1 = (bf16[80,128]{1,0:T(8,128)(2,1)S(1)}, bf16[80,128]{1,0:T(8,128)(2,1)S(1)}, u32[]{:S(2)}, u32[]{:S(2)}) collective-permute-start(bf16[80,128]{1,0:T(8,128)(2,1)S(1)} %shard_map.118.refs_0_.refs_3_), channel_id=1, source_target_pairs={{0,4},{4,8},{8,12},{12,0},{1,5},{5,9},{9,13},{13,1},{2,6},{6,10},{... | collective-permute-start | bytes 61448 | tf_op jit(solution)/shard_map/ppermute | solution.py:276
  3.8 4.0 %collective-permute-start = (bf16[80,128]{1,0:T(8,128)(2,1)S(1)}, bf16[80,128]{1,0:T(8,128)(2,1)S(1)}, u32[]{:S(2)}, u32[]{:S(2)}) collective-permute-start(bf16[80,128]{1,0:T(8,128)(2,1)S(1)} %shard_map.118.refs_0_.refs_3_), channel_id=1, source_target_pairs={{0,12},{4,0},{8,4},{12,8},{1,13},{5,1},{9,5},{13,9},{2,14},{6,2},{... | collective-permute-start | bytes 61448 | tf_op jit(solution)/shard_map/ppermute | solution.py:276
  7.8 1.8 %collective-permute-start.3 = (bf16[3,80,128]{2,1,0:T(8,128)(2,1)S(1)}, bf16[3,80,128]{2,1,0:T(8,128)(2,1)S(1)}, u32[]{:S(2)}, u32[]{:S(2)}) collective-permute-start(bf16[3,80,128]{2,1,0:T(8,128)(2,1)S(1)} %pad_maximum_fusion.refs_0_), channel_id=1, source_target_pairs={{0,1},{1,0},{2,3},{3,2},{4,5},{5,4},{6,7},{7,6},{8,9},{9,8},{10,11... | collective-permute-start | bytes 184328 | tf_op jit(solution)/shard_map/ppermute | solution.py:276
  7.9 4.4 %collective-permute-start.2 = (bf16[3,80,128]{2,1,0:T(8,128)(2,1)S(1)}, bf16[3,80,128]{2,1,0:T(8,128)(2,1)S(1)}, u32[]{:S(2)}, u32[]{:S(2)}) collective-permute-start(bf16[3,80,128]{2,1,0:T(8,128)(2,1)S(1)} %pad_maximum_fusion.refs_0_), channel_id=1, source_target_pairs={{0,2},{2,0},{1,3},{3,1},{4,6},{6,4},{5,7},{7,5},{8,10},{10,8},{9,1... | collective-permute-start | bytes 184328 | tf_op jit(solution)/shard_map/ppermute | solution.py:276
  12.3 2.8 %collective-permute-start.4 = (bf16[3,80,128]{2,1,0:T(8,128)(2,1)S(1)}, bf16[3,80,128]{2,1,0:T(8,128)(2,1)S(1)}, u32[]{:S(2)}, u32[]{:S(2)}) collective-permute-start(bf16[3,80,128]{2,1,0:T(8,128)(2,1)S(1)} %collective-permute-done.2.refs_0_), channel_id=1, source_target_pairs={{0,1},{1,0},{2,3},{3,2},{4,5},{5,4},{6,7},{7,6},{8,9},{9,8},{10,11... | collective-permute-start | bytes 184328 | tf_op jit(solution)/shard_map/ppermute | solution.py:276

commit v4 on v3

--- a/solution.py
+++ b/solution.py
@@ -81,7 +81,7 @@
     return far * (CELL_EDGE * GAP_SCALE), jnp.where(keep, cosine * cosine * LOG_TWO, 0.0)
 
 
-def add_pairs(units, cells, lanes, w1, w2, acc, k, f):
+def add_pairs(units, cells, lanes, w1, w2, acc, k, f, start=None):
     reps = lanes // 128
     centers = lax.broadcasted_iota(jnp.int32, (PAD_K, 128), 0).astype(F32)
     centers = centers * (GAP_SCALE * CELL_EDGE / (k - 1))
@@ -92,12 +92,11 @@
     first, second = {}, {}
     for n in range(len(units) + 2):
         if n < len(units):
-            gap = (units[n][1]() - centers).astype(BF16)
-            grid = jnp.exp2(gap * -gap)
+            gap = units[n][1]() - centers
+            grid = jnp.exp2(gap * -gap).astype(BF16)
             first[n] = jnp.dot(w1[...], jnp.concatenate([grid, ones], axis=0), preferred_element_type=F32)
         if 0 <= n - 1 < len(units):
-            hidden = first.pop(n - 1).astype(BF16)
-            hidden = jnp.log2(jnp.exp2(hidden) + jnp.array(0.5, BF16))
+            hidden = jnp.log2(jnp.exp2(first.pop(n - 1)) + 0.5).astype(BF16)
             weight = jnp.broadcast_to(units[n - 1][2](), (EXTRA, lanes)).astype(BF16)
             hidden = (hidden.reshape(f // EXTRA, EXTRA, lanes) * weight[None]).reshape(f, lanes)
             second[n - 1] = jnp.dot(w2[...], jnp.concatenate([hidden, weight], axis=0), preferred_element_type=F32)
@@ -107,7 +106,7 @@
             totals[c] = term if totals[c] is None else totals[c] + term
             left[c] -= 1
             if left[c] == 0:
-                acc[c] += totals[c]
+                acc[c] = totals[c] + (acc if start is None else start)[c]
 
 
 def unit(rads, wgts, proj, c, at, cell):
@@ -131,8 +130,8 @@
 
 
 def first_kernel(
-    sizes, packed, in_w, basis_w, basis_b, filt_w, filt_b, dense_w, dense_b, final_w, final_b,
-    acc, w1, w2, in_t, dense_o, final_o, biases, by_j, pick, own, proj, zrow, rads, wgts
+    sizes, counts_ref, packed, in_w, basis_w, basis_b, filt_w, filt_b, dense_w, dense_b, final_w, final_b,
+    acc, w1, w2, in_t, dense_o, final_o, biases, by_j, pick, own, filled, proj, zrow, rads, wgts
 ):
     cells, a, f, k = sizes
     lanes, base = a * a, cells * a
@@ -150,6 +149,9 @@
     final_o[...] = final_w[...]
     biases[0:1, :] = dense_b[...]
     biases[1:2, :] = final_b[...]
+    slot = lax.broadcasted_iota(jnp.int32, (a, f), 0)
+    for c in range(cells):
+        filled[c * a : (c + 1) * a, :] = (slot < counts_ref[c]).astype(F32)
     by_j[...] = spread(a, lanes, f, True)
     pick[...] = spread(a, lanes, a, False)
     line = packed.reshape(1, *packed.shape)
@@ -169,7 +171,7 @@
     add_pairs(units, cells, lanes, w1, w2, acc, k, f)
 
 
-def near_kernel(sizes, line, low_line, high_line, own, w1, w2, in_t, by_j, acc, proj, zrow, rads, wgts):
+def near_kernel(sizes, line, low_line, high_line, own, w1, w2, in_t, by_j, acc0, acc, proj, zrow, rads, wgts):
     cells, a, f, k = sizes
     lanes, base, wide = a * a, cells * a, cells + 2
     for p in range(3):
@@ -182,23 +184,16 @@
             there = [zrow[d, r : r + cells, :] for d in range(3)]
             moves = ((1 - p,), (0,), (r - 1,))
             rads[p * 3 + r], wgts[p * 3 + r] = pair_terms(there, own_rows(own, cells), moves, None)
-    acc[...] = jnp.zeros(acc.shape, F32)
-
-    def step(t, carry):
-        p = 2 * t
-        units = [unit(rads, wgts, proj, c, p * 3 + r, p * wide + c + r) for c in range(cells) for r in range(3)]
-        add_pairs(units, cells, lanes, w1, w2, acc, k, f)
-        return carry
-
-    lax.fori_loop(0, 2, step, 0)
-    units = [unit(rads, wgts, proj, c, 3 + r, wide + c + r) for c, r in ((0, 0), (cells - 1, 2))]
-    add_pairs(units, cells, lanes, w1, w2, acc, k, f)
+    for p in range(3):
+        spans = [(c, r) for c in range(cells) for r in range(3)] if p != 1 else [(0, 0), (cells - 1, 2)]
+        units = [unit(rads, wgts, proj, c, p * 3 + r, p * wide + c + r) for c, r in spans]
+        add_pairs(units, cells, lanes, w1, w2, acc, k, f, acc0 if p == 0 else None)
 
 
 def plane_kernel(sizes, ways, *refs):
     cells, a, f, k = sizes
     lines, refs = refs[: len(ways)], refs[len(ways) :]
-    own, w1, w2, in_t, by_j, acc, proj, zrow, rads, wgts = refs
+    own, w1, w2, in_t, by_j, acc1, acc, proj, zrow, rads, wgts = refs
     lanes, base, n_ways = a * a, cells * a, len(ways)
     for p in range(3):
         for way, moves_y in enumerate(ways):
@@ -210,21 +205,16 @@
                 there = [zrow[d, r : r + cells, :] for d in range(3)]
                 moves = ((1 - p,), moves_y, (r - 1,))
                 rads[at * 3 + r], wgts[at * 3 + r] = pair_terms(there, own_rows(own, cells), moves, None)
-    acc[...] = jnp.zeros(acc.shape, F32)
-
-    def step(at, carry):
+    for at in range(3 * n_ways):
         units = [unit(rads, wgts, proj, c, at * 3 + r, at * cells + c + r - 1) for c, r in inside(cells)]
-        add_pairs(units, cells, lanes, w1, w2, acc, k, f)
-        return carry
-
-    lax.fori_loop(0, 3 * n_ways, step, 0)
-
-
-def last_kernel(sizes, ways, counts_ref, *refs):
+        add_pairs(units, cells, lanes, w1, w2, acc, k, f, acc1 if at == 0 else None)
+
+
+def last_kernel(sizes, ways, *refs):
     cells, a, f, k = sizes
     lows, highs, refs = refs[: len(ways)], refs[len(ways) : 2 * len(ways)], refs[2 * len(ways) :]
-    packed, own, w1, w2, in_t, by_j, pick, dense_w, final_w, biases, acc0, acc1, acc2 = refs[:13]
-    out_ref, acc, proj, rads, wgts = refs[13:]
+    packed, own, w1, w2, in_t, by_j, pick, dense_w, final_w, biases, filled, acc2 = refs[:12]
+    out_ref, acc, proj, rads, wgts = refs[12:]
     lanes, base, n_ways = a * a, cells * a, len(ways)
     coords = own_rows(own, cells)
     units = []
@@ -242,25 +232,20 @@
                 units.append((
                     c, lambda at=at: rads[at], lambda at=at: wgts[at], lambda at=at: proj[at],
                 ))
-    acc[...] = acc0[...] + acc1[...] + acc2[...]
-    add_pairs(units, cells, lanes, w1, w2, acc, k, f)
+    units.sort(key=lambda u: u[0])
+    add_pairs(units, cells, lanes, w1, w2, acc, k, f, acc2)
 
     messages = []
     for c in range(cells):
-        head, tail = split_bf16(acc[c], 2)
-        messages.append(
-            lax.dot_general(pick[...], head, NT, preferred_element_type=F32)
-            + lax.dot_general(pick[...], tail, NT, preferred_element_type=F32)
-        )
+        head = (acc if c in (0, cells - 1) else acc2)[c].astype(BF16)
+        messages.append(lax.dot_general(pick[...], head, NT, preferred_element_type=F32))
     message = jnp.concatenate(messages, axis=0).astype(BF16)
     inner = jnp.dot(message, dense_w[...], preferred_element_type=F32) + biases[0:1, :]
     inner = (jax.nn.softplus(inner) - LOG_TWO).astype(BF16)
     update = jnp.dot(inner, final_w[...], preferred_element_type=F32) + biases[1:2, :]
-    slot = lax.broadcasted_iota(jnp.int32, (a, f), 0)
-    for c in range(cells):
-        here = packed[c * a : (c + 1) * a, :].astype(F32)
-        value = here + update[c * a : (c + 1) * a]
-        out_ref[c] = jnp.where(slot < counts_ref[c], value, 0.0).astype(BF16)
+    value = (packed[: cells * a, :].astype(F32) + update) * filled[...]
+    for c in range(cells):
+        out_ref[c] = value[c * a : (c + 1) * a].astype(BF16)
 
 
 def shifted(value, steps):
@@ -331,7 +316,7 @@
     def terms(n, rows):
         return [pltpu.VMEM((n, rows, lanes), F32)] * 2
 
-    acc0, w1, w2, in_t, dense_w, final_w, biases, by_j, pick, own = call(
+    acc0, w1, w2, in_t, dense_w, final_w, biases, by_j, pick, own, filled = call(
         lambda *refs: first_kernel(sizes, *refs),
         [
             sums,
@@ -344,6 +329,7 @@
             pltpu.VMEM((f, lanes), BF16),
             pltpu.VMEM((a, lanes), BF16),
             pltpu.VMEM((16, lanes), F32),
+            pltpu.VMEM((cells * a, f), F32),
         ],
         [tiles(cells), row] + terms(3, cells),
         (
@@ -358,6 +344,7 @@
             final_weight,
             final_bias.reshape(1, f),
         ),
+        (counts,),
     )
     above, below, acc0 = lax.optimization_barrier((above, below, acc0))
     line = jnp.stack([above, packed, below])
@@ -373,7 +360,7 @@
         lambda *refs: near_kernel(sizes, *refs),
         sums,
         [tiles(3 * (cells + 2)), row] + terms(9, cells),
-        (on_chip(line), on_chip(near_z[0]), on_chip(near_z[-1])) + shared,
+        (on_chip(line), on_chip(near_z[0]), on_chip(near_z[-1])) + shared + (on_chip(acc0),),
     )
     y_lines, acc1 = lax.optimization_barrier((y_lines, acc1))
     far_z = [[shifted(y_line, [("gz", -z)]) for z in z_steps] for y_line in y_lines]
@@ -381,7 +368,7 @@
         lambda *refs: plane_kernel(sizes, ways, *refs),
         sums,
         [tiles(3 * n_ways * cells), row] + terms(9 * n_ways, cells),
-        tuple(map(on_chip, y_lines)) + shared,
+        tuple(map(on_chip, y_lines)) + shared + (on_chip(acc1),),
     )
     far_z, acc2 = lax.optimization_barrier((far_z, acc2))
     out = call(
@@ -390,8 +377,7 @@
         [sums, tiles(6 * n_ways)] + terms(6 * n_ways, 1),
         tuple(map(on_chip, [z[0] for z in far_z] + [z[-1] for z in far_z] + [packed]))
         + shared
-        + tuple(map(on_chip, (pick, dense_w, final_w, biases, acc0, acc1, acc2))),
-        (counts,),
+        + tuple(map(on_chip, (pick, dense_w, final_w, biases, filled, acc2))),
     )
     return out.reshape(atoms.shape)
 

time: 17.9 us -> 16.4 us (0.916)
  Pallas kernels: 10.4 us -> 8.21 us
  waiting for transfers between devices: 0.16 us -> 1.04 us
  starting transfers between devices: 7.06 us -> 6.83 us
    pallas_call x4, Pallas kernels: 9.62 us -> 7.48 us  [call(): pl.pallas_call(kernel, out_shape=out_shape, in_specs=[smem] * len(scalars...]
    ppermute x5, waiting for transfers between devices: 0.16 us -> 1.04 us  [shifted(): return lax.ppermute(value, tuple(axes), pairs)]
    ppermute x5, starting transfers between devices: 7.06 us -> 6.83 us  [shifted(): return lax.ppermute(value, tuple(axes), pairs)]
  transfers between devices with their start and end apart: 5 -> 5, of which waited for: 1 -> 2; matrix products, arithmetic and copies ran while one was open for 0% -> 0% of each run, Pallas kernels for 41% -> 36%
where the time goes in v4:
time: 16.4 us; the launch traced here: 16.1 us
  Pallas kernels  8.21 us (50%)
  starting transfers between devices  6.83 us (42%)
  waiting for transfers between devices  1.04 us (6%)
    pallas_call x4, Pallas kernels, call(): pl.pallas_call(kernel, out_shape=out_shape, in_specs=[smem] * len(scalars...  7.48 us
    ppermute x5, starting transfers between devices, shifted(): return lax.ppermute(value, tuple(axes), pairs)  6.83 us
    ppermute x5, waiting for transfers between devices, shifted(): return lax.ppermute(value, tuple(axes), pairs)  1.04 us
    pallas_call x1, Pallas kernels, shards(): pl.pallas_call(pack_kernel, out_shape=pltpu.VMEM((cells * a + 16, f), BF1...  0.74 us
  transfers between devices with their start and end apart: 5, of which 2 were waited for; matrix products, arithmetic and copies ran while one was open for 0% of the time, Pallas kernels for 36%

profile of v4, /device:TPU:0, one launch (start us, length us, event | category | flops | bytes accessed | tf_op | source)
XLA Modules:
  0.0 16.1 jit_solution(11435176058287300705)
XLA Ops:
  0.0 0.7 %shard_map.118.refs_1_.refs_2_ = bf16[80,128]{1,0:T(8,128)(2,1)S(1)} custom-call(s32[4]{0:T(128)} %bitcast.18, bf16[4,16,128]{2,1,0:T(8,128)(2,1)} %bitcast.16, bf16[3,4,16]{2,1,0:T(4,128)(2,1)} %bitcast.17), custom_call_target="tpu_custom_call" | custom-call | tf_op jit(solution)/shard_map/pallas_call | solution.py:291
  0.7 3.1 %collective-permute-start.1 = (bf16[80,128]{1,0:T(8,128)(2,1)S(1)}, bf16[80,128]{1,0:T(8,128)(2,1)S(1)}, u32[]{:S(2)}, u32[]{:S(2)}) collective-permute-start(bf16[80,128]{1,0:T(8,128)(2,1)S(1)} %shard_map.118.refs_1_.refs_2_), channel_id=1, source_target_pairs={{0,4},{4,8},{8,12},{12,0},{1,5},{5,9},{9,13},{13,1},{2,6},{6,10},{... | collective-permute-start | bytes 61448 | tf_op jit(solution)/shard_map/ppermute | solution.py:261
  3.8 2.1 %collective-permute-start = (bf16[80,128]{1,0:T(8,128)(2,1)S(1)}, bf16[80,128]{1,0:T(8,128)(2,1)S(1)}, u32[]{:S(2)}, u32[]{:S(2)}) collective-permute-start(bf16[80,128]{1,0:T(8,128)(2,1)S(1)} %shard_map.118.refs_1_.refs_2_), channel_id=1, source_target_pairs={{0,12},{4,0},{8,4},{12,8},{1,13},{5,1},{9,5},{13,9},{2,14},{6,2},{... | collective-permute-start | bytes 61448 | tf_op jit(solution)/shard_map/ppermute | solution.py:261
  5.9 1.8 %shard_map.119 = (f32[4,128,256]{2,1,0:T(8,128)S(1)}, bf16[128,80]{1,0:T(8,128)(2,1)S(1)}, bf16[128,144]{1,0:T(8,128)(2,1)S(1)}, bf16[128,128]{1,0:T(8,128)(2,1)...) custom-call(s32[4]{0:T(128)} %bitcast.19, ...), custom_call_target="tpu_custom_call" | custom-call | flops 1000000000 | bytes 1000000 | tf_op jit(solution)/shard_map/pallas_call | solution.py:304
  7.7 0.0 collective-permute-done.1
  7.7 0.1 collective-permute-done
  7.8 0.1 collective-permute-start.3
  7.9 1.6 %collective-permute-start.2 = (bf16[3,80,128]{2,1,0:T(8,128)(2,1)S(1)}, bf16[3,80,128]{2,1,0:T(8,128)(2,1)S(1)}, u32[]{:S(2)}, u32[]{:S(2)}) collective-permute-start(bf16[3,80,128]{2,1,0:T(8,128)(2,1)S(1)} %pad_maximum_fusion.refs_0_), channel_id=1, source_target_pairs={{0,2},{2,0},{1,3},{3,1},{4,6},{6,4},{5,7},{7,5},{8,10},{10,8},{9,1... | collective-permute-start | bytes 184328 | tf_op jit(solution)/shard_map/ppermute | solution.py:261
  9.5 0.0 collective-permute-done.3.refs_1_.refs_2_
  9.5 1.9 %shard_map.120.refs_6_ = f32[4,128,256]{2,1,0:T(8,128)S(1)} custom-call(bf16[3,80,128]{2,1,0:T(8,128)(2,1)S(1)} %pad_maximum_fusion.refs_0_, bf16[3,80,128]{2,1,0:T(8,128)(2,1)S(1)} %collective-permute-done.3.refs_1_.refs_2_, bf16[3,80,128]{2,1,0:T(8,128)(2,1)S(1)} %collective-permute-done.3.refs_1_.refs_2_, ...), custom_call_target="tpu_custom_call" | custom-call | flops 1000000000 | bytes 1000000 | tf_op jit(solution)/shard_map/pallas_call | solution.py:304
  11.4 0.9 %collective-permute-done.2.refs_0_ = bf16[3,80,128]{2,1,0:T(8,128)(2,1)S(1)} collective-permute-done((bf16[3,80,128]{2,1,0:T(8,128)(2,1)S(1)}, bf16[3,80,128]{2,1,0:T(8,128)(2,1)S(1)}, u32[]{:S(2)}, u32[]{:S(2)}) %collective-permute-start.2) | collective-permute-done | bytes 61472 | tf_op jit(solution)/shard_map/ppermute | solution.py:261
  12.3 0.0 collective-permute-start.4
  12.3 2.1 %shard_map.121.refs_13_ = f32[4,128,256]{2,1,0:T(8,128)S(1)} custom-call(bf16[3,80,128]{2,1,0:T(8,128)(2,1)S(1)} %collective-permute-done.2.refs_0_, f32[16,256]{1,0:T(8,128)S(1)} %get-tuple-element.26.refs_3_.refs_1_, bf16[128,80]{1,0:T(8,128)(2,1)S(1)} %get-tuple-element.27.refs_4_.refs_2_, bf16[128,144]{1,0:T(8,128)(2,1)S(1)} %get-tuple-element.28.refs_5_.refs_3_, ...), custom_call_target="tpu_custom_call" | custom-call | flops 1000000000 | bytes 1000000 | tf_op jit(solution)/shard_map/pallas_call | solution.py:304
  14.4 0.0 collective-permute-done.4.refs_0_.refs_1_
  14.4 1.7 %shard_map.122 = bf16[4,16,128]{2,1,0:T(8,128)(2,1)} custom-call(bf16[3,80,128]{2,1,0:T(8,128)(2,1)S(1)} %collective-permute-done.4.refs_0_.refs_1_, bf16[3,80,128]{2,1,0:T(8,128)(2,1)S(1)} %collective-permute-done.4.refs_0_.refs_1_, bf16[80,128]{1,0:T(8,128)(2,1)S(1)} %shard_map.118.refs_1_.refs_2_, f32[16,256]{1,0:T(8,128)S(1)} %get-tuple-element.26.refs_3_.refs_1_, ...), custom_call_target="tpu_custom_call" | custom-call | flops 1000000000 | bytes 1000000 | tf_op jit(solution)/shard_map/pallas_call | solution.py:304
  (1 shorter events, 0.0 us)
Async XLA Ops:
  0.7 7.0 %collective-permute-start.1 = (bf16[80,128]{1,0:T(8,128)(2,1)S(1)}, bf16[80,128]{1,0:T(8,128)(2,1)S(1)}, u32[]{:S(2)}, u32[]{:S(2)}) collective-permute-start(bf16[80,128]{1,0:T(8,128)(2,1)S(1)} %shard_map.118.refs_1_.refs_2_), channel_id=1, source_target_pairs={{0,4},{4,8},{8,12},{12,0},{1,5},{5,9},{9,13},{13,1},{2,6},{6,10},{... | collective-permute-start | bytes 61448 | tf_op jit(solution)/shard_map/ppermute | solution.py:261
  3.8 4.0 %collective-permute-start = (bf16[80,128]{1,0:T(8,128)(2,1)S(1)}, bf16[80,128]{1,0:T(8,128)(2,1)S(1)}, u32[]{:S(2)}, u32[]{:S(2)}) collective-permute-start(bf16[80,128]{1,0:T(8,128)(2,1)S(1)} %shard_map.118.refs_1_.refs_2_), channel_id=1, source_target_pairs={{0,12},{4,0},{8,4},{12,8},{1,13},{5,1},{9,5},{13,9},{2,14},{6,2},{... | collective-permute-start | bytes 61448 | tf_op jit(solution)/shard_map/ppermute | solution.py:261
  7.8 1.7 %collective-permute-start.3 = (bf16[3,80,128]{2,1,0:T(8,128)(2,1)S(1)}, bf16[3,80,128]{2,1,0:T(8,128)(2,1)S(1)}, u32[]{:S(2)}, u32[]{:S(2)}) collective-permute-start(bf16[3,80,128]{2,1,0:T(8,128)(2,1)S(1)} %pad_maximum_fusion.refs_0_), channel_id=1, source_target_pairs={{0,1},{1,0},{2,3},{3,2},{4,5},{5,4},{6,7},{7,6},{8,9},{9,8},{10,11... | collective-permute-start | bytes 184328 | tf_op jit(solution)/shard_map/ppermute | solution.py:261
  7.9 4.4 %collective-permute-start.2 = (bf16[3,80,128]{2,1,0:T(8,128)(2,1)S(1)}, bf16[3,80,128]{2,1,0:T(8,128)(2,1)S(1)}, u32[]{:S(2)}, u32[]{:S(2)}) collective-permute-start(bf16[3,80,128]{2,1,0:T(8,128)(2,1)S(1)} %pad_maximum_fusion.refs_0_), channel_id=1, source_target_pairs={{0,2},{2,0},{1,3},{3,1},{4,6},{6,4},{5,7},{7,5},{8,10},{10,8},{9,1... | collective-permute-start | bytes 184328 | tf_op jit(solution)/shard_map/ppermute | solution.py:261
  12.3 2.1 %collective-permute-start.4 = (bf16[3,80,128]{2,1,0:T(8,128)(2,1)S(1)}, bf16[3,80,128]{2,1,0:T(8,128)(2,1)S(1)}, u32[]{:S(2)}, u32[]{:S(2)}) collective-permute-start(bf16[3,80,128]{2,1,0:T(8,128)(2,1)S(1)} %collective-permute-done.2.refs_0_), channel_id=1, source_target_pairs={{0,1},{1,0},{2,3},{3,2},{4,5},{5,4},{6,7},{7,6},{8,9},{9,8},{10,11... | collective-permute-start | bytes 184328 | tf_op jit(solution)/shard_map/ppermute | solution.py:261

commit v5 on v4

--- a/solution.py
+++ b/solution.py
@@ -53,9 +53,17 @@
     return (row == (lane % a if by_j else lane // a)).astype(F32).astype(BF16)
 
 
-def project(block, p, c, a, in_t):
-    rows = block[p, c * a : (c + 1) * a, :]
-    return lax.dot_general(in_t[...], jnp.concatenate([rows] * (128 // a), axis=0), NT, preferred_element_type=F32)
+def project(proj, slots, in_t, a):
+    reps = 128 // a
+    f = in_t.shape[0]
+    lane = lax.broadcasted_iota(jnp.int32, (1, 128), 1) % a
+    for n in range(0, len(slots), reps):
+        some = slots[n : n + reps]
+        rows = [block[p, c * a : (c + 1) * a, :] for _, block, p, c in some]
+        rows = jnp.concatenate(rows + rows[-1:] * (reps - len(rows)), axis=0)
+        tile = lax.dot_general(in_t[...], rows, NT, preferred_element_type=F32)
+        for m, (at, _, _, _) in enumerate(some):
+            proj[at] = jnp.take_along_axis(tile, jnp.broadcast_to(lane + m * a, (f, 128)), axis=1)
 
 
 def spots(block, p, base, by_j):
@@ -64,9 +72,11 @@
 
 def pair_terms(there, own, moves, drop):
     square = None
-    for d, move in enumerate(moves):
-        gap = there[d] - own[d]
-        if len(move) == 2:
+    for d, move in enumerate(moves or ((), (), ())):
+        gap = there[d] if own is None else there[d] - own[d]
+        if len(move) == 0:
+            pass
+        elif len(move) == 2:
             gap = jnp.minimum(jnp.abs(gap + 1.0), jnp.abs(gap - 1.0))
         else:
             gap = gap + float(move[0])
@@ -87,8 +97,7 @@
     centers = centers * (GAP_SCALE * CELL_EDGE / (k - 1))
     centers = jnp.concatenate([centers] * reps, axis=1)
     ones = jnp.ones((EXTRA, lanes), BF16)
-    totals = [None] * cells
-    left = [sum(u[0] == c for u in units) for c in range(cells)]
+    total, opened = None, set()
     first, second = {}, {}
     for n in range(len(units) + 2):
         if n < len(units):
@@ -103,10 +112,11 @@
         if 0 <= n - 2 < len(units):
             c = units[n - 2][0]
             term = second.pop(n - 2) * jnp.concatenate([units[n - 2][3]()] * reps, axis=1)
-            totals[c] = term if totals[c] is None else totals[c] + term
-            left[c] -= 1
-            if left[c] == 0:
-                acc[c] = totals[c] + (acc if start is None else start)[c]
+            total = term if total is None else total + term
+            if n - 1 == len(units) or units[n - 1][0] != c:
+                acc[c] = total + (acc if start is None or c in opened else start)[c]
+                total = None
+                opened.add(c)
 
 
 def unit(rads, wgts, proj, c, at, cell):
@@ -160,8 +170,7 @@
     window(zrow, (table, table, table), cells)
     small = lax.broadcasted_iota(jnp.int32, (1, lanes), 1)
     other = small % a != small // a
-    for c in range(cells):
-        proj[c] = project(line, 0, c, a, in_t)
+    project(proj, [(c, line, 0, c) for c in range(cells)], in_t, a)
     for r in range(3):
         there = [zrow[d, r : r + cells, :] for d in range(3)]
         moves = ((0,), (0,), (r - 1,))
@@ -174,20 +183,22 @@
 def near_kernel(sizes, line, low_line, high_line, own, w1, w2, in_t, by_j, acc0, acc, proj, zrow, rads, wgts):
     cells, a, f, k = sizes
     lanes, base, wide = a * a, cells * a, cells + 2
+    slots = []
     for p in range(3):
-        proj[p * wide] = project(low_line, p, cells - 1, a, in_t)
-        proj[p * wide + cells + 1] = project(high_line, p, 0, a, in_t)
-        for c in range(cells if p != 1 else 0):
-            proj[p * wide + c + 1] = project(line, p, c, a, in_t)
+        slots += [(p * wide, low_line, p, cells - 1), (p * wide + cells + 1, high_line, p, 0)]
+        slots += [(p * wide + c + 1, line, p, c) for c in range(cells if p != 1 else 0)]
         window(zrow, [spots(l, p, base, by_j) for l in (low_line, line, high_line)], cells)
         for r in range(3):
             there = [zrow[d, r : r + cells, :] for d in range(3)]
             moves = ((1 - p,), (0,), (r - 1,))
             rads[p * 3 + r], wgts[p * 3 + r] = pair_terms(there, own_rows(own, cells), moves, None)
+    project(proj, slots, in_t, a)
+    units = []
     for p in range(3):
         spans = [(c, r) for c in range(cells) for r in range(3)] if p != 1 else [(0, 0), (cells - 1, 2)]
-        units = [unit(rads, wgts, proj, c, p * 3 + r, p * wide + c + r) for c, r in spans]
-        add_pairs(units, cells, lanes, w1, w2, acc, k, f, acc0 if p == 0 else None)
+        units += [unit(rads, wgts, proj, c, p * 3 + r, p * wide + c + r) for c, r in spans]
+    units.sort(key=lambda u: u[0])
+    add_pairs(units, cells, lanes, w1, w2, acc, k, f, acc0)
 
 
 def plane_kernel(sizes, ways, *refs):
@@ -195,43 +206,70 @@
     lines, refs = refs[: len(ways)], refs[len(ways) :]
     own, w1, w2, in_t, by_j, acc1, acc, proj, zrow, rads, wgts = refs
     lanes, base, n_ways = a * a, cells * a, len(ways)
+    slots = []
     for p in range(3):
         for way, moves_y in enumerate(ways):
             at = p * n_ways + way
-            for c in range(cells):
-                proj[at * cells + c] = project(lines[way], p, c, a, in_t)
+            slots += [(at * cells + c, lines[way], p, c) for c in range(cells)]
             window(zrow, [spots(lines[way], p, base, by_j)] * 3, cells)
             for r in range(3):
                 there = [zrow[d, r : r + cells, :] for d in range(3)]
                 moves = ((1 - p,), moves_y, (r - 1,))
                 rads[at * 3 + r], wgts[at * 3 + r] = pair_terms(there, own_rows(own, cells), moves, None)
+    project(proj, slots, in_t, a)
+    units = []
     for at in range(3 * n_ways):
-        units = [unit(rads, wgts, proj, c, at * 3 + r, at * cells + c + r - 1) for c, r in inside(cells)]
-        add_pairs(units, cells, lanes, w1, w2, acc, k, f, acc1 if at == 0 else None)
-
-
-def last_kernel(sizes, ways, *refs):
+        units += [unit(rads, wgts, proj, c, at * 3 + r, at * cells + c + r - 1) for c, r in inside(cells)]
+    units.sort(key=lambda u: u[0])
+    add_pairs(units, cells, lanes, w1, w2, acc, k, f, acc1)
+
+
+def last_kernel(sizes, ways, sides, *refs):
     cells, a, f, k = sizes
-    lows, highs, refs = refs[: len(ways)], refs[len(ways) : 2 * len(ways)], refs[2 * len(ways) :]
+    lows, highs = refs[: len(ways)], refs[(sides - 1) * len(ways) : sides * len(ways)]
+    refs = refs[sides * len(ways) :]
     packed, own, w1, w2, in_t, by_j, pick, dense_w, final_w, biases, filled, acc2 = refs[:12]
-    out_ref, acc, proj, rads, wgts = refs[12:]
+    out_ref, acc, proj, gaps, rads, wgts = refs[12:]
     lanes, base, n_ways = a * a, cells * a, len(ways)
     coords = own_rows(own, cells)
-    units = []
-    for p in range(3):
-        for way, moves_y in enumerate(ways):
-            for high in range(2):
-                block, cell, c, r = (highs[way], 0, cells - 1, 2) if high else (lows[way], cells - 1, 0, 0)
-                at = (p * n_ways + way) * 2 + high
-                proj[at] = project(block, p, cell, a, in_t)
-                table = spots(block, p, base, by_j)
-                there = [table[d * cells + cell : d * cells + cell + 1] for d in range(3)]
-                here = [coords[d][c : c + 1] for d in range(3)]
-                moves = ((1 - p,), moves_y, (r - 1,))
-                rads[at], wgts[at] = pair_terms(there, here, moves, None)
-                units.append((
-                    c, lambda at=at: rads[at], lambda at=at: wgts[at], lambda at=at: proj[at],
-                ))
+    edge = [(p, way, high) for p in range(3) for way in range(n_ways) for high in range(2)]
+    count = len(edge)
+    slots, units = [], []
+    stacked = [jnp.concatenate([block[p, base : base + 16, :] for p in range(3)], axis=0) for block in lows]
+    low_rows = [jnp.dot(rows, by_j[...], preferred_element_type=F32) for rows in stacked]
+    if highs[0] is lows[0]:
+        high_rows = low_rows
+    else:
+        stacked = [jnp.concatenate([block[p, base : base + 16, :] for p in range(3)], axis=0) for block in highs]
+        high_rows = [jnp.dot(rows, by_j[...], preferred_element_type=F32) for rows in stacked]
+    for at, (p, way, high) in enumerate(edge):
+        block, cell, c = (highs[way], 0, cells - 1) if high else (lows[way], cells - 1, 0)
+        slots.append((at, block, p, cell))
+        table = (high_rows if high else low_rows)[way]
+        for d in range(3):
+            row = p * 16 + d * cells + cell
+            gaps[d, at : at + 1, :] = table[row : row + 1] - coords[d][c : c + 1]
+        units.append((
+            c, lambda at=at: rads[at : at + 1, :], lambda at=at: wgts[at : at + 1, :], lambda at=at: proj[at],
+        ))
+    project(proj, slots, in_t, a)
+    index = lax.broadcasted_iota(jnp.int32, (count, lanes), 0)
+
+    def per_row(value):
+        out = jnp.zeros((count, lanes), F32)
+        for at, key in enumerate(edge):
+            if value(*key):
+                out = jnp.where(index == at, float(value(*key)), out)
+        return out
+
+    gap = [gaps[d, 0:count, :] for d in range(3)]
+    gap[0] = gap[0] + per_row(lambda p, way, high: 1 - p)
+    gap[2] = gap[2] + per_row(lambda p, way, high: 2 * high - 1)
+    if n_ways == 1:
+        gap[1] = jnp.minimum(jnp.abs(gap[1] + 1.0), jnp.abs(gap[1] - 1.0))
+    else:
+        gap[1] = gap[1] + per_row(lambda p, way, high: ways[way][0])
+    rads[...], wgts[...] = pair_terms(gap, None, None, None)
     units.sort(key=lambda u: u[0])
     add_pairs(units, cells, lanes, w1, w2, acc, k, f, acc2)
 
@@ -241,7 +279,7 @@
         messages.append(lax.dot_general(pick[...], head, NT, preferred_element_type=F32))
     message = jnp.concatenate(messages, axis=0).astype(BF16)
     inner = jnp.dot(message, dense_w[...], preferred_element_type=F32) + biases[0:1, :]
-    inner = (jax.nn.softplus(inner) - LOG_TWO).astype(BF16)
+    inner = (jnp.maximum(inner, 0.0) + jnp.log(0.5 + 0.5 * jnp.exp(-jnp.abs(inner)))).astype(BF16)
     update = jnp.dot(inner, final_w[...], preferred_element_type=F32) + biases[1:2, :]
     value = (packed[: cells * a, :].astype(F32) + update) * filled[...]
     for c in range(cells):
@@ -372,10 +410,11 @@
     )
     far_z, acc2 = lax.optimization_barrier((far_z, acc2))
     out = call(
-        lambda *refs: last_kernel(sizes, ways, *refs),
+        lambda *refs: last_kernel(sizes, ways, len(z_steps), *refs),
         jax.ShapeDtypeStruct((cells, a, f), BF16),
-        [sums, tiles(6 * n_ways)] + terms(6 * n_ways, 1),
-        tuple(map(on_chip, [z[0] for z in far_z] + [z[-1] for z in far_z] + [packed]))
+        [sums, tiles(6 * n_ways), pltpu.VMEM((3, 8 * n_ways, lanes), F32)]
+        + [pltpu.VMEM((6 * n_ways, lanes), F32)] * 2,
+        tuple(map(on_chip, [z[side] for side in range(len(z_steps)) for z in far_z] + [packed]))
         + shared
         + tuple(map(on_chip, (pick, dense_w, final_w, biases, filled, acc2))),
     )

time: 16.4 us -> 16.1 us (0.982)
  Pallas kernels: 8.21 us -> 7.63 us
  waiting for transfers between devices: 1.04 us -> 1.33 us
    pallas_call x4, Pallas kernels: 7.48 us -> 6.9 us  [call(): pl.pallas_call(kernel, out_shape=out_shape, in_specs=[smem] * len(scalars...]
    ppermute x5, waiting for transfers between devices: 1.04 us -> 1.33 us  [shifted(): return lax.ppermute(value, tuple(axes), pairs)]
  transfers between devices with their start and end apart: 5 -> 5, of which waited for: 2 -> 2; matrix products, arithmetic and copies ran while one was open for 0% -> 0% of each run, Pallas kernels for 36% -> 33%
where the time goes in v5:
time: 16.1 us; the launch traced here: 15.9 us
  Pallas kernels  7.63 us (47%)
  starting transfers between devices  6.84 us (42%)
  waiting for transfers between devices  1.33 us (8%)
    pallas_call x4, Pallas kernels, call(): pl.pallas_call(kernel, out_shape=out_shape, in_specs=[smem] * len(scalars...  6.9 us
    ppermute x5, starting transfers between devices, shifted(): return lax.ppermute(value, tuple(axes), pairs)  6.84 us
    ppermute x5, waiting for transfers between devices, shifted(): return lax.ppermute(value, tuple(axes), pairs)  1.33 us
    pallas_call x1, Pallas kernels, shards(): pl.pallas_call(pack_kernel, out_shape=pltpu.VMEM((cells * a + 16, f), BF1...  0.74 us
  transfers between devices with their start and end apart: 5, of which 2 were waited for; matrix products, arithmetic and copies ran while one was open for 0% of the time, Pallas kernels for 33%

profile of v5, /device:TPU:0, one launch (start us, length us, event | category | flops | bytes accessed | tf_op | source)
XLA Modules:
  0.0 15.9 jit_solution(2930514195964420594)
XLA Ops:
  0.0 0.7 %shard_map.118.refs_1_ = bf16[80,128]{1,0:T(8,128)(2,1)S(1)} custom-call(s32[4]{0:T(128)} %bitcast.18, bf16[4,16,128]{2,1,0:T(8,128)(2,1)} %bitcast.16, bf16[3,4,16]{2,1,0:T(4,128)(2,1)} %bitcast.17), custom_call_target="tpu_custom_call" | custom-call | tf_op jit(solution)/shard_map/pallas_call | solution.py:329
  0.7 3.1 %collective-permute-start.1 = (bf16[80,128]{1,0:T(8,128)(2,1)S(1)}, bf16[80,128]{1,0:T(8,128)(2,1)S(1)}, u32[]{:S(2)}, u32[]{:S(2)}) collective-permute-start(bf16[80,128]{1,0:T(8,128)(2,1)S(1)} %shard_map.118.refs_1_), channel_id=1, source_target_pairs={{0,4},{4,8},{8,12},{12,0},{1,5},{5,9},{9,13},{13,1},{2,6},{6,10},{... | collective-permute-start | bytes 61448 | tf_op jit(solution)/shard_map/ppermute | solution.py:299
  3.8 2.1 %collective-permute-start = (bf16[80,128]{1,0:T(8,128)(2,1)S(1)}, bf16[80,128]{1,0:T(8,128)(2,1)S(1)}, u32[]{:S(2)}, u32[]{:S(2)}) collective-permute-start(bf16[80,128]{1,0:T(8,128)(2,1)S(1)} %shard_map.118.refs_1_), channel_id=1, source_target_pairs={{0,12},{4,0},{8,4},{12,8},{1,13},{5,1},{9,5},{13,9},{2,14},{6,2},{... | collective-permute-start | bytes 61448 | tf_op jit(solution)/shard_map/ppermute | solution.py:299
  5.9 1.8 %shard_map.119 = (f32[4,128,256]{2,1,0:T(8,128)S(1)}, bf16[128,80]{1,0:T(8,128)(2,1)S(1)}, bf16[128,144]{1,0:T(8,128)(2,1)S(1)}, bf16[128,128]{1,0:T(8,128)(2,1)...) custom-call(s32[4]{0:T(128)} %bitcast.19, ...), custom_call_target="tpu_custom_call" | custom-call | flops 1000000000 | bytes 1000000 | tf_op jit(solution)/shard_map/pallas_call | solution.py:342
  7.7 0.0 collective-permute-done.1
  7.7 0.1 collective-permute-done
  7.8 0.1 collective-permute-start.3
  7.9 1.6 %collective-permute-start.2 = (bf16[3,80,128]{2,1,0:T(8,128)(2,1)S(1)}, bf16[3,80,128]{2,1,0:T(8,128)(2,1)S(1)}, u32[]{:S(2)}, u32[]{:S(2)}) collective-permute-start(bf16[3,80,128]{2,1,0:T(8,128)(2,1)S(1)} %pad_maximum_fusion.refs_0_), channel_id=1, source_target_pairs={{0,2},{2,0},{1,3},{3,1},{4,6},{6,4},{5,7},{7,5},{8,10},{10,8},{9,1... | collective-permute-start | bytes 184328 | tf_op jit(solution)/shard_map/ppermute | solution.py:299
  9.5 0.0 collective-permute-done.3.refs_1_.refs_2_
  9.5 1.6 %shard_map.120.refs_6_ = f32[4,128,256]{2,1,0:T(8,128)S(1)} custom-call(bf16[3,80,128]{2,1,0:T(8,128)(2,1)S(1)} %pad_maximum_fusion.refs_0_, bf16[3,80,128]{2,1,0:T(8,128)(2,1)S(1)} %collective-permute-done.3.refs_1_.refs_2_, bf16[3,80,128]{2,1,0:T(8,128)(2,1)S(1)} %collective-permute-done.3.refs_1_.refs_2_, ...), custom_call_target="tpu_custom_call" | custom-call | flops 1000000000 | bytes 1000000 | tf_op jit(solution)/shard_map/pallas_call | solution.py:342
  11.2 1.2 %collective-permute-done.2.refs_0_ = bf16[3,80,128]{2,1,0:T(8,128)(2,1)S(1)} collective-permute-done((bf16[3,80,128]{2,1,0:T(8,128)(2,1)S(1)}, bf16[3,80,128]{2,1,0:T(8,128)(2,1)S(1)}, u32[]{:S(2)}, u32[]{:S(2)}) %collective-permute-start.2) | collective-permute-done | bytes 61472 | tf_op jit(solution)/shard_map/ppermute | solution.py:299
  12.3 0.0 collective-permute-start.4
  12.3 1.8 %shard_map.121.refs_12_ = f32[4,128,256]{2,1,0:T(8,128)S(1)} custom-call(bf16[3,80,128]{2,1,0:T(8,128)(2,1)S(1)} %collective-permute-done.2.refs_0_, f32[16,256]{1,0:T(8,128)S(1)} %get-tuple-element.26.refs_3_.refs_1_.refs_2_, bf16[128,80]{1,0:T(8,128)(2,1)S(1)} %get-tuple-element.27.refs_4_.refs_2_.refs_3_, ...), custom_call_target="tpu_custom_call" | custom-call | flops 1000000000 | bytes 1000000 | tf_op jit(solution)/shard_map/pallas_call | solution.py:342
  14.2 0.0 collective-permute-done.4.refs_0_
  14.2 1.7 %shard_map.122 = bf16[4,16,128]{2,1,0:T(8,128)(2,1)} custom-call(bf16[3,80,128]{2,1,0:T(8,128)(2,1)S(1)} %collective-permute-done.4.refs_0_, bf16[80,128]{1,0:T(8,128)(2,1)S(1)} %shard_map.118.refs_1_, f32[16,256]{1,0:T(8,128)S(1)} %get-tuple-element.26.refs_3_.refs_1_.refs_2_, bf16[128,80]{1,0:T(8,128)(2,1)S(1)} %get-tuple-element.27.refs_4_.refs_2_.refs_3_, ...), custom_call_target="tpu_custom_call" | custom-call | flops 1000000000 | bytes 1000000 | tf_op jit(solution)/shard_map/pallas_call | solution.py:342
  (1 shorter events, 0.0 us)
Async XLA Ops:
  0.7 7.0 %collective-permute-start.1 = (bf16[80,128]{1,0:T(8,128)(2,1)S(1)}, bf16[80,128]{1,0:T(8,128)(2,1)S(1)}, u32[]{:S(2)}, u32[]{:S(2)}) collective-permute-start(bf16[80,128]{1,0:T(8,128)(2,1)S(1)} %shard_map.118.refs_1_), channel_id=1, source_target_pairs={{0,4},{4,8},{8,12},{12,0},{1,5},{5,9},{9,13},{13,1},{2,6},{6,10},{... | collective-permute-start | bytes 61448 | tf_op jit(solution)/shard_map/ppermute | solution.py:299
  3.8 4.0 %collective-permute-start = (bf16[80,128]{1,0:T(8,128)(2,1)S(1)}, bf16[80,128]{1,0:T(8,128)(2,1)S(1)}, u32[]{:S(2)}, u32[]{:S(2)}) collective-permute-start(bf16[80,128]{1,0:T(8,128)(2,1)S(1)} %shard_map.118.refs_1_), channel_id=1, source_target_pairs={{0,12},{4,0},{8,4},{12,8},{1,13},{5,1},{9,5},{13,9},{2,14},{6,2},{... | collective-permute-start | bytes 61448 | tf_op jit(solution)/shard_map/ppermute | solution.py:299
  7.8 1.7 %collective-permute-start.3 = (bf16[3,80,128]{2,1,0:T(8,128)(2,1)S(1)}, bf16[3,80,128]{2,1,0:T(8,128)(2,1)S(1)}, u32[]{:S(2)}, u32[]{:S(2)}) collective-permute-start(bf16[3,80,128]{2,1,0:T(8,128)(2,1)S(1)} %pad_maximum_fusion.refs_0_), channel_id=1, source_target_pairs={{0,1},{1,0},{2,3},{3,2},{4,5},{5,4},{6,7},{7,6},{8,9},{9,8},{10,11... | collective-permute-start | bytes 184328 | tf_op jit(solution)/shard_map/ppermute | solution.py:299
  7.9 4.4 %collective-permute-start.2 = (bf16[3,80,128]{2,1,0:T(8,128)(2,1)S(1)}, bf16[3,80,128]{2,1,0:T(8,128)(2,1)S(1)}, u32[]{:S(2)}, u32[]{:S(2)}) collective-permute-start(bf16[3,80,128]{2,1,0:T(8,128)(2,1)S(1)} %pad_maximum_fusion.refs_0_), channel_id=1, source_target_pairs={{0,2},{2,0},{1,3},{3,1},{4,6},{6,4},{5,7},{7,5},{8,10},{10,8},{9,1... | collective-permute-start | bytes 184328 | tf_op jit(solution)/shard_map/ppermute | solution.py:299
  12.3 1.8 %collective-permute-start.4 = (bf16[3,80,128]{2,1,0:T(8,128)(2,1)S(1)}, bf16[3,80,128]{2,1,0:T(8,128)(2,1)S(1)}, u32[]{:S(2)}, u32[]{:S(2)}) collective-permute-start(bf16[3,80,128]{2,1,0:T(8,128)(2,1)S(1)} %collective-permute-done.2.refs_0_), channel_id=1, source_target_pairs={{0,1},{1,0},{2,3},{3,2},{4,5},{5,4},{6,7},{7,6},{8,9},{9,8},{10,11... | collective-permute-start | bytes 184328 | tf_op jit(solution)/shard_map/ppermute | solution.py:299

commit v6 on v5

--- a/solution.py
+++ b/solution.py
@@ -15,6 +15,8 @@
 GAP_SCALE = math.sqrt(BASIS_GAMMA * LOG2_E)
 FAR = 8.0
 PAD_K = 64
+SLOTS = 16
+SPOT_ROWS = 8
 EXTRA = 16
 
 COS_SERIES = [(-1.0) ** m * (math.pi / 2) ** (2 * m) / math.factorial(2 * m) for m in range(9)]
@@ -38,19 +40,27 @@
         out_ref[c * a : (c + 1) * a, :] = atoms_ref[c]
     cell = lax.broadcasted_iota(jnp.int32, (cells, a), 0)
     slot = lax.broadcasted_iota(jnp.int32, (cells, a), 1)
-    filled = jnp.zeros((cells, a), jnp.int32)
-    for c in range(cells):
+    filled = jnp.full((cells, a), counts_ref[0], jnp.int32)
+    for c in range(1, cells):
         filled = jnp.where(cell == c, counts_ref[c], filled)
     out_ref[cells * a :, :] = jnp.zeros((out_ref.shape[0] - cells * a, f), BF16)
     spots = [jnp.where(slot < filled, places_ref[d].astype(F32), FAR) for d in range(3)]
     table = jnp.concatenate(spots, axis=0)
-    out_ref[cells * a : cells * a + 3 * cells, :a] = table.astype(BF16)
-
-
-def spread(a, lanes, rows, by_j):
-    row = lax.broadcasted_iota(jnp.int32, (rows, lanes), 0)
-    lane = lax.broadcasted_iota(jnp.int32, (1, lanes), 1)
-    return (row == (lane % a if by_j else lane // a)).astype(F32).astype(BF16)
+    for n in range(0, 3 * cells, SPOT_ROWS):
+        rows, at = table[n : n + SPOT_ROWS], n // SPOT_ROWS * a
+        out_ref[cells * a : cells * a + rows.shape[0], at : at + a] = rows.astype(BF16)
+
+
+def spread(a, lanes, rows, by_j, groups=1):
+    row = lax.broadcasted_iota(jnp.int32, (rows, groups * lanes), 0)
+    lane = lax.broadcasted_iota(jnp.int32, (1, groups * lanes), 1)
+    inner = lane % lanes
+    slot = (inner % a if by_j else inner // a) + lane // lanes * a
+    return (row == slot).astype(F32).astype(BF16)
+
+
+def spot_groups(cells):
+    return -(-3 * cells // SPOT_ROWS)
 
 
 def project(proj, slots, in_t, a):
@@ -67,7 +77,9 @@
 
 
 def spots(block, p, base, by_j):
-    return jnp.dot(block[p, base : base + 16, :], by_j[...], preferred_element_type=F32)
+    table = jnp.dot(block[p, base : base + SPOT_ROWS, :], by_j[...], preferred_element_type=F32)
+    lanes = by_j.shape[1] // spot_groups(base // SLOTS)
+    return jnp.concatenate([table[:, n : n + lanes] for n in range(0, table.shape[1], lanes)], axis=0)
 
 
 def pair_terms(there, own, moves, drop):
@@ -162,10 +174,10 @@
     slot = lax.broadcasted_iota(jnp.int32, (a, f), 0)
     for c in range(cells):
         filled[c * a : (c + 1) * a, :] = (slot < counts_ref[c]).astype(F32)
-    by_j[...] = spread(a, lanes, f, True)
+    by_j[...] = spread(a, lanes, f, True, spot_groups(cells))
     pick[...] = spread(a, lanes, a, False)
     line = packed.reshape(1, *packed.shape)
-    own[...] = spots(line, 0, base, spread(a, lanes, f, False))
+    own[...] = spots(line, 0, base, spread(a, lanes, f, False, spot_groups(cells)))
     table = spots(line, 0, base, by_j)
     window(zrow, (table, table, table), cells)
     small = lax.broadcasted_iota(jnp.int32, (1, lanes), 1)
@@ -235,19 +247,16 @@
     edge = [(p, way, high) for p in range(3) for way in range(n_ways) for high in range(2)]
     count = len(edge)
     slots, units = [], []
-    stacked = [jnp.concatenate([block[p, base : base + 16, :] for p in range(3)], axis=0) for block in lows]
-    low_rows = [jnp.dot(rows, by_j[...], preferred_element_type=F32) for rows in stacked]
-    if highs[0] is lows[0]:
-        high_rows = low_rows
-    else:
-        stacked = [jnp.concatenate([block[p, base : base + 16, :] for p in range(3)], axis=0) for block in highs]
-        high_rows = [jnp.dot(rows, by_j[...], preferred_element_type=F32) for rows in stacked]
+    low_rows = [[spots(block, p, base, by_j) for p in range(3)] for block in lows]
+    high_rows = low_rows
+    if highs[0] is not lows[0]:
+        high_rows = [[spots(block, p, base, by_j) for p in range(3)] for block in highs]
     for at, (p, way, high) in enumerate(edge):
         block, cell, c = (highs[way], 0, cells - 1) if high else (lows[way], cells - 1, 0)
         slots.append((at, block, p, cell))
-        table = (high_rows if high else low_rows)[way]
+        table = (high_rows if high else low_rows)[way][p]
         for d in range(3):
-            row = p * 16 + d * cells + cell
+            row = d * cells + cell
             gaps[d, at : at + 1, :] = table[row : row + 1] - coords[d][c : c + 1]
         units.append((
             c, lambda at=at: rads[at : at + 1, :], lambda at=at: wgts[at : at + 1, :], lambda at=at: proj[at],
@@ -318,7 +327,7 @@
     final_bias,
 ):
     cells_x, cells_y, cells_z, a, f = atoms.shape
-    assert cells_x == 1 and cells_y == 1
+    assert cells_x == 1 and cells_y == 1 and a == SLOTS
     cells = cells_z
     k = basis_weight.shape[0]
     lanes = a * a
@@ -328,7 +337,7 @@
     counts = counts.reshape(cells)
     packed = pl.pallas_call(
         pack_kernel,
-        out_shape=pltpu.VMEM((cells * a + 16, f), BF16),
+        out_shape=pltpu.VMEM((cells * a + SPOT_ROWS, f), BF16),
         in_specs=[smem, vmem, vmem],
         out_specs=vmem,
     )(counts, atoms.reshape(cells, a, f), jnp.swapaxes(places, 2, 3).reshape(3, cells, a))
@@ -364,7 +373,7 @@
             pltpu.VMEM((f, f), BF16),
             pltpu.VMEM((f, f), BF16),
             pltpu.VMEM((2, f), F32),
-            pltpu.VMEM((f, lanes), BF16),
+            pltpu.VMEM((f, spot_groups(cells) * lanes), BF16),
             pltpu.VMEM((a, lanes), BF16),
             pltpu.VMEM((16, lanes), F32),
             pltpu.VMEM((cells * a, f), F32),

time: 16.1 us -> 15.9 us (0.988)
  waiting for transfers between devices: 1.33 us -> 1 us
    ppermute x5, waiting for transfers between devices: 1.33 us -> 1 us  [shifted(): return lax.ppermute(value, tuple(axes), pairs)]
  transfers between devices with their start and end apart: 5 -> 5, of which waited for: 2 -> 2; matrix products, arithmetic and copies ran while one was open for 0% -> 0% of each run, Pallas kernels for 33% -> 34%
where the time goes in v6:
time: 15.9 us; the launch traced here: 15.7 us
  Pallas kernels  7.78 us (49%)
  starting transfers between devices  6.83 us (43%)
  waiting for transfers between devices  1 us (6%)
    pallas_call x4, Pallas kernels, call(): pl.pallas_call(kernel, out_shape=out_shape, in_specs=[smem] * len(scalars...  6.97 us
    ppermute x5, starting transfers between devices, shifted(): return lax.ppermute(value, tuple(axes), pairs)  6.83 us
    ppermute x5, waiting for transfers between devices, shifted(): return lax.ppermute(value, tuple(axes), pairs)  1 us
    pallas_call x1, Pallas kernels, shards(): pl.pallas_call(pack_kernel, out_shape=pltpu.VMEM((cells * a + SPOT_ROWS,...  0.8 us
  transfers between devices with their start and end apart: 5, of which 2 were waited for; matrix products, arithmetic and copies ran while one was open for 0% of the time, Pallas kernels for 34%

profile of v6, /device:TPU:0, one launch (start us, length us, event | category | flops | bytes accessed | tf_op | source)
XLA Modules:
  0.0 15.7 jit_solution(3175858304673581049)
XLA Ops:
  0.0 0.8 %shard_map.118.refs_1_ = bf16[72,128]{1,0:T(8,128)(2,1)S(1)} custom-call(s32[4]{0:T(128)} %bitcast.18, bf16[4,16,128]{2,1,0:T(8,128)(2,1)} %bitcast.16, bf16[3,4,16]{2,1,0:T(4,128)(2,1)} %bitcast.17), custom_call_target="tpu_custom_call" | custom-call | tf_op jit(solution)/shard_map/pallas_call | solution.py:338
  0.8 3.0 %collective-permute-start.1 = (bf16[72,128]{1,0:T(8,128)(2,1)S(1)}, bf16[72,128]{1,0:T(8,128)(2,1)S(1)}, u32[]{:S(2)}, u32[]{:S(2)}) collective-permute-start(bf16[72,128]{1,0:T(8,128)(2,1)S(1)} %shard_map.118.refs_1_), channel_id=1, source_target_pairs={{0,4},{4,8},{8,12},{12,0},{1,5},{5,9},{9,13},{13,1},{2,6},{6,10},{... | collective-permute-start | bytes 55304 | tf_op jit(solution)/shard_map/ppermute | solution.py:308
  3.8 2.1 %collective-permute-start = (bf16[72,128]{1,0:T(8,128)(2,1)S(1)}, bf16[72,128]{1,0:T(8,128)(2,1)S(1)}, u32[]{:S(2)}, u32[]{:S(2)}) collective-permute-start(bf16[72,128]{1,0:T(8,128)(2,1)S(1)} %shard_map.118.refs_1_), channel_id=1, source_target_pairs={{0,12},{4,0},{8,4},{12,8},{1,13},{5,1},{9,5},{13,9},{2,14},{6,2},{... | collective-permute-start | bytes 55304 | tf_op jit(solution)/shard_map/ppermute | solution.py:308
  5.9 1.8 %shard_map.119 = (f32[4,128,256]{2,1,0:T(8,128)S(1)}, bf16[128,80]{1,0:T(8,128)(2,1)S(1)}, bf16[128,144]{1,0:T(8,128)(2,1)S(1)}, bf16[128,128]{1,0:T(8,128)(2,1)...) custom-call(s32[4]{0:T(128)} %bitcast.19, ...), custom_call_target="tpu_custom_call" | custom-call | flops 1000000000 | bytes 1000000 | tf_op jit(solution)/shard_map/pallas_call | solution.py:351
  7.7 0.0 collective-permute-done.1
  7.7 0.1 collective-permute-done
  7.8 0.0 collective-permute-start.3
  7.8 1.7 %collective-permute-start.2 = (bf16[3,72,128]{2,1,0:T(8,128)(2,1)S(1)}, bf16[3,72,128]{2,1,0:T(8,128)(2,1)S(1)}, u32[]{:S(2)}, u32[]{:S(2)}) collective-permute-start(bf16[3,72,128]{2,1,0:T(8,128)(2,1)S(1)} %pad_maximum_fusion.refs_0_), channel_id=1, source_target_pairs={{0,2},{2,0},{1,3},{3,1},{4,6},{6,4},{5,7},{7,5},{8,10},{10,8},{9,1... | collective-permute-start | bytes 165896 | tf_op jit(solution)/shard_map/ppermute | solution.py:308
  9.5 0.0 collective-permute-done.3.refs_1_.refs_2_
  9.5 1.7 %shard_map.120.refs_6_ = f32[4,128,256]{2,1,0:T(8,128)S(1)} custom-call(bf16[3,72,128]{2,1,0:T(8,128)(2,1)S(1)} %pad_maximum_fusion.refs_0_, bf16[3,72,128]{2,1,0:T(8,128)(2,1)S(1)} %collective-permute-done.3.refs_1_.refs_2_, bf16[3,72,128]{2,1,0:T(8,128)(2,1)S(1)} %collective-permute-done.3.refs_1_.refs_2_, ...), custom_call_target="tpu_custom_call" | custom-call | flops 1000000000 | bytes 1000000 | tf_op jit(solution)/shard_map/pallas_call | solution.py:351
  11.2 0.9 %collective-permute-done.2.refs_0_ = bf16[3,72,128]{2,1,0:T(8,128)(2,1)S(1)} collective-permute-done((bf16[3,72,128]{2,1,0:T(8,128)(2,1)S(1)}, bf16[3,72,128]{2,1,0:T(8,128)(2,1)S(1)}, u32[]{:S(2)}, u32[]{:S(2)}) %collective-permute-start.2) | collective-permute-done | bytes 55328 | tf_op jit(solution)/shard_map/ppermute | solution.py:308
  12.1 0.0 collective-permute-start.4
  12.1 1.8 %shard_map.121.refs_12_ = f32[4,128,256]{2,1,0:T(8,128)S(1)} custom-call(bf16[3,72,128]{2,1,0:T(8,128)(2,1)S(1)} %collective-permute-done.2.refs_0_, f32[16,256]{1,0:T(8,128)S(1)} %get-tuple-element.26.refs_3_.refs_1_.refs_2_, bf16[128,80]{1,0:T(8,128)(2,1)S(1)} %get-tuple-element.27.refs_4_.refs_2_.refs_3_, ...), custom_call_target="tpu_custom_call" | custom-call | flops 1000000000 | bytes 1000000 | tf_op jit(solution)/shard_map/pallas_call | solution.py:351
  14.0 0.0 collective-permute-done.4.refs_0_
  14.0 1.7 %shard_map.122 = bf16[4,16,128]{2,1,0:T(8,128)(2,1)} custom-call(bf16[3,72,128]{2,1,0:T(8,128)(2,1)S(1)} %collective-permute-done.4.refs_0_, bf16[72,128]{1,0:T(8,128)(2,1)S(1)} %shard_map.118.refs_1_, f32[16,256]{1,0:T(8,128)S(1)} %get-tuple-element.26.refs_3_.refs_1_.refs_2_, bf16[128,80]{1,0:T(8,128)(2,1)S(1)} %get-tuple-element.27.refs_4_.refs_2_.refs_3_, ...), custom_call_target="tpu_custom_call" | custom-call | flops 1000000000 | bytes 1000000 | tf_op jit(solution)/shard_map/pallas_call | solution.py:351
  (1 shorter events, 0.0 us)
Async XLA Ops:
  0.8 6.9 %collective-permute-start.1 = (bf16[72,128]{1,0:T(8,128)(2,1)S(1)}, bf16[72,128]{1,0:T(8,128)(2,1)S(1)}, u32[]{:S(2)}, u32[]{:S(2)}) collective-permute-start(bf16[72,128]{1,0:T(8,128)(2,1)S(1)} %shard_map.118.refs_1_), channel_id=1, source_target_pairs={{0,4},{4,8},{8,12},{12,0},{1,5},{5,9},{9,13},{13,1},{2,6},{6,10},{... | collective-permute-start | bytes 55304 | tf_op jit(solution)/shard_map/ppermute | solution.py:308
  3.8 4.0 %collective-permute-start = (bf16[72,128]{1,0:T(8,128)(2,1)S(1)}, bf16[72,128]{1,0:T(8,128)(2,1)S(1)}, u32[]{:S(2)}, u32[]{:S(2)}) collective-permute-start(bf16[72,128]{1,0:T(8,128)(2,1)S(1)} %shard_map.118.refs_1_), channel_id=1, source_target_pairs={{0,12},{4,0},{8,4},{12,8},{1,13},{5,1},{9,5},{13,9},{2,14},{6,2},{... | collective-permute-start | bytes 55304 | tf_op jit(solution)/shard_map/ppermute | solution.py:308
  7.8 1.7 %collective-permute-start.3 = (bf16[3,72,128]{2,1,0:T(8,128)(2,1)S(1)}, bf16[3,72,128]{2,1,0:T(8,128)(2,1)S(1)}, u32[]{:S(2)}, u32[]{:S(2)}) collective-permute-start(bf16[3,72,128]{2,1,0:T(8,128)(2,1)S(1)} %pad_maximum_fusion.refs_0_), channel_id=1, source_target_pairs={{0,1},{1,0},{2,3},{3,2},{4,5},{5,4},{6,7},{7,6},{8,9},{9,8},{10,11... | collective-permute-start | bytes 165896 | tf_op jit(solution)/shard_map/ppermute | solution.py:308
  7.8 4.3 %collective-permute-start.2 = (bf16[3,72,128]{2,1,0:T(8,128)(2,1)S(1)}, bf16[3,72,128]{2,1,0:T(8,128)(2,1)S(1)}, u32[]{:S(2)}, u32[]{:S(2)}) collective-permute-start(bf16[3,72,128]{2,1,0:T(8,128)(2,1)S(1)} %pad_maximum_fusion.refs_0_), channel_id=1, source_target_pairs={{0,2},{2,0},{1,3},{3,1},{4,6},{6,4},{5,7},{7,5},{8,10},{10,8},{9,1... | collective-permute-start | bytes 165896 | tf_op jit(solution)/shard_map/ppermute | solution.py:308
  12.1 1.8 %collective-permute-start.4 = (bf16[3,72,128]{2,1,0:T(8,128)(2,1)S(1)}, bf16[3,72,128]{2,1,0:T(8,128)(2,1)S(1)}, u32[]{:S(2)}, u32[]{:S(2)}) collective-permute-start(bf16[3,72,128]{2,1,0:T(8,128)(2,1)S(1)} %collective-permute-done.2.refs_0_), channel_id=1, source_target_pairs={{0,1},{1,0},{2,3},{3,2},{4,5},{5,4},{6,7},{7,6},{8,9},{9,8},{10,11... | collective-permute-start | bytes 165896 | tf_op jit(solution)/shard_map/ppermute | solution.py:308

commit v7 on v6

--- a/solution.py
+++ b/solution.py
@@ -14,7 +14,7 @@
 CELL_EDGE = 5.0
 GAP_SCALE = math.sqrt(BASIS_GAMMA * LOG2_E)
 FAR = 8.0
-PAD_K = 64
+PAD_K = 56
 SLOTS = 16
 SPOT_ROWS = 8
 EXTRA = 16
@@ -34,21 +34,32 @@
     return out
 
 
-def pack_kernel(counts_ref, atoms_ref, places_ref, out_ref):
-    cells, a, f = atoms_ref.shape
-    for c in range(cells):
-        out_ref[c * a : (c + 1) * a, :] = atoms_ref[c]
+def pack_kernel(counts_hbm, atoms_hbm, places_hbm, out_ref, counts_ref, places_ref, done):
+    _, cells, a = places_ref.shape
+    top = cells * a
+    copies = [
+        pltpu.make_async_copy(counts_hbm, counts_ref, done.at[0]),
+        pltpu.make_async_copy(places_hbm, places_ref, done.at[1]),
+        pltpu.make_async_copy(atoms_hbm, out_ref.at[0:top, :], done.at[2]),
+    ]
+    for copy in copies:
+        copy.start()
     cell = lax.broadcasted_iota(jnp.int32, (cells, a), 0)
     slot = lax.broadcasted_iota(jnp.int32, (cells, a), 1)
+    copies[0].wait()
     filled = jnp.full((cells, a), counts_ref[0], jnp.int32)
     for c in range(1, cells):
         filled = jnp.where(cell == c, counts_ref[c], filled)
-    out_ref[cells * a :, :] = jnp.zeros((out_ref.shape[0] - cells * a, f), BF16)
+    copies[1].wait()
     spots = [jnp.where(slot < filled, places_ref[d].astype(F32), FAR) for d in range(3)]
     table = jnp.concatenate(spots, axis=0)
-    for n in range(0, 3 * cells, SPOT_ROWS):
-        rows, at = table[n : n + SPOT_ROWS], n // SPOT_ROWS * a
-        out_ref[cells * a : cells * a + rows.shape[0], at : at + a] = rows.astype(BF16)
+    groups = [table[n : n + SPOT_ROWS] for n in range(0, 3 * cells, SPOT_ROWS)]
+    short = SPOT_ROWS - groups[-1].shape[0]
+    if short:
+        groups[-1] = jnp.concatenate([groups[-1], jnp.zeros((short, a), F32)], axis=0)
+    groups.append(jnp.zeros((SPOT_ROWS, out_ref.shape[1] - a * len(groups)), F32))
+    out_ref[top:, :] = jnp.concatenate(groups, axis=1).astype(BF16)
+    copies[2].wait()
 
 
 def spread(a, lanes, rows, by_j, groups=1):
@@ -108,27 +119,22 @@
     centers = lax.broadcasted_iota(jnp.int32, (PAD_K, 128), 0).astype(F32)
     centers = centers * (GAP_SCALE * CELL_EDGE / (k - 1))
     centers = jnp.concatenate([centers] * reps, axis=1)
-    ones = jnp.ones((EXTRA, lanes), BF16)
+    ones = jnp.ones((8, lanes), F32)
     total, opened = None, set()
-    first, second = {}, {}
-    for n in range(len(units) + 2):
-        if n < len(units):
-            gap = units[n][1]() - centers
-            grid = jnp.exp2(gap * -gap).astype(BF16)
-            first[n] = jnp.dot(w1[...], jnp.concatenate([grid, ones], axis=0), preferred_element_type=F32)
-        if 0 <= n - 1 < len(units):
-            hidden = jnp.log2(jnp.exp2(first.pop(n - 1)) + 0.5).astype(BF16)
-            weight = jnp.broadcast_to(units[n - 1][2](), (EXTRA, lanes)).astype(BF16)
-            hidden = (hidden.reshape(f // EXTRA, EXTRA, lanes) * weight[None]).reshape(f, lanes)
-            second[n - 1] = jnp.dot(w2[...], jnp.concatenate([hidden, weight], axis=0), preferred_element_type=F32)
-        if 0 <= n - 2 < len(units):
-            c = units[n - 2][0]
-            term = second.pop(n - 2) * jnp.concatenate([units[n - 2][3]()] * reps, axis=1)
-            total = term if total is None else total + term
-            if n - 1 == len(units) or units[n - 1][0] != c:
-                acc[c] = total + (acc if start is None or c in opened else start)[c]
-                total = None
-                opened.add(c)
+    for n, (c, radius, weight, tile) in enumerate(units):
+        gap = radius() - centers
+        grid = jnp.concatenate([jnp.exp2(gap * -gap), ones], axis=0).astype(BF16)
+        hidden = jnp.dot(w1[...], grid, preferred_element_type=F32)
+        hidden = jnp.log2(jnp.exp2(hidden) + 0.5).astype(BF16)
+        scale = jnp.broadcast_to(weight(), (EXTRA, lanes)).astype(BF16)
+        hidden = (hidden.reshape(f // EXTRA, EXTRA, lanes) * scale[None]).reshape(f, lanes)
+        filt = jnp.dot(w2[...], jnp.concatenate([hidden, scale], axis=0), preferred_element_type=F32)
+        term = filt * jnp.concatenate([tile()] * reps, axis=1)
+        total = term if total is None else total + term
+        if n + 1 == len(units) or units[n + 1][0] != c:
+            acc[c] = total + (acc if start is None or c in opened else start)[c]
+            total = None
+            opened.add(c)
 
 
 def unit(rads, wgts, proj, c, at, cell):
@@ -338,9 +344,14 @@
     packed = pl.pallas_call(
         pack_kernel,
         out_shape=pltpu.VMEM((cells * a + SPOT_ROWS, f), BF16),
-        in_specs=[smem, vmem, vmem],
+        in_specs=[pl.BlockSpec(memory_space=pl.ANY)] * 3,
         out_specs=vmem,
-    )(counts, atoms.reshape(cells, a, f), jnp.swapaxes(places, 2, 3).reshape(3, cells, a))
+        scratch_shapes=[
+            pltpu.SMEM((cells,), jnp.int32),
+            pltpu.VMEM((3, cells, a), BF16),
+            pltpu.SemaphoreType.DMA((3,)),
+        ],
+    )(counts, atoms.reshape(cells * a, f), jnp.swapaxes(places, 2, 3).reshape(3, cells, a))
     above = shifted(packed, [("gx", -1)])
     below = shifted(packed, [("gx", 1)])
     sums = pltpu.VMEM((cells, f, lanes), F32)
@@ -367,7 +378,7 @@
         lambda *refs: first_kernel(sizes, *refs),
         [
             sums,
-            pltpu.VMEM((f, PAD_K + EXTRA), BF16),
+            pltpu.VMEM((f, PAD_K + 8), BF16),
             pltpu.VMEM((f, f + EXTRA), BF16),
             pltpu.VMEM((f, f), BF16),
             pltpu.VMEM((f, f), BF16),

time: 15.9 us -> 16 us (level)
  transfers between devices with their start and end apart: 5 -> 5, of which waited for: 2 -> 2; matrix products, arithmetic and copies ran while one was open for 0% -> 0% of each run, Pallas kernels for 34% -> 33%
where the time goes in v7:
time: 16 us; the launch traced here: 15.7 us
  Pallas kernels  7.68 us (48%)
  starting transfers between devices  6.92 us (43%)
  waiting for transfers between devices  1.04 us (6%)
    ppermute x5, starting transfers between devices, shifted(): return lax.ppermute(value, tuple(axes), pairs)  6.92 us
    pallas_call x4, Pallas kernels, call(): pl.pallas_call(kernel, out_shape=out_shape, in_specs=[smem] * len(scalars...  6.89 us
    ppermute x5, waiting for transfers between devices, shifted(): return lax.ppermute(value, tuple(axes), pairs)  1.04 us
    pallas_call x1, Pallas kernels, shards(): pl.pallas_call(pack_kernel, out_shape=pltpu.VMEM((cells * a + SPOT_ROWS,...  0.79 us
  transfers between devices with their start and end apart: 5, of which 2 were waited for; matrix products, arithmetic and copies ran while one was open for 0% of the time, Pallas kernels for 33%

profile of v7, /device:TPU:0, one launch (start us, length us, event | category | flops | bytes accessed | tf_op | source)
XLA Modules:
  0.0 15.7 jit_solution(2377237589523651430)
XLA Ops:
  0.0 0.8 %shard_map.118.refs_1_ = bf16[72,128]{1,0:T(8,128)(2,1)S(1)} custom-call(s32[4]{0:T(128)} %bitcast.18, bf16[64,128]{1,0:T(8,128)(2,1)} %bitcast.16, bf16[3,4,16]{2,1,0:T(4,128)(2,1)} %bitcast.17), custom_call_target="tpu_custom_call" | custom-call | tf_op jit(solution)/shard_map/pallas_call | solution.py:344
  0.8 3.1 %collective-permute-start.1 = (bf16[72,128]{1,0:T(8,128)(2,1)S(1)}, bf16[72,128]{1,0:T(8,128)(2,1)S(1)}, u32[]{:S(2)}, u32[]{:S(2)}) collective-permute-start(bf16[72,128]{1,0:T(8,128)(2,1)S(1)} %shard_map.118.refs_1_), channel_id=1, source_target_pairs={{0,4},{4,8},{8,12},{12,0},{1,5},{5,9},{9,13},{13,1},{2,6},{6,10},{... | collective-permute-start | bytes 55304 | tf_op jit(solution)/shard_map/ppermute | solution.py:314
  3.9 2.1 %collective-permute-start = (bf16[72,128]{1,0:T(8,128)(2,1)S(1)}, bf16[72,128]{1,0:T(8,128)(2,1)S(1)}, u32[]{:S(2)}, u32[]{:S(2)}) collective-permute-start(bf16[72,128]{1,0:T(8,128)(2,1)S(1)} %shard_map.118.refs_1_), channel_id=1, source_target_pairs={{0,12},{4,0},{8,4},{12,8},{1,13},{5,1},{9,5},{13,9},{2,14},{6,2},{... | collective-permute-start | bytes 55304 | tf_op jit(solution)/shard_map/ppermute | solution.py:314
  6.0 1.8 %shard_map.119 = (f32[4,128,256]{2,1,0:T(8,128)S(1)}, bf16[128,64]{1,0:T(8,128)(2,1)S(1)}, bf16[128,144]{1,0:T(8,128)(2,1)S(1)}, bf16[128,128]{1,0:T(8,128)(2,1)...) custom-call(s32[4]{0:T(128)} %bitcast.19, ...), custom_call_target="tpu_custom_call" | custom-call | flops 1000000000 | bytes 1000000 | tf_op jit(solution)/shard_map/pallas_call | solution.py:362
  7.8 0.0 collective-permute-done.1
  7.8 0.1 collective-permute-done
  7.8 0.0 collective-permute-start.3
  7.9 1.7 %collective-permute-start.2 = (bf16[3,72,128]{2,1,0:T(8,128)(2,1)S(1)}, bf16[3,72,128]{2,1,0:T(8,128)(2,1)S(1)}, u32[]{:S(2)}, u32[]{:S(2)}) collective-permute-start(bf16[3,72,128]{2,1,0:T(8,128)(2,1)S(1)} %pad_maximum_fusion.refs_0_), channel_id=1, source_target_pairs={{0,2},{2,0},{1,3},{3,1},{4,6},{6,4},{5,7},{7,5},{8,10},{10,8},{9,1... | collective-permute-start | bytes 165896 | tf_op jit(solution)/shard_map/ppermute | solution.py:314
  9.6 0.0 collective-permute-done.3.refs_1_.refs_2_
  9.6 1.6 %shard_map.120.refs_6_ = f32[4,128,256]{2,1,0:T(8,128)S(1)} custom-call(bf16[3,72,128]{2,1,0:T(8,128)(2,1)S(1)} %pad_maximum_fusion.refs_0_, bf16[3,72,128]{2,1,0:T(8,128)(2,1)S(1)} %collective-permute-done.3.refs_1_.refs_2_, bf16[3,72,128]{2,1,0:T(8,128)(2,1)S(1)} %collective-permute-done.3.refs_1_.refs_2_, ...), custom_call_target="tpu_custom_call" | custom-call | flops 1000000000 | bytes 1000000 | tf_op jit(solution)/shard_map/pallas_call | solution.py:362
  11.2 1.0 %collective-permute-done.2.refs_0_ = bf16[3,72,128]{2,1,0:T(8,128)(2,1)S(1)} collective-permute-done((bf16[3,72,128]{2,1,0:T(8,128)(2,1)S(1)}, bf16[3,72,128]{2,1,0:T(8,128)(2,1)S(1)}, u32[]{:S(2)}, u32[]{:S(2)}) %collective-permute-start.2) | collective-permute-done | bytes 55328 | tf_op jit(solution)/shard_map/ppermute | solution.py:314
  12.2 0.0 collective-permute-start.4
  12.2 1.8 %shard_map.121.refs_12_ = f32[4,128,256]{2,1,0:T(8,128)S(1)} custom-call(bf16[3,72,128]{2,1,0:T(8,128)(2,1)S(1)} %collective-permute-done.2.refs_0_, f32[16,256]{1,0:T(8,128)S(1)} %get-tuple-element.26.refs_3_.refs_1_.refs_2_, bf16[128,64]{1,0:T(8,128)(2,1)S(1)} %get-tuple-element.27.refs_4_.refs_2_.refs_3_, ...), custom_call_target="tpu_custom_call" | custom-call | flops 1000000000 | bytes 1000000 | tf_op jit(solution)/shard_map/pallas_call | solution.py:362
  13.9 0.0 collective-permute-done.4.refs_0_
  14.0 1.7 %shard_map.122 = bf16[4,16,128]{2,1,0:T(8,128)(2,1)} custom-call(bf16[3,72,128]{2,1,0:T(8,128)(2,1)S(1)} %collective-permute-done.4.refs_0_, bf16[72,128]{1,0:T(8,128)(2,1)S(1)} %shard_map.118.refs_1_, f32[16,256]{1,0:T(8,128)S(1)} %get-tuple-element.26.refs_3_.refs_1_.refs_2_, bf16[128,64]{1,0:T(8,128)(2,1)S(1)} %get-tuple-element.27.refs_4_.refs_2_.refs_3_, ...), custom_call_target="tpu_custom_call" | custom-call | flops 1000000000 | bytes 1000000 | tf_op jit(solution)/shard_map/pallas_call | solution.py:362
  (1 shorter events, 0.0 us)
Async XLA Ops:
  0.8 7.0 %collective-permute-start.1 = (bf16[72,128]{1,0:T(8,128)(2,1)S(1)}, bf16[72,128]{1,0:T(8,128)(2,1)S(1)}, u32[]{:S(2)}, u32[]{:S(2)}) collective-permute-start(bf16[72,128]{1,0:T(8,128)(2,1)S(1)} %shard_map.118.refs_1_), channel_id=1, source_target_pairs={{0,4},{4,8},{8,12},{12,0},{1,5},{5,9},{9,13},{13,1},{2,6},{6,10},{... | collective-permute-start | bytes 55304 | tf_op jit(solution)/shard_map/ppermute | solution.py:314
  3.9 4.0 %collective-permute-start = (bf16[72,128]{1,0:T(8,128)(2,1)S(1)}, bf16[72,128]{1,0:T(8,128)(2,1)S(1)}, u32[]{:S(2)}, u32[]{:S(2)}) collective-permute-start(bf16[72,128]{1,0:T(8,128)(2,1)S(1)} %shard_map.118.refs_1_), channel_id=1, source_target_pairs={{0,12},{4,0},{8,4},{12,8},{1,13},{5,1},{9,5},{13,9},{2,14},{6,2},{... | collective-permute-start | bytes 55304 | tf_op jit(solution)/shard_map/ppermute | solution.py:314
  7.8 1.8 %collective-permute-start.3 = (bf16[3,72,128]{2,1,0:T(8,128)(2,1)S(1)}, bf16[3,72,128]{2,1,0:T(8,128)(2,1)S(1)}, u32[]{:S(2)}, u32[]{:S(2)}) collective-permute-start(bf16[3,72,128]{2,1,0:T(8,128)(2,1)S(1)} %pad_maximum_fusion.refs_0_), channel_id=1, source_target_pairs={{0,1},{1,0},{2,3},{3,2},{4,5},{5,4},{6,7},{7,6},{8,9},{9,8},{10,11... | collective-permute-start | bytes 165896 | tf_op jit(solution)/shard_map/ppermute | solution.py:314
  7.9 4.3 %collective-permute-start.2 = (bf16[3,72,128]{2,1,0:T(8,128)(2,1)S(1)}, bf16[3,72,128]{2,1,0:T(8,128)(2,1)S(1)}, u32[]{:S(2)}, u32[]{:S(2)}) collective-permute-start(bf16[3,72,128]{2,1,0:T(8,128)(2,1)S(1)} %pad_maximum_fusion.refs_0_), channel_id=1, source_target_pairs={{0,2},{2,0},{1,3},{3,1},{4,6},{6,4},{5,7},{7,5},{8,10},{10,8},{9,1... | collective-permute-start | bytes 165896 | tf_op jit(solution)/shard_map/ppermute | solution.py:314
  12.2 1.8 %collective-permute-start.4 = (bf16[3,72,128]{2,1,0:T(8,128)(2,1)S(1)}, bf16[3,72,128]{2,1,0:T(8,128)(2,1)S(1)}, u32[]{:S(2)}, u32[]{:S(2)}) collective-permute-start(bf16[3,72,128]{2,1,0:T(8,128)(2,1)S(1)} %collective-permute-done.2.refs_0_), channel_id=1, source_target_pairs={{0,1},{1,0},{2,3},{3,2},{4,5},{5,4},{6,7},{7,6},{8,9},{9,8},{10,11... | collective-permute-start | bytes 165896 | tf_op jit(solution)/shard_map/ppermute | solution.py:314

commit v8 on v7

--- a/solution.py
+++ b/solution.py
@@ -34,32 +34,21 @@
     return out
 
 
-def pack_kernel(counts_hbm, atoms_hbm, places_hbm, out_ref, counts_ref, places_ref, done):
-    _, cells, a = places_ref.shape
-    top = cells * a
-    copies = [
-        pltpu.make_async_copy(counts_hbm, counts_ref, done.at[0]),
-        pltpu.make_async_copy(places_hbm, places_ref, done.at[1]),
-        pltpu.make_async_copy(atoms_hbm, out_ref.at[0:top, :], done.at[2]),
-    ]
-    for copy in copies:
-        copy.start()
+def pack_kernel(counts_ref, atoms_ref, places_ref, out_ref):
+    cells, a, f = atoms_ref.shape
+    for c in range(cells):
+        out_ref[c * a : (c + 1) * a, :] = atoms_ref[c]
     cell = lax.broadcasted_iota(jnp.int32, (cells, a), 0)
     slot = lax.broadcasted_iota(jnp.int32, (cells, a), 1)
-    copies[0].wait()
     filled = jnp.full((cells, a), counts_ref[0], jnp.int32)
     for c in range(1, cells):
         filled = jnp.where(cell == c, counts_ref[c], filled)
-    copies[1].wait()
+    out_ref[cells * a :, :] = jnp.zeros((out_ref.shape[0] - cells * a, f), BF16)
     spots = [jnp.where(slot < filled, places_ref[d].astype(F32), FAR) for d in range(3)]
     table = jnp.concatenate(spots, axis=0)
-    groups = [table[n : n + SPOT_ROWS] for n in range(0, 3 * cells, SPOT_ROWS)]
-    short = SPOT_ROWS - groups[-1].shape[0]
-    if short:
-        groups[-1] = jnp.concatenate([groups[-1], jnp.zeros((short, a), F32)], axis=0)
-    groups.append(jnp.zeros((SPOT_ROWS, out_ref.shape[1] - a * len(groups)), F32))
-    out_ref[top:, :] = jnp.concatenate(groups, axis=1).astype(BF16)
-    copies[2].wait()
+    for n in range(0, 3 * cells, SPOT_ROWS):
+        rows, at = table[n : n + SPOT_ROWS], n // SPOT_ROWS * a
+        out_ref[cells * a : cells * a + rows.shape[0], at : at + a] = rows.astype(BF16)
 
 
 def spread(a, lanes, rows, by_j, groups=1):
@@ -238,7 +227,7 @@
     units = []
     for at in range(3 * n_ways):
         units += [unit(rads, wgts, proj, c, at * 3 + r, at * cells + c + r - 1) for c, r in inside(cells)]
-    units.sort(key=lambda u: u[0])
+    units.sort(key=lambda u: (u[0] in (0, cells - 1), u[0]))
     add_pairs(units, cells, lanes, w1, w2, acc, k, f, acc1)
 
 
@@ -344,14 +333,9 @@
     packed = pl.pallas_call(
         pack_kernel,
         out_shape=pltpu.VMEM((cells * a + SPOT_ROWS, f), BF16),
-        in_specs=[pl.BlockSpec(memory_space=pl.ANY)] * 3,
+        in_specs=[smem, vmem, vmem],
         out_specs=vmem,
-        scratch_shapes=[
-            pltpu.SMEM((cells,), jnp.int32),
-            pltpu.VMEM((3, cells, a), BF16),
-            pltpu.SemaphoreType.DMA((3,)),
-        ],
-    )(counts, atoms.reshape(cells * a, f), jnp.swapaxes(places, 2, 3).reshape(3, cells, a))
+    )(counts, atoms.reshape(cells, a, f), jnp.swapaxes(places, 2, 3).reshape(3, cells, a))
     above = shifted(packed, [("gx", -1)])
     below = shifted(packed, [("gx", 1)])
     sums = pltpu.VMEM((cells, f, lanes), F32)

time: 16 us -> 15.9 us (level)
  no operation moved by 1% of the time
where the time goes in v8:
time: 15.9 us; the launch traced here: 15.7 us
  Pallas kernels  7.7 us (48%)
  starting transfers between devices  6.86 us (43%)
  waiting for transfers between devices  1.04 us (7%)
    pallas_call x4, Pallas kernels, call(): pl.pallas_call(kernel, out_shape=out_shape, in_specs=[smem] * len(scalars...  6.9 us
    ppermute x5, starting transfers between devices, shifted(): return lax.ppermute(value, tuple(axes), pairs)  6.86 us
    ppermute x5, waiting for transfers between devices, shifted(): return lax.ppermute(value, tuple(axes), pairs)  1.04 us
    pallas_call x1, Pallas kernels, shards(): pl.pallas_call(pack_kernel, out_shape=pltpu.VMEM((cells * a + SPOT_ROWS,...  0.8 us
  transfers between devices with their start and end apart: 5, of which 2 were waited for; matrix products, arithmetic and copies ran while one was open for 0% of the time, Pallas kernels for 33%

profile of v8, /device:TPU:0, one launch (start us, length us, event | category | flops | bytes accessed | tf_op | source)
XLA Modules:
  0.0 15.7 jit_solution(10190545375038383549)
XLA Ops:
  0.0 0.8 %shard_map.118.refs_1_ = bf16[72,128]{1,0:T(8,128)(2,1)S(1)} custom-call(s32[4]{0:T(128)} %bitcast.18, bf16[4,16,128]{2,1,0:T(8,128)(2,1)} %bitcast.16, bf16[3,4,16]{2,1,0:T(4,128)(2,1)} %bitcast.17), custom_call_target="tpu_custom_call" | custom-call | tf_op jit(solution)/shard_map/pallas_call | solution.py:333
  0.8 3.0 %collective-permute-start.1 = (bf16[72,128]{1,0:T(8,128)(2,1)S(1)}, bf16[72,128]{1,0:T(8,128)(2,1)S(1)}, u32[]{:S(2)}, u32[]{:S(2)}) collective-permute-start(bf16[72,128]{1,0:T(8,128)(2,1)S(1)} %shard_map.118.refs_1_), channel_id=1, source_target_pairs={{0,4},{4,8},{8,12},{12,0},{1,5},{5,9},{9,13},{13,1},{2,6},{6,10},{... | collective-permute-start | bytes 55304 | tf_op jit(solution)/shard_map/ppermute | solution.py:303
  3.8 2.1 %collective-permute-start = (bf16[72,128]{1,0:T(8,128)(2,1)S(1)}, bf16[72,128]{1,0:T(8,128)(2,1)S(1)}, u32[]{:S(2)}, u32[]{:S(2)}) collective-permute-start(bf16[72,128]{1,0:T(8,128)(2,1)S(1)} %shard_map.118.refs_1_), channel_id=1, source_target_pairs={{0,12},{4,0},{8,4},{12,8},{1,13},{5,1},{9,5},{13,9},{2,14},{6,2},{... | collective-permute-start | bytes 55304 | tf_op jit(solution)/shard_map/ppermute | solution.py:303
  5.9 1.8 %shard_map.119 = (f32[4,128,256]{2,1,0:T(8,128)S(1)}, bf16[128,64]{1,0:T(8,128)(2,1)S(1)}, bf16[128,144]{1,0:T(8,128)(2,1)S(1)}, bf16[128,128]{1,0:T(8,128)(2,1)...) custom-call(s32[4]{0:T(128)} %bitcast.19, ...), custom_call_target="tpu_custom_call" | custom-call | flops 1000000000 | bytes 1000000 | tf_op jit(solution)/shard_map/pallas_call | solution.py:346
  7.7 0.0 collective-permute-done.1
  7.7 0.1 collective-permute-done
  7.8 0.0 collective-permute-start.3
  7.8 1.7 %collective-permute-start.2 = (bf16[3,72,128]{2,1,0:T(8,128)(2,1)S(1)}, bf16[3,72,128]{2,1,0:T(8,128)(2,1)S(1)}, u32[]{:S(2)}, u32[]{:S(2)}) collective-permute-start(bf16[3,72,128]{2,1,0:T(8,128)(2,1)S(1)} %pad_maximum_fusion.refs_0_), channel_id=1, source_target_pairs={{0,2},{2,0},{1,3},{3,1},{4,6},{6,4},{5,7},{7,5},{8,10},{10,8},{9,1... | collective-permute-start | bytes 165896 | tf_op jit(solution)/shard_map/ppermute | solution.py:303
  9.5 0.0 collective-permute-done.3.refs_1_.refs_2_
  9.6 1.6 %shard_map.120.refs_6_ = f32[4,128,256]{2,1,0:T(8,128)S(1)} custom-call(bf16[3,72,128]{2,1,0:T(8,128)(2,1)S(1)} %pad_maximum_fusion.refs_0_, bf16[3,72,128]{2,1,0:T(8,128)(2,1)S(1)} %collective-permute-done.3.refs_1_.refs_2_, bf16[3,72,128]{2,1,0:T(8,128)(2,1)S(1)} %collective-permute-done.3.refs_1_.refs_2_, ...), custom_call_target="tpu_custom_call" | custom-call | flops 1000000000 | bytes 1000000 | tf_op jit(solution)/shard_map/pallas_call | solution.py:346
  11.2 1.0 %collective-permute-done.2.refs_0_ = bf16[3,72,128]{2,1,0:T(8,128)(2,1)S(1)} collective-permute-done((bf16[3,72,128]{2,1,0:T(8,128)(2,1)S(1)}, bf16[3,72,128]{2,1,0:T(8,128)(2,1)S(1)}, u32[]{:S(2)}, u32[]{:S(2)}) %collective-permute-start.2) | collective-permute-done | bytes 55328 | tf_op jit(solution)/shard_map/ppermute | solution.py:303
  12.1 0.0 collective-permute-start.4
  12.1 1.8 %shard_map.121.refs_12_ = f32[4,128,256]{2,1,0:T(8,128)S(1)} custom-call(bf16[3,72,128]{2,1,0:T(8,128)(2,1)S(1)} %collective-permute-done.2.refs_0_, f32[16,256]{1,0:T(8,128)S(1)} %get-tuple-element.26.refs_3_.refs_1_.refs_2_, bf16[128,64]{1,0:T(8,128)(2,1)S(1)} %get-tuple-element.27.refs_4_.refs_2_.refs_3_, ...), custom_call_target="tpu_custom_call" | custom-call | flops 1000000000 | bytes 1000000 | tf_op jit(solution)/shard_map/pallas_call | solution.py:346
  13.9 0.0 collective-permute-done.4.refs_0_
  13.9 1.7 %shard_map.122 = bf16[4,16,128]{2,1,0:T(8,128)(2,1)} custom-call(bf16[3,72,128]{2,1,0:T(8,128)(2,1)S(1)} %collective-permute-done.4.refs_0_, bf16[72,128]{1,0:T(8,128)(2,1)S(1)} %shard_map.118.refs_1_, f32[16,256]{1,0:T(8,128)S(1)} %get-tuple-element.26.refs_3_.refs_1_.refs_2_, bf16[128,64]{1,0:T(8,128)(2,1)S(1)} %get-tuple-element.27.refs_4_.refs_2_.refs_3_, ...), custom_call_target="tpu_custom_call" | custom-call | flops 1000000000 | bytes 1000000 | tf_op jit(solution)/shard_map/pallas_call | solution.py:346
  (1 shorter events, 0.0 us)
Async XLA Ops:
  0.8 6.9 %collective-permute-start.1 = (bf16[72,128]{1,0:T(8,128)(2,1)S(1)}, bf16[72,128]{1,0:T(8,128)(2,1)S(1)}, u32[]{:S(2)}, u32[]{:S(2)}) collective-permute-start(bf16[72,128]{1,0:T(8,128)(2,1)S(1)} %shard_map.118.refs_1_), channel_id=1, source_target_pairs={{0,4},{4,8},{8,12},{12,0},{1,5},{5,9},{9,13},{13,1},{2,6},{6,10},{... | collective-permute-start | bytes 55304 | tf_op jit(solution)/shard_map/ppermute | solution.py:303
  3.8 4.0 %collective-permute-start = (bf16[72,128]{1,0:T(8,128)(2,1)S(1)}, bf16[72,128]{1,0:T(8,128)(2,1)S(1)}, u32[]{:S(2)}, u32[]{:S(2)}) collective-permute-start(bf16[72,128]{1,0:T(8,128)(2,1)S(1)} %shard_map.118.refs_1_), channel_id=1, source_target_pairs={{0,12},{4,0},{8,4},{12,8},{1,13},{5,1},{9,5},{13,9},{2,14},{6,2},{... | collective-permute-start | bytes 55304 | tf_op jit(solution)/shard_map/ppermute | solution.py:303
  7.8 1.8 %collective-permute-start.3 = (bf16[3,72,128]{2,1,0:T(8,128)(2,1)S(1)}, bf16[3,72,128]{2,1,0:T(8,128)(2,1)S(1)}, u32[]{:S(2)}, u32[]{:S(2)}) collective-permute-start(bf16[3,72,128]{2,1,0:T(8,128)(2,1)S(1)} %pad_maximum_fusion.refs_0_), channel_id=1, source_target_pairs={{0,1},{1,0},{2,3},{3,2},{4,5},{5,4},{6,7},{7,6},{8,9},{9,8},{10,11... | collective-permute-start | bytes 165896 | tf_op jit(solution)/shard_map/ppermute | solution.py:303
  7.8 4.3 %collective-permute-start.2 = (bf16[3,72,128]{2,1,0:T(8,128)(2,1)S(1)}, bf16[3,72,128]{2,1,0:T(8,128)(2,1)S(1)}, u32[]{:S(2)}, u32[]{:S(2)}) collective-permute-start(bf16[3,72,128]{2,1,0:T(8,128)(2,1)S(1)} %pad_maximum_fusion.refs_0_), channel_id=1, source_target_pairs={{0,2},{2,0},{1,3},{3,1},{4,6},{6,4},{5,7},{7,5},{8,10},{10,8},{9,1... | collective-permute-start | bytes 165896 | tf_op jit(solution)/shard_map/ppermute | solution.py:303
  12.1 1.8 %collective-permute-start.4 = (bf16[3,72,128]{2,1,0:T(8,128)(2,1)S(1)}, bf16[3,72,128]{2,1,0:T(8,128)(2,1)S(1)}, u32[]{:S(2)}, u32[]{:S(2)}) collective-permute-start(bf16[3,72,128]{2,1,0:T(8,128)(2,1)S(1)} %collective-permute-done.2.refs_0_), channel_id=1, source_target_pairs={{0,1},{1,0},{2,3},{3,2},{4,5},{5,4},{6,7},{7,6},{8,9},{9,8},{10,11... | collective-permute-start | bytes 165896 | tf_op jit(solution)/shard_map/ppermute | solution.py:303
